TPU v7x, 128 devices: a whole 4x4x4 slice. The times are simulated.
128 devices in a mesh: tile: 16 (over x, y_hi, core), gz: 8 (over z, y_lo).
Axes of the slice: x: 4, y: 4 (y_hi: 2, y_lo: 2; y = y_hi * 2 + y_lo), z: 4, core: 2. Of those that a mesh axis runs over, the one named last changes fastest.
Arguments:
- trans_x: float32 [256, 128, 512], P('tile', 'gz'), may hold values from 3 to 10
- trans_y: float32 [256, 128, 512], P('tile', 'gz'), may hold values from 0.5 to 2
- trans_z: float32 [256, 128, 512], P('tile', 'gz'), may hold values from 0.1 to 0.3
- accumulation: float32 [256, 128, 512], P('tile', 'gz'), may hold values from 0.02 to 0.2
- source: float32 [256, 128, 512], P('tile', 'gz'), may hold values from -6 to 6
- well_cell: int32 [256, 8], P('tile', 'gz'), may hold values from 0 to 131071
- well_rate: float32 [256, 8], P('tile', 'gz'), may hold values from -48 to 48
Outputs:
- basis: float32 [8, 256, 128, 512], P(None, 'tile', 'gz')
- pressure: float32 [256, 128, 512], P('tile', 'gz')
- residual: float32 [256, 128, 512], P('tile', 'gz')
Inputs may be any that keep to these rules, and one draw needn't show every extreme that they name: `well_cell`: each value indexes a cell as (x * 16 + z) * 512 + y inside the block of 16 x 16 x 512 cells of its row's tile index and its column's gz index; several wells may share a cell.
All inputs are finite; a program needn't handle non-finite values.
Results may differ from a plain program's by a relative error of at most 0.0003.
Values sent between devices are 32-bit elements; how exact they have to be, the bound alone decides.
A program may use at most 192 MiB of HBM per device.

v0:
```python
import jax
import jax.numpy as jnp
from jax import lax
from jax.sharding import PartitionSpec as P

SWEEPS = 4
COARSE_ITERS = 6


OMEGA = 2.0 / 3.0
COARSE_STEP = 0.5


def extended(array, sides, width):
    edges = {}
    for axis, dim in sides:
        size, length = (lax.axis_size(axis), array.shape[dim])
        up = [(i, (i + 1) % size) for i in range(size - 1)]
        last = lax.slice_in_dim(array, length - width, length, axis=dim)
        initial = lax.slice_in_dim(array, 0, width, axis=dim)
        edges[dim] = (
            lax.ppermute(last, axis, up),
            lax.ppermute(initial, axis, [(b, a) for a, b in up]),
        )
    done = []
    for _, dim in sides:
        low, high = edges[dim]
        around = [(width, width) if d in done else (0, 0) for d in range(array.ndim)]
        array = jnp.concatenate([jnp.pad(low, around), array, jnp.pad(high, around)], axis=dim)
        done.append(dim)
    return array


def extended_2(cells, sides, width):
    for axis, dim in sides:
        count = lax.axis_size(axis)
        ends = count - 1
        head = lax.slice_in_dim(cells, 0, width, axis=dim)
        tail = lax.slice_in_dim(cells, cells.shape[dim] - width, cells.shape[dim], axis=dim)
        cells = jnp.concatenate(
            [
                lax.ppermute(tail, axis, [(i, (i + 1) % count) for i in range(ends)]),
                cells,
                lax.ppermute(head, axis, [((i + 1) % count, i) for i in range(ends)]),
            ],
            axis=dim,
        )
    return cells


def shifted(array, axis, by):
    size = lax.axis_size(axis)
    pairs = [(i, i + by) for i in range(size) if 0 <= i + by < size]
    return lax.ppermute(array, axis, pairs)


def axis_nodes(position, extent):
    block = position // 8
    upper = position % 8 >= 4
    rows = [block + jnp.where(block % 2 == parity, 0, jnp.where(upper, 1, -1)) for parity in (0, 1)]
    nodes = jnp.stack(rows)
    inside = (nodes >= 0) & (nodes < extent // 8)
    return (nodes, inside)


def axis_geometry(position, extent):
    nodes, inside = axis_nodes(position, extent)
    after, unused_after = axis_nodes(position + 1, extent)
    before, unused_before = axis_nodes(position - 1, extent)
    has_after = position + 1 < extent
    has_before = position >= 1
    same_after = (after == nodes).astype(jnp.float32)
    same_before = (before == nodes).astype(jnp.float32)
    inner = ((after == nodes) | ~has_after[None]) & ((before == nodes) | ~has_before[None])
    offsets = nodes - (position // 8)[None]
    edge_after = (((position + 1) % 8 == 0) & has_after).astype(jnp.float32)
    edge_before = ((position % 8 == 0) & has_before).astype(jnp.float32)
    return (
        inside.astype(jnp.float32),
        inner.astype(jnp.float32),
        same_after,
        same_before,
        offsets,
        edge_after,
        edge_before,
        has_after.astype(jnp.float32),
    )


def spread_slots(pair, axis):
    picks = []
    for slot in range(8):
        digit = slot // 4 if axis == 1 else slot // 2 % 2 if axis == 2 else slot % 2
        picks.append(pair[digit])
    shape = [8, 1, 1, 1]
    shape[axis] = pair.shape[1]
    return jnp.stack(picks).reshape(shape)


def along(vector, axis):
    shape = [1, 1, 1]
    shape[axis] = vector.shape[0]
    return vector.reshape(shape)


def flux_apply(padded, faces, sames):
    center = padded[..., 1:-1, 1:-1, :]
    zero_col = jnp.zeros_like(center[..., :1])
    neighbours = (
        padded[..., 2:, 1:-1, :],
        padded[..., :-2, 1:-1, :],
        padded[..., 1:-1, 2:, :],
        padded[..., 1:-1, :-2, :],
        jnp.concatenate([center[..., 1:], zero_col], -1),
        jnp.concatenate([zero_col, center[..., :-1]], -1),
    )
    result = faces[0] * (center - sames[0] * neighbours[0])
    for index in range(1, 6):
        result = result + faces[index] * (center - sames[index] * neighbours[index])
    return result


def block_sum(field):
    size_x, size_z, size_y = field.shape
    return field.reshape(size_x // 8, 8, size_z // 8, 8, size_y // 8, 8).sum(axis=(1, 3, 5))


def one_hot_offsets(offsets):
    table = (offsets[:, :, None] == jnp.arange(-1, 2, dtype=jnp.int32)[None, None]).astype(
        jnp.float32
    )
    return table.reshape(2, offsets.shape[1] // 8, 8, 3)


def coarse_operator(edge_term, off_x, off_z, off_y):
    size_x, size_z, size_y = edge_term.shape[1:]
    shaped = edge_term.reshape(2, 2, 2, size_x // 8, 8, size_z // 8, 8, size_y // 8, 8)
    return jnp.einsum(
        "abcIiKkJj,aIix,bKkz,cJjy->xzyIKJ",
        shaped,
        one_hot_offsets(off_x),
        one_hot_offsets(off_z),
        one_hot_offsets(off_y),
        precision=lax.Precision.HIGHEST,
    )


def apply_coarse(coarse_op, padded):
    full = jnp.pad(padded, ((0, 0), (0, 0), (1, 1)))
    count_x = padded.shape[0] - 2
    count_z = padded.shape[1] - 2
    count_y = padded.shape[2]
    result = jnp.zeros((count_x, count_z, count_y), jnp.float32)
    for ix in range(3):
        for iz in range(3):
            for iy in range(3):
                result = (
                    result
                    + coarse_op[ix, iz, iy]
                    * full[ix : ix + count_x, iz : iz + count_z, iy : iy + count_y]
                )
    return result


def selection(offsets, padded_count):
    local = jnp.arange(offsets.shape[1], dtype=jnp.int32) // 8
    target = local[None] + 1 + offsets
    return (target[:, :, None] == jnp.arange(padded_count, dtype=jnp.int32)[None, None]).astype(
        jnp.float32
    )


def prolong(basis, padded_coarse, off_x, off_z, off_y):
    size_x, size_z, size_y = basis.shape[1:]
    values = jnp.einsum(
        "aXi,bZk,cYj,ikj->abcXZY",
        selection(off_x, padded_coarse.shape[0]),
        selection(off_z, padded_coarse.shape[1]),
        selection(off_y, padded_coarse.shape[2] + 2),
        jnp.pad(padded_coarse, ((0, 0), (0, 0), (1, 1))),
        precision=lax.Precision.HIGHEST,
    )
    return jnp.sum(basis * values.reshape(8, size_x, size_z, size_y), axis=0)


def basis_outer(basis):
    return extended(basis, (("tile", 1), ("gz", 2)), 1)


def coarse_outer(coarse):
    return extended_2(coarse, (("tile", 0), ("gz", 1)), 1)


def body(trans_x, trans_y, trans_z, accumulation, source, well_cell, well_rate):
    size_x, size_z, size_y = trans_x.shape
    tiles = lax.axis_size("tile")
    layers = lax.axis_size("gz")
    tile_index = lax.axis_index("tile")
    layer_index = lax.axis_index("gz")
    geo_x = axis_geometry(tile_index * size_x + jnp.arange(size_x, dtype=jnp.int32), size_x * tiles)
    geo_z = axis_geometry(
        layer_index * size_z + jnp.arange(size_z, dtype=jnp.int32), size_z * layers
    )
    geo_y = axis_geometry(jnp.arange(size_y, dtype=jnp.int32), size_y)
    tx = trans_x * along(geo_x[7], 0)
    tz = trans_z * along(geo_z[7], 1)
    ty = trans_y * along(geo_y[7], 2)
    tx_prev = jnp.concatenate([shifted(tx[-1:], "tile", 1), tx[:-1]], 0)
    tz_prev = jnp.concatenate([shifted(tz[:, -1:], "gz", 1), tz[:, :-1]], 1)
    ty_prev = jnp.concatenate([jnp.zeros_like(ty[:, :, :1]), ty[:, :, :-1]], 2)
    faces = (tx, tx_prev, tz, tz_prev, ty, ty_prev)
    ones = (1.0, 1.0, 1.0, 1.0, 1.0, 1.0)
    diagonal = tx + tx_prev + tz + tz_prev + ty + ty_prev
    valid = spread_slots(geo_x[0], 1) * spread_slots(geo_z[0], 2) * spread_slots(geo_y[0], 3)
    inner = (
        valid * spread_slots(geo_x[1], 1) * spread_slots(geo_z[1], 2) * spread_slots(geo_y[1], 3)
    )
    sames = (
        spread_slots(geo_x[2], 1),
        spread_slots(geo_x[3], 1),
        spread_slots(geo_z[2], 2),
        spread_slots(geo_z[3], 2),
        spread_slots(geo_y[2], 3),
        spread_slots(geo_y[3], 3),
    )
    basis = (
        valid
        * spread_slots((geo_x[4] == 0).astype(jnp.float32), 1)
        * spread_slots((geo_z[4] == 0).astype(jnp.float32), 2)
        * spread_slots((geo_y[4] == 0).astype(jnp.float32), 3)
    )
    for sweep in range(SWEEPS):
        padded = basis_outer(basis)
        flow = flux_apply(padded, faces, sames)
        basis = basis - OMEGA * inner * flow / diagonal
        basis = basis / jnp.sum(basis, axis=0)
    padded = basis_outer(basis)
    block_faces = (
        tx * along(geo_x[5], 0),
        tx_prev * along(geo_x[6], 0),
        tz * along(geo_z[5], 1),
        tz_prev * along(geo_z[6], 1),
        ty * along(geo_y[5], 2),
        ty_prev * along(geo_y[6], 2),
    )
    edge_term = accumulation * basis + flux_apply(padded, block_faces, ones)
    coarse_op = coarse_operator(edge_term, geo_x[4], geo_z[4], geo_y[4])
    flat = well_cell.reshape(-1)
    rhs = source.reshape(-1).at[flat].add(well_rate.reshape(-1)).reshape(size_x, size_z, size_y)
    coarse_rhs = block_sum(rhs)
    coarse_scale = block_sum(
        accumulation
        + block_faces[0]
        + block_faces[1]
        + block_faces[2]
        + block_faces[3]
        + block_faces[4]
        + block_faces[5]
    )
    coarse = jnp.zeros_like(coarse_rhs)
    for step in range(COARSE_ITERS):
        coarse_pad = coarse_outer(coarse)
        coarse = (
            coarse + COARSE_STEP * (coarse_rhs - apply_coarse(coarse_op, coarse_pad)) / coarse_scale
        )
    coarse_pad = coarse_outer(coarse)
    pressure = prolong(basis, coarse_pad, geo_x[4], geo_z[4], geo_y[4])
    pressure_pad = extended_2(pressure, (("tile", 0), ("gz", 1)), 1)
    residual = rhs - (accumulation * pressure + flux_apply(pressure_pad, faces, ones))
    return (basis, pressure, residual)


def solution(mesh):
    placed = (
        P("tile", "gz", None),
        P("tile", "gz", None),
        P("tile", "gz", None),
        P("tile", "gz", None),
        P("tile", "gz", None),
        P("tile", "gz"),
        P("tile", "gz"),
    )
    return jax.shard_map(
        body,
        mesh=mesh,
        in_specs=placed,
        out_specs=(P(None, "tile", "gz", None), P("tile", "gz", None), P("tile", "gz", None)),
        check_vma=False,
    )
```

profile of v0, /device:TPU:36, one launch (start us, length us, event | category | flops | bytes accessed | tf_op | source)
XLA Modules:
  0.0 518.6 jit_solution(16932167708825932438)
XLA Ops:
  3.1 6.0 %collective-permute-start.23 = (f32[1,2,64]{2,1,0:T(2,128)}, f32[1,2,64]{2,1,0:T(2,128)S(1)}, u32[]{:S(2)}, u32[]{:S(2)}) collective-permute-start(f32[1,2,64]{2,1,0:T(2,128)} %broadcast.3460), channel_id=1, source_target_pairs={{8,0},{16,8},{24,16},{32,24},{40,32},{48,40},{56,48},{64,56},{72,6... | collective-permute-start | bytes 1544 | tf_op jit(solution)/shard_map/ppermute | solution.py:44
  17.6 3.2 collective-permute-start.3
  20.7 4.9 fusion.463
  33.5 6.2 %reshape_reshape.3 = f32[2,8,2,8,64,8]{5,4,3,2,1,0:T(8,128)} reshape(f32[131072]{0:T(1024)S(1)} %scatter_fusion) | data formatting | bytes 1048576 | tf_op jit(solution)/shard_map/reshape;reshape | solution.py:125
  39.7 4.3 reduce_sum.67
  44.0 2.8 collective-permute-start.24
  46.8 3.9 collective-permute-start.25
  53.2 4.4 collective-permute-start.4
  58.6 2.7 collective-permute-start.5
  61.3 3.9 add_add_fusion
  65.2 7.1 %reshape.1737 = f32[2,8,2,8,64,8]{5,4,3,2,1,0:T(8,128)} reshape(f32[16,16,512]{2,1,0:T(8,128)} %get-tuple-element.3) | data formatting | bytes 1048576 | tf_op jit(solution)/shard_map/reshape | solution.py:125
  72.3 4.3 reduce_sum.68
  79.1 12.2 %fusion.447 = (f32[16,16,512]{2,1,0:T(8,128)S(1)}, f32[8,16,16,512]{3,2,1,0:T(8,128)S(1)}) fusion(f32[16,16,512]{2,1,0:T(8,128)S(1)} %get-tuple-element.92, f32[8,16,16,511]{3,2,1,0:T(8,128)} %get-tuple-element.57, f32[8,512]{1,0:T(8,128)S(1)} %add_convert_fusion.4, f32[16,16,512]{2,1,0:T(8,128)S(1)} %get-tuple-element.93, ...), kind=kLoop, calls=%fused_computation.962 | loop fusion | flops 51249152 | bytes 22097920 | tf_op jit(solution)/shard_map/reduce_sum | solution.py:236
  92.8 5.3 %collective-permute-start.6 = (f32[8,1,16,512]{3,2,1,0:T(8,128)S(1)}, f32[8,1,16,512]{3,2,1,0:T(8,128)S(1)}, u32[]{:S(2)}, u32[]{:S(2)}) collective-permute-start(f32[8,1,16,512]{3,2,1,0:T(8,128)S(1)} %get-tuple-element.49), channel_id=1, source_target_pairs={{8,0},{16,8},{24,16},{32,24},{40,32},{48,40},{56,48},{64,56},{72,6... | collective-permute-start | bytes 786440 | tf_op jit(solution)/shard_map/ppermute | solution.py:23
  102.1 4.1 collective-permute-start.9
  108.3 2.8 collective-permute-done.8
  111.1 5.8 %collective-permute-done.9 = f32[8,16,1,512]{3,2,1,0:T(1,128)S(1)} collective-permute-done((f32[8,16,1,512]{3,2,1,0:T(1,128)S(1)}, f32[8,16,1,512]{3,2,1,0:T(1,128)S(1)}, u32[]{:S(2)}, u32[]{:S(2)}) %collective-permute-start.9) | collective-permute-done | bytes 262176 | tf_op jit(solution)/shard_map/ppermute | solution.py:22
  117.0 10.2 %fusion.445 = (f32[16,16,512]{2,1,0:T(8,128)S(1)}, f32[8,16,16,512]{3,2,1,0:T(8,128)S(1)}) fusion(f32[8,16,16,512]{3,2,1,0:T(8,128)S(1)} %broadcast_divide_fusion.3, f32[16,16,512]{2,1,0:T(8,128)S(1)} %get-tuple-element.92, f32[8,16,16,511]{3,2,1,0:T(8,128)S(1)} %get-tuple-element.51, f32[8,512]{1,0:T(8,128)S(1)} %add_convert_fusion.4, ...), kind=kLoop, calls=%fused_computation.961 | loop fusion | flops 48103424 | bytes 22080512 | tf_op jit(solution)/shard_map/reduce_sum | solution.py:236
  128.3 4.5 collective-permute-start.10
  136.7 3.9 collective-permute-start.13
  143.0 2.8 collective-permute-done.12
  145.8 3.3 collective-permute-done.13
  149.1 10.2 %fusion.443 = (f32[16,16,512]{2,1,0:T(8,128)S(1)}, f32[8,16,16,512]{3,2,1,0:T(8,128)S(1)}) fusion(f32[8,16,16,512]{3,2,1,0:T(8,128)S(1)} %broadcast_divide_fusion.2, f32[16,16,512]{2,1,0:T(8,128)S(1)} %get-tuple-element.92, f32[8,16,16,511]{3,2,1,0:T(8,128)S(1)} %get-tuple-element.45, f32[8,512]{1,0:T(8,128)S(1)} %add_convert_fusion.4, ...), kind=kLoop, calls=%fused_computation.960 | loop fusion | flops 48103424 | bytes 22080512 | tf_op jit(solution)/shard_map/reduce_sum | solution.py:236
  160.5 4.7 collective-permute-start.14
  169.2 15.6 %collective-permute-start.17 = (f32[8,16,1,512]{3,2,1,0:T(1,128)S(1)}, f32[8,16,1,512]{3,2,1,0:T(1,128)S(1)}, u32[]{:S(2)}, u32[]{:S(2)}) collective-permute-start(f32[8,16,1,512]{3,2,1,0:T(1,128)S(1)} %get-tuple-element.35), channel_id=1, source_target_pairs={{0,1},{1,2},{2,3},{3,4},{4,5},{5,6},{6,7},{8,9},{9,10},{10,11},{11... | collective-permute-start | bytes 786440 | tf_op jit(solution)/shard_map/ppermute | solution.py:22
  186.6 10.2 %fusion.441 = (f32[16,16,512]{2,1,0:T(8,128)S(1)}, f32[8,16,16,512]{3,2,1,0:T(8,128)S(1)}) fusion(f32[8,16,16,512]{3,2,1,0:T(8,128)S(1)} %broadcast_divide_fusion.1, f32[16,16,512]{2,1,0:T(8,128)S(1)} %get-tuple-element.92, f32[8,16,16,511]{3,2,1,0:T(8,128)S(1)} %get-tuple-element.39, f32[8,512]{1,0:T(8,128)S(1)} %add_convert_fusion.4, ...), kind=kLoop, calls=%fused_computation.959 | loop fusion | flops 48103424 | bytes 22080512 | tf_op jit(solution)/shard_map/reduce_sum | solution.py:236
  199.6 5.5 %collective-permute-start.18 = (f32[8,1,16,512]{3,2,1,0:T(8,128)S(1)}, f32[8,1,16,512]{3,2,1,0:T(8,128)S(1)}, u32[]{:S(2)}, u32[]{:S(2)}) collective-permute-start(f32[8,1,16,512]{3,2,1,0:T(8,128)S(1)} %get-tuple-element.33), channel_id=1, source_target_pairs={{8,0},{16,8},{24,16},{32,24},{40,32},{48,40},{56,48},{64,56},{72,6... | collective-permute-start | bytes 786440 | tf_op jit(solution)/shard_map/ppermute | solution.py:23
  209.4 4.3 collective-permute-start.21
  215.5 3.5 collective-permute-done.20
  219.0 3.7 collective-permute-done.21
  222.8 8.6 %fusion.40 = f32[8,16,16,512]{3,2,1,0:T(8,128)} fusion(f32[8,16,16,512]{3,2,1,0:T(8,128)S(1)} %broadcast_divide_fusion, f32[8,16,1,512]{3,2,1,0:T(1,128)S(1)} %collective-permute-done.21, f32[8,1,16,512]{3,2,1,0:T(8,128)S(1)} %collective-permute-done.18, f32[8,1,16,512]{3,2,1,0:T(8,128)S(1)} %collective-permute-done.19, ...), kind=kLoop, calls=%fused_computation.44 | loop fusion | flops 34603008 | bytes 21479424 | tf_op jit(solution)/shard_map/add | solution.py:246
  231.3 41.9 %reshape.1736 = f32[2,2,2,2,8,2,8,64,8]{8,7,6,5,4,3,2,1,0:T(8,128)} reshape(f32[8,16,16,512]{3,2,1,0:T(8,128)} %fusion.40) | data formatting | bytes 8388608 | tf_op jit(solution)/shard_map/reshape | solution.py:137
  273.2 40.2 %copy.3027 = f32[2,2,2,2,8,2,8,64,8]{7,4,0,8,6,5,2,1,3:T(8,128)} copy(f32[2,2,2,2,8,2,8,64,8]{8,7,6,5,4,3,2,1,0:T(8,128)} %reshape.1736) | data formatting | bytes 8388608 | tf_op jit(solution)/shard_map/reshape | solution.py:137
  313.4 7.3 %convolution_bitcast_fusion.1 = f32[2,3,2,2,2,8,64,8]{6,1,7,5,4,3,2,0:T(4,128)S(1)} fusion(f32[2,2,2,2,8,2,8,64,8]{7,4,0,8,6,5,2,1,3:T(8,128)} %copy.3027, s32[2,2,8]{2,0,1:T(2,128)S(1)} %copy-done.37, s32[3]{0:T(128)S(1)} %copy-done.36), kind=kOutput, calls=%fused_computation.165 | convolution fusion | flops 37748832 | bytes 4980876 | tf_op jit(solution)/shard_map/abcIiKkJj,aIix,bKkz,cJjy->xzyIKJ/dot_general | solution.py:138
  322.4 3.9 copy.3030
  326.2 5.2 %convolution_bitcast_fusion.2 = f32[3,3,3,2,2,64]{2,1,4,0,3,5:T(4,128)S(1)} fusion(f32[2,3,2,2,64,8,3]{5,6,2,3,1,0,4:T(4,128)} %copy.3030, s32[2,64,8]{2,0,1:T(2,128)S(1)} %copy.3029, s32[3]{0:T(128)S(1)} %copy-done.36), kind=kOutput, calls=%fused_computation.168 | convolution fusion | flops 1330176 | bytes 179212 | tf_op jit(solution)/shard_map/abcIiKkJj,aIix,bKkz,cJjy->xzyIKJ/dot_general | solution.py:138
  331.5 4.9 fusion.464
  366.3 4.6 collective-permute-start.26
  370.9 3.4 collective-permute-start.27
  375.6 3.7 collective-permute-start.28
  379.3 3.1 collective-permute-start.29
  382.4 3.6 collective-permute-done.29
  386.9 4.6 collective-permute-start.30
  391.6 3.4 collective-permute-start.31
  396.2 4.8 collective-permute-start.32
  403.0 3.5 collective-permute-done.33
  407.5 2.8 collective-permute-start.34
  410.3 5.2 collective-permute-start.35
  416.8 4.3 collective-permute-start.36
  423.6 3.0 collective-permute-done.37
  429.5 6.0 %collective-permute-start.39 = (f32[1,2,64]{2,1,0:T(2,128)S(1)}, f32[1,2,64]{2,1,0:T(2,128)S(1)}, u32[]{:S(2)}, u32[]{:S(2)}) collective-permute-start(f32[1,2,64]{2,1,0:T(2,128)S(1)} %get-tuple-element.115), channel_id=1, source_target_pairs={{8,0},{16,8},{24,16},{32,24},{40,32},{48,40},{56,48},{64,56},{72,6... | collective-permute-start | bytes 1544 | tf_op jit(solution)/shard_map/ppermute | solution.py:44
  436.9 4.8 collective-permute-start.40
  443.6 3.5 collective-permute-done.41
  450.1 6.0 %collective-permute-start.43 = (f32[1,2,64]{2,1,0:T(2,128)S(1)}, f32[1,2,64]{2,1,0:T(2,128)S(1)}, u32[]{:S(2)}, u32[]{:S(2)}) collective-permute-start(f32[1,2,64]{2,1,0:T(2,128)S(1)} %get-tuple-element.113), channel_id=1, source_target_pairs={{8,0},{16,8},{24,16},{32,24},{40,32},{48,40},{56,48},{64,56},{72,6... | collective-permute-start | bytes 1544 | tf_op jit(solution)/shard_map/ppermute | solution.py:44
  457.4 2.8 collective-permute-start.44
  460.2 3.9 collective-permute-start.45
  468.6 6.0 %collective-permute-start.47 = (f32[1,2,64]{2,1,0:T(2,128)S(1)}, f32[1,2,64]{2,1,0:T(2,128)S(1)}, u32[]{:S(2)}, u32[]{:S(2)}) collective-permute-start(f32[1,2,64]{2,1,0:T(2,128)S(1)} %get-tuple-element.111), channel_id=1, source_target_pairs={{8,0},{16,8},{24,16},{32,24},{40,32},{48,40},{56,48},{64,56},{72,6... | collective-permute-start | bytes 1544 | tf_op jit(solution)/shard_map/ppermute | solution.py:44
  476.0 2.8 collective-permute-start.48
  478.8 4.2 collective-permute-start.49
  490.8 5.9 %collective-permute-start.50 = (f32[1,16,512]{2,1,0:T(8,128)S(1)}, f32[1,16,512]{2,1,0:T(8,128)S(1)}, u32[]{:S(2)}, u32[]{:S(2)}) collective-permute-start(f32[1,16,512]{2,1,0:T(8,128)S(1)} %get-tuple-element.90), channel_id=1, source_target_pairs={{8,0},{16,8},{24,16},{32,24},{40,32},{48,40},{56,48},{64,56},{72,6... | collective-permute-start | bytes 98312 | tf_op jit(solution)/shard_map/ppermute | solution.py:44
  500.6 3.8 collective-permute-done.51
  504.4 3.9 collective-permute-start.52
  510.5 4.6 collective-permute-done.53
  515.1 3.0 fusion.125
  (338 shorter events, 126.2 us)
Async XLA Ops:
  1.2 42.7 %collective-permute-start.22 = (f32[1,2,64]{2,1,0:T(2,128)}, f32[1,2,64]{2,1,0:T(2,128)S(1)}, u32[]{:S(2)}, u32[]{:S(2)}) collective-permute-start(f32[1,2,64]{2,1,0:T(2,128)} %broadcast.3460), channel_id=1, source_target_pairs={{0,8},{8,16},{16,24},{24,32},{32,40},{40,48},{48,56},{56,64},{64,7... | collective-permute-start | bytes 1544 | tf_op jit(solution)/shard_map/ppermute | solution.py:42
  3.1 40.8 %collective-permute-start.23 = (f32[1,2,64]{2,1,0:T(2,128)}, f32[1,2,64]{2,1,0:T(2,128)S(1)}, u32[]{:S(2)}, u32[]{:S(2)}) collective-permute-start(f32[1,2,64]{2,1,0:T(2,128)} %broadcast.3460), channel_id=1, source_target_pairs={{8,0},{16,8},{24,16},{32,24},{40,32},{48,40},{56,48},{64,56},{72,6... | collective-permute-start | bytes 1544 | tf_op jit(solution)/shard_map/ppermute | solution.py:44
  11.9 66.4 %collective-permute-start = (f32[8,1,16,512]{3,2,1,0:T(8,128)}, f32[8,1,16,512]{3,2,1,0:T(8,128)}, u32[]{:S(2)}, u32[]{:S(2)}) collective-permute-start(f32[8,1,16,512]{3,2,1,0:T(8,128)} %get-tuple-element.55), channel_id=1, source_target_pairs={{8,0},{16,8},{24,16},{32,24},{40,32},{48,40},{56,48},{64,56},{72,6... | collective-permute-start | bytes 786440 | tf_op jit(solution)/shard_map/ppermute | solution.py:23
  13.8 64.5 %collective-permute-start.2 = (f32[8,1,16,512]{3,2,1,0:T(8,128)}, f32[8,1,16,512]{3,2,1,0:T(8,128)}, u32[]{:S(2)}, u32[]{:S(2)}) collective-permute-start(f32[8,1,16,512]{3,2,1,0:T(8,128)} %get-tuple-element.54), channel_id=1, source_target_pairs={{0,8},{8,16},{16,24},{24,32},{32,40},{40,48},{48,56},{56,64},{64,7... | collective-permute-start | bytes 786440 | tf_op jit(solution)/shard_map/ppermute | solution.py:22
  17.6 60.8 %collective-permute-start.3 = (f32[8,16,1,512]{3,2,1,0:T(1,128)}, f32[8,16,1,512]{3,2,1,0:T(1,128)}, u32[]{:S(2)}, u32[]{:S(2)}) collective-permute-start(f32[8,16,1,512]{3,2,1,0:T(1,128)} %get-tuple-element.52), channel_id=1, source_target_pairs={{1,0},{2,1},{3,2},{4,3},{5,4},{6,5},{7,6},{9,8},{10,9},{11,10},{12... | collective-permute-start | bytes 786440 | tf_op jit(solution)/shard_map/ppermute | solution.py:23
  27.7 48.8 %copy-start.22 = (f32[512]{0:T(512)}, f32[512]{0:T(512)S(1)}, u32[]{:S(2)}) copy-start(f32[512]{0:T(512)S(1)} %fusion.403) | copy-start | bytes 6148
  44.0 28.3 %copy-start.24 = (f32[2,2,64]{2,1,0:T(2,128)}, f32[2,2,64]{2,1,0:T(2,128)S(1)}, u32[]{:S(2)}) copy-start(f32[2,2,64]{2,1,0:T(2,128)S(1)} %broadcast_in_dim.62) | copy-start | bytes 3076
  44.0 6.9 %collective-permute-start.24 = (f32[4,1,64]{2,1,0:T(1,128)S(1)}, f32[4,1,64]{2,1,0:T(1,128)S(1)}, u32[]{:S(2)}, u32[]{:S(2)}) collective-permute-start(f32[4,1,64]{2,1,0:T(1,128)S(1)} %get-tuple-element.106), channel_id=1, source_target_pairs={{0,1},{1,2},{2,3},{3,4},{4,5},{5,6},{6,7},{8,9},{9,10},{10,11},{11... | collective-permute-start | bytes 3080 | tf_op jit(solution)/shard_map/ppermute | solution.py:42
  46.8 6.3 %collective-permute-start.25 = (f32[4,1,64]{2,1,0:T(1,128)S(1)}, f32[4,1,64]{2,1,0:T(1,128)S(1)}, u32[]{:S(2)}, u32[]{:S(2)}) collective-permute-start(f32[4,1,64]{2,1,0:T(1,128)S(1)} %get-tuple-element.107), channel_id=1, source_target_pairs={{1,0},{2,1},{3,2},{4,3},{5,4},{6,5},{7,6},{9,8},{10,9},{11,10},{12... | collective-permute-start | bytes 3080 | tf_op jit(solution)/shard_map/ppermute | solution.py:44
  51.0 7.6 %collective-permute-start.1 = (f32[1,16,512]{2,1,0:T(8,128)S(1)}, f32[1,16,512]{2,1,0:T(8,128)S(1)}, u32[]{:S(2)}, u32[]{:S(2)}) collective-permute-start(f32[1,16,512]{2,1,0:T(8,128)S(1)} %slice.1597), channel_id=1, source_target_pairs={{0,8},{8,16},{16,24},{24,32},{32,40},{40,48},{48,56},{56,64},{64,7... | collective-permute-start | bytes 98312 | tf_op jit(solution)/shard_map/ppermute | solution.py:54
  53.2 8.1 %collective-permute-start.4 = (f32[16,1,512]{2,1,0:T(1,128)S(1)}, f32[16,1,512]{2,1,0:T(1,128)S(1)}, u32[]{:S(2)}, u32[]{:S(2)}) collective-permute-start(f32[16,1,512]{2,1,0:T(1,128)S(1)} %slice.1601), channel_id=1, source_target_pairs={{0,1},{1,2},{2,3},{3,4},{4,5},{5,6},{6,7},{8,9},{9,10},{10,11},{11... | collective-permute-start | bytes 98312 | tf_op jit(solution)/shard_map/ppermute | solution.py:54
  58.6 19.7 %collective-permute-start.5 = (f32[8,16,1,512]{3,2,1,0:T(1,128)}, f32[8,16,1,512]{3,2,1,0:T(1,128)}, u32[]{:S(2)}, u32[]{:S(2)}) collective-permute-start(f32[8,16,1,512]{3,2,1,0:T(1,128)} %get-tuple-element.53), channel_id=1, source_target_pairs={{0,1},{1,2},{2,3},{3,4},{4,5},{5,6},{6,7},{8,9},{9,10},{10,11},{11... | collective-permute-start | bytes 786440 | tf_op jit(solution)/shard_map/ppermute | solution.py:22
  92.8 15.2 %collective-permute-start.6 = (f32[8,1,16,512]{3,2,1,0:T(8,128)S(1)}, f32[8,1,16,512]{3,2,1,0:T(8,128)S(1)}, u32[]{:S(2)}, u32[]{:S(2)}) collective-permute-start(f32[8,1,16,512]{3,2,1,0:T(8,128)S(1)} %get-tuple-element.49), channel_id=1, source_target_pairs={{8,0},{16,8},{24,16},{32,24},{40,32},{48,40},{56,48},{64,56},{72,6... | collective-permute-start | bytes 786440 | tf_op jit(solution)/shard_map/ppermute | solution.py:23
  98.1 10.2 %collective-permute-start.7 = (f32[8,1,16,512]{3,2,1,0:T(8,128)S(1)}, f32[8,1,16,512]{3,2,1,0:T(8,128)S(1)}, u32[]{:S(2)}, u32[]{:S(2)}) collective-permute-start(f32[8,1,16,512]{3,2,1,0:T(8,128)S(1)} %get-tuple-element.48), channel_id=1, source_target_pairs={{0,8},{8,16},{16,24},{24,32},{32,40},{40,48},{48,56},{56,64},{64,7... | collective-permute-start | bytes 786440 | tf_op jit(solution)/shard_map/ppermute | solution.py:22
  100.0 11.1 %collective-permute-start.8 = (f32[8,16,1,512]{3,2,1,0:T(1,128)S(1)}, f32[8,16,1,512]{3,2,1,0:T(1,128)S(1)}, u32[]{:S(2)}, u32[]{:S(2)}) collective-permute-start(f32[8,16,1,512]{3,2,1,0:T(1,128)S(1)} %get-tuple-element.46), channel_id=1, source_target_pairs={{1,0},{2,1},{3,2},{4,3},{5,4},{6,5},{7,6},{9,8},{10,9},{11,10},{12... | collective-permute-start | bytes 786440 | tf_op jit(solution)/shard_map/ppermute | solution.py:23
  102.1 14.9 %collective-permute-start.9 = (f32[8,16,1,512]{3,2,1,0:T(1,128)S(1)}, f32[8,16,1,512]{3,2,1,0:T(1,128)S(1)}, u32[]{:S(2)}, u32[]{:S(2)}) collective-permute-start(f32[8,16,1,512]{3,2,1,0:T(1,128)S(1)} %get-tuple-element.47), channel_id=1, source_target_pairs={{0,1},{1,2},{2,3},{3,4},{4,5},{5,6},{6,7},{8,9},{9,10},{10,11},{11... | collective-permute-start | bytes 786440 | tf_op jit(solution)/shard_map/ppermute | solution.py:22
  128.3 14.1 %collective-permute-start.10 = (f32[8,1,16,512]{3,2,1,0:T(8,128)S(1)}, f32[8,1,16,512]{3,2,1,0:T(8,128)S(1)}, u32[]{:S(2)}, u32[]{:S(2)}) collective-permute-start(f32[8,1,16,512]{3,2,1,0:T(8,128)S(1)} %get-tuple-element.43), channel_id=1, source_target_pairs={{8,0},{16,8},{24,16},{32,24},{40,32},{48,40},{56,48},{64,56},{72,6... | collective-permute-start | bytes 786440 | tf_op jit(solution)/shard_map/ppermute | solution.py:23
  132.8 10.2 %collective-permute-start.11 = (f32[8,1,16,512]{3,2,1,0:T(8,128)S(1)}, f32[8,1,16,512]{3,2,1,0:T(8,128)S(1)}, u32[]{:S(2)}, u32[]{:S(2)}) collective-permute-start(f32[8,1,16,512]{3,2,1,0:T(8,128)S(1)} %get-tuple-element.42), channel_id=1, source_target_pairs={{0,8},{8,16},{16,24},{24,32},{32,40},{40,48},{48,56},{56,64},{64,7... | collective-permute-start | bytes 786440 | tf_op jit(solution)/shard_map/ppermute | solution.py:22
  134.7 11.1 %collective-permute-start.12 = (f32[8,16,1,512]{3,2,1,0:T(1,128)S(1)}, f32[8,16,1,512]{3,2,1,0:T(1,128)S(1)}, u32[]{:S(2)}, u32[]{:S(2)}) collective-permute-start(f32[8,16,1,512]{3,2,1,0:T(1,128)S(1)} %get-tuple-element.40), channel_id=1, source_target_pairs={{1,0},{2,1},{3,2},{4,3},{5,4},{6,5},{7,6},{9,8},{10,9},{11,10},{12... | collective-permute-start | bytes 786440 | tf_op jit(solution)/shard_map/ppermute | solution.py:23
  136.7 12.5 %collective-permute-start.13 = (f32[8,16,1,512]{3,2,1,0:T(1,128)S(1)}, f32[8,16,1,512]{3,2,1,0:T(1,128)S(1)}, u32[]{:S(2)}, u32[]{:S(2)}) collective-permute-start(f32[8,16,1,512]{3,2,1,0:T(1,128)S(1)} %get-tuple-element.41), channel_id=1, source_target_pairs={{0,1},{1,2},{2,3},{3,4},{4,5},{5,6},{6,7},{8,9},{9,10},{10,11},{11... | collective-permute-start | bytes 786440 | tf_op jit(solution)/shard_map/ppermute | solution.py:22
  160.5 26.2 %collective-permute-start.14 = (f32[8,1,16,512]{3,2,1,0:T(8,128)S(1)}, f32[8,1,16,512]{3,2,1,0:T(8,128)S(1)}, u32[]{:S(2)}, u32[]{:S(2)}) collective-permute-start(f32[8,1,16,512]{3,2,1,0:T(8,128)S(1)} %get-tuple-element.37), channel_id=1, source_target_pairs={{8,0},{16,8},{24,16},{32,24},{40,32},{48,40},{56,48},{64,56},{72,6... | collective-permute-start | bytes 786440 | tf_op jit(solution)/shard_map/ppermute | solution.py:23
  165.2 21.4 %collective-permute-start.15 = (f32[8,1,16,512]{3,2,1,0:T(8,128)S(1)}, f32[8,1,16,512]{3,2,1,0:T(8,128)S(1)}, u32[]{:S(2)}, u32[]{:S(2)}) collective-permute-start(f32[8,1,16,512]{3,2,1,0:T(8,128)S(1)} %get-tuple-element.36), channel_id=1, source_target_pairs={{0,8},{8,16},{16,24},{24,32},{32,40},{40,48},{48,56},{56,64},{64,7... | collective-permute-start | bytes 786440 | tf_op jit(solution)/shard_map/ppermute | solution.py:22
  167.1 19.5 %collective-permute-start.16 = (f32[8,16,1,512]{3,2,1,0:T(1,128)S(1)}, f32[8,16,1,512]{3,2,1,0:T(1,128)S(1)}, u32[]{:S(2)}, u32[]{:S(2)}) collective-permute-start(f32[8,16,1,512]{3,2,1,0:T(1,128)S(1)} %get-tuple-element.34), channel_id=1, source_target_pairs={{1,0},{2,1},{3,2},{4,3},{5,4},{6,5},{7,6},{9,8},{10,9},{11,10},{12... | collective-permute-start | bytes 786440 | tf_op jit(solution)/shard_map/ppermute | solution.py:23
  169.2 17.4 %collective-permute-start.17 = (f32[8,16,1,512]{3,2,1,0:T(1,128)S(1)}, f32[8,16,1,512]{3,2,1,0:T(1,128)S(1)}, u32[]{:S(2)}, u32[]{:S(2)}) collective-permute-start(f32[8,16,1,512]{3,2,1,0:T(1,128)S(1)} %get-tuple-element.35), channel_id=1, source_target_pairs={{0,1},{1,2},{2,3},{3,4},{4,5},{5,6},{6,7},{8,9},{9,10},{10,11},{11... | collective-permute-start | bytes 786440 | tf_op jit(solution)/shard_map/ppermute | solution.py:22
  199.6 15.9 %collective-permute-start.18 = (f32[8,1,16,512]{3,2,1,0:T(8,128)S(1)}, f32[8,1,16,512]{3,2,1,0:T(8,128)S(1)}, u32[]{:S(2)}, u32[]{:S(2)}) collective-permute-start(f32[8,1,16,512]{3,2,1,0:T(8,128)S(1)} %get-tuple-element.33), channel_id=1, source_target_pairs={{8,0},{16,8},{24,16},{32,24},{40,32},{48,40},{56,48},{64,56},{72,6... | collective-permute-start | bytes 786440 | tf_op jit(solution)/shard_map/ppermute | solution.py:23
  205.1 10.4 %collective-permute-start.19 = (f32[8,1,16,512]{3,2,1,0:T(8,128)S(1)}, f32[8,1,16,512]{3,2,1,0:T(8,128)S(1)}, u32[]{:S(2)}, u32[]{:S(2)}) collective-permute-start(f32[8,1,16,512]{3,2,1,0:T(8,128)S(1)} %get-tuple-element.32), channel_id=1, source_target_pairs={{0,8},{8,16},{16,24},{24,32},{32,40},{40,48},{48,56},{56,64},{64,7... | collective-permute-start | bytes 786440 | tf_op jit(solution)/shard_map/ppermute | solution.py:22
  207.0 12.0 %collective-permute-start.20 = (f32[8,16,1,512]{3,2,1,0:T(1,128)S(1)}, f32[8,16,1,512]{3,2,1,0:T(1,128)S(1)}, u32[]{:S(2)}, u32[]{:S(2)}) collective-permute-start(f32[8,16,1,512]{3,2,1,0:T(1,128)S(1)} %get-tuple-element.30), channel_id=1, source_target_pairs={{1,0},{2,1},{3,2},{4,3},{5,4},{6,5},{7,6},{9,8},{10,9},{11,10},{12... | collective-permute-start | bytes 786440 | tf_op jit(solution)/shard_map/ppermute | solution.py:23
  209.4 13.3 %collective-permute-start.21 = (f32[8,16,1,512]{3,2,1,0:T(1,128)S(1)}, f32[8,16,1,512]{3,2,1,0:T(1,128)S(1)}, u32[]{:S(2)}, u32[]{:S(2)}) collective-permute-start(f32[8,16,1,512]{3,2,1,0:T(1,128)S(1)} %get-tuple-element.31), channel_id=1, source_target_pairs={{0,1},{1,2},{2,3},{3,4},{4,5},{5,6},{6,7},{8,9},{9,10},{10,11},{11... | collective-permute-start | bytes 786440 | tf_op jit(solution)/shard_map/ppermute | solution.py:22
  273.2 40.2 %copy-start.36 = (s32[3]{0:T(128)S(1)}, s32[3]{0:T(128)}, u32[]{:S(2)}) copy-start(s32[3]{0:T(128)} %iota_add_fusion.3) | copy-start | bytes 40
  273.2 40.2 %copy-start.37 = (s32[2,2,8]{2,0,1:T(2,128)S(1)}, s32[2,2,8]{2,0,1:T(2,128)}, u32[]{:S(2)}) copy-start(s32[2,2,8]{2,0,1:T(2,128)} %add_subtract_fusion.1) | copy-start | bytes 388
  366.3 8.0 %collective-permute-start.26 = (f32[1,2,64]{2,1,0:T(2,128)S(1)}, f32[1,2,64]{2,1,0:T(2,128)S(1)}, u32[]{:S(2)}, u32[]{:S(2)}) collective-permute-start(f32[1,2,64]{2,1,0:T(2,128)S(1)} %get-tuple-element.120), channel_id=1, source_target_pairs={{0,8},{8,16},{16,24},{24,32},{32,40},{40,48},{48,56},{56,64},{64,7... | collective-permute-start | bytes 1544 | tf_op jit(solution)/shard_map/ppermute | solution.py:42
  370.9 4.7 collective-permute-start.27
  375.6 6.8 %collective-permute-start.28 = (f32[4,1,64]{2,1,0:T(1,128)S(1)}, f32[4,1,64]{2,1,0:T(1,128)S(1)}, u32[]{:S(2)}, u32[]{:S(2)}) collective-permute-start(f32[4,1,64]{2,1,0:T(1,128)S(1)} %get-tuple-element.104), channel_id=1, source_target_pairs={{0,1},{1,2},{2,3},{3,4},{4,5},{5,6},{6,7},{8,9},{9,10},{10,11},{11... | collective-permute-start | bytes 3080 | tf_op jit(solution)/shard_map/ppermute | solution.py:42
  379.3 6.6 %collective-permute-start.29 = (f32[4,1,64]{2,1,0:T(1,128)S(1)}, f32[4,1,64]{2,1,0:T(1,128)S(1)}, u32[]{:S(2)}, u32[]{:S(2)}) collective-permute-start(f32[4,1,64]{2,1,0:T(1,128)S(1)} %get-tuple-element.105), channel_id=1, source_target_pairs={{1,0},{2,1},{3,2},{4,3},{5,4},{6,5},{7,6},{9,8},{10,9},{11,10},{12... | collective-permute-start | bytes 3080 | tf_op jit(solution)/shard_map/ppermute | solution.py:44
  386.9 8.0 %collective-permute-start.30 = (f32[1,2,64]{2,1,0:T(2,128)S(1)}, f32[1,2,64]{2,1,0:T(2,128)S(1)}, u32[]{:S(2)}, u32[]{:S(2)}) collective-permute-start(f32[1,2,64]{2,1,0:T(2,128)S(1)} %get-tuple-element.118), channel_id=1, source_target_pairs={{0,8},{8,16},{16,24},{24,32},{32,40},{40,48},{48,56},{56,64},{64,7... | collective-permute-start | bytes 1544 | tf_op jit(solution)/shard_map/ppermute | solution.py:42
  391.6 4.7 collective-permute-start.31
  396.2 6.8 %collective-permute-start.32 = (f32[4,1,64]{2,1,0:T(1,128)S(1)}, f32[4,1,64]{2,1,0:T(1,128)S(1)}, u32[]{:S(2)}, u32[]{:S(2)}) collective-permute-start(f32[4,1,64]{2,1,0:T(1,128)S(1)} %get-tuple-element.102), channel_id=1, source_target_pairs={{0,1},{1,2},{2,3},{3,4},{4,5},{5,6},{6,7},{8,9},{9,10},{10,11},{11... | collective-permute-start | bytes 3080 | tf_op jit(solution)/shard_map/ppermute | solution.py:42
  401.1 5.5 %collective-permute-start.33 = (f32[4,1,64]{2,1,0:T(1,128)S(1)}, f32[4,1,64]{2,1,0:T(1,128)S(1)}, u32[]{:S(2)}, u32[]{:S(2)}) collective-permute-start(f32[4,1,64]{2,1,0:T(1,128)S(1)} %get-tuple-element.103), channel_id=1, source_target_pairs={{1,0},{2,1},{3,2},{4,3},{5,4},{6,5},{7,6},{9,8},{10,9},{11,10},{12... | collective-permute-start | bytes 3080 | tf_op jit(solution)/shard_map/ppermute | solution.py:44
  407.5 8.0 %collective-permute-start.34 = (f32[1,2,64]{2,1,0:T(2,128)S(1)}, f32[1,2,64]{2,1,0:T(2,128)S(1)}, u32[]{:S(2)}, u32[]{:S(2)}) collective-permute-start(f32[1,2,64]{2,1,0:T(2,128)S(1)} %get-tuple-element.116), channel_id=1, source_target_pairs={{0,8},{8,16},{16,24},{24,32},{32,40},{40,48},{48,56},{56,64},{64,7... | collective-permute-start | bytes 1544 | tf_op jit(solution)/shard_map/ppermute | solution.py:42
  410.3 6.4 %collective-permute-start.35 = (f32[1,2,64]{2,1,0:T(2,128)S(1)}, f32[1,2,64]{2,1,0:T(2,128)S(1)}, u32[]{:S(2)}, u32[]{:S(2)}) collective-permute-start(f32[1,2,64]{2,1,0:T(2,128)S(1)} %get-tuple-element.117), channel_id=1, source_target_pairs={{8,0},{16,8},{24,16},{32,24},{40,32},{48,40},{56,48},{64,56},{72,6... | collective-permute-start | bytes 1544 | tf_op jit(solution)/shard_map/ppermute | solution.py:44
  416.8 6.8 %collective-permute-start.36 = (f32[4,1,64]{2,1,0:T(1,128)S(1)}, f32[4,1,64]{2,1,0:T(1,128)S(1)}, u32[]{:S(2)}, u32[]{:S(2)}) collective-permute-start(f32[4,1,64]{2,1,0:T(1,128)S(1)} %get-tuple-element.100), channel_id=1, source_target_pairs={{0,1},{1,2},{2,3},{3,4},{4,5},{5,6},{6,7},{8,9},{9,10},{10,11},{11... | collective-permute-start | bytes 3080 | tf_op jit(solution)/shard_map/ppermute | solution.py:42
  421.1 5.5 %collective-permute-start.37 = (f32[4,1,64]{2,1,0:T(1,128)S(1)}, f32[4,1,64]{2,1,0:T(1,128)S(1)}, u32[]{:S(2)}, u32[]{:S(2)}) collective-permute-start(f32[4,1,64]{2,1,0:T(1,128)S(1)} %get-tuple-element.101), channel_id=1, source_target_pairs={{1,0},{2,1},{3,2},{4,3},{5,4},{6,5},{7,6},{9,8},{10,9},{11,10},{12... | collective-permute-start | bytes 3080 | tf_op jit(solution)/shard_map/ppermute | solution.py:44
  427.6 8.0 %collective-permute-start.38 = (f32[1,2,64]{2,1,0:T(2,128)S(1)}, f32[1,2,64]{2,1,0:T(2,128)S(1)}, u32[]{:S(2)}, u32[]{:S(2)}) collective-permute-start(f32[1,2,64]{2,1,0:T(2,128)S(1)} %get-tuple-element.114), channel_id=1, source_target_pairs={{0,8},{8,16},{16,24},{24,32},{32,40},{40,48},{48,56},{56,64},{64,7... | collective-permute-start | bytes 1544 | tf_op jit(solution)/shard_map/ppermute | solution.py:42
  429.5 7.3 %collective-permute-start.39 = (f32[1,2,64]{2,1,0:T(2,128)S(1)}, f32[1,2,64]{2,1,0:T(2,128)S(1)}, u32[]{:S(2)}, u32[]{:S(2)}) collective-permute-start(f32[1,2,64]{2,1,0:T(2,128)S(1)} %get-tuple-element.115), channel_id=1, source_target_pairs={{8,0},{16,8},{24,16},{32,24},{40,32},{48,40},{56,48},{64,56},{72,6... | collective-permute-start | bytes 1544 | tf_op jit(solution)/shard_map/ppermute | solution.py:44
  436.9 6.8 %collective-permute-start.40 = (f32[4,1,64]{2,1,0:T(1,128)S(1)}, f32[4,1,64]{2,1,0:T(1,128)S(1)}, u32[]{:S(2)}, u32[]{:S(2)}) collective-permute-start(f32[4,1,64]{2,1,0:T(1,128)S(1)} %get-tuple-element.98), channel_id=1, source_target_pairs={{0,1},{1,2},{2,3},{3,4},{4,5},{5,6},{6,7},{8,9},{9,10},{10,11},{11... | collective-permute-start | bytes 3080 | tf_op jit(solution)/shard_map/ppermute | solution.py:42
  441.7 5.5 %collective-permute-start.41 = (f32[4,1,64]{2,1,0:T(1,128)S(1)}, f32[4,1,64]{2,1,0:T(1,128)S(1)}, u32[]{:S(2)}, u32[]{:S(2)}) collective-permute-start(f32[4,1,64]{2,1,0:T(1,128)S(1)} %get-tuple-element.99), channel_id=1, source_target_pairs={{1,0},{2,1},{3,2},{4,3},{5,4},{6,5},{7,6},{9,8},{10,9},{11,10},{12... | collective-permute-start | bytes 3080 | tf_op jit(solution)/shard_map/ppermute | solution.py:44
  448.1 8.0 %collective-permute-start.42 = (f32[1,2,64]{2,1,0:T(2,128)S(1)}, f32[1,2,64]{2,1,0:T(2,128)S(1)}, u32[]{:S(2)}, u32[]{:S(2)}) collective-permute-start(f32[1,2,64]{2,1,0:T(2,128)S(1)} %get-tuple-element.112), channel_id=1, source_target_pairs={{0,8},{8,16},{16,24},{24,32},{32,40},{40,48},{48,56},{56,64},{64,7... | collective-permute-start | bytes 1544 | tf_op jit(solution)/shard_map/ppermute | solution.py:42
  450.1 7.3 %collective-permute-start.43 = (f32[1,2,64]{2,1,0:T(2,128)S(1)}, f32[1,2,64]{2,1,0:T(2,128)S(1)}, u32[]{:S(2)}, u32[]{:S(2)}) collective-permute-start(f32[1,2,64]{2,1,0:T(2,128)S(1)} %get-tuple-element.113), channel_id=1, source_target_pairs={{8,0},{16,8},{24,16},{32,24},{40,32},{48,40},{56,48},{64,56},{72,6... | collective-permute-start | bytes 1544 | tf_op jit(solution)/shard_map/ppermute | solution.py:44
  457.4 7.5 %collective-permute-start.44 = (f32[4,1,64]{2,1,0:T(1,128)S(1)}, f32[4,1,64]{2,1,0:T(1,128)S(1)}, u32[]{:S(2)}, u32[]{:S(2)}) collective-permute-start(f32[4,1,64]{2,1,0:T(1,128)S(1)} %get-tuple-element.96), channel_id=1, source_target_pairs={{0,1},{1,2},{2,3},{3,4},{4,5},{5,6},{6,7},{8,9},{9,10},{10,11},{11... | collective-permute-start | bytes 3080 | tf_op jit(solution)/shard_map/ppermute | solution.py:42
  460.2 5.5 %collective-permute-start.45 = (f32[4,1,64]{2,1,0:T(1,128)S(1)}, f32[4,1,64]{2,1,0:T(1,128)S(1)}, u32[]{:S(2)}, u32[]{:S(2)}) collective-permute-start(f32[4,1,64]{2,1,0:T(1,128)S(1)} %get-tuple-element.97), channel_id=1, source_target_pairs={{1,0},{2,1},{3,2},{4,3},{5,4},{6,5},{7,6},{9,8},{10,9},{11,10},{12... | collective-permute-start | bytes 3080 | tf_op jit(solution)/shard_map/ppermute | solution.py:44
  466.7 8.0 %collective-permute-start.46 = (f32[1,2,64]{2,1,0:T(2,128)S(1)}, f32[1,2,64]{2,1,0:T(2,128)S(1)}, u32[]{:S(2)}, u32[]{:S(2)}) collective-permute-start(f32[1,2,64]{2,1,0:T(2,128)S(1)} %get-tuple-element.110), channel_id=1, source_target_pairs={{0,8},{8,16},{16,24},{24,32},{32,40},{40,48},{48,56},{56,64},{64,7... | collective-permute-start | bytes 1544 | tf_op jit(solution)/shard_map/ppermute | solution.py:42
  468.6 7.3 %collective-permute-start.47 = (f32[1,2,64]{2,1,0:T(2,128)S(1)}, f32[1,2,64]{2,1,0:T(2,128)S(1)}, u32[]{:S(2)}, u32[]{:S(2)}) collective-permute-start(f32[1,2,64]{2,1,0:T(2,128)S(1)} %get-tuple-element.111), channel_id=1, source_target_pairs={{8,0},{16,8},{24,16},{32,24},{40,32},{48,40},{56,48},{64,56},{72,6... | collective-permute-start | bytes 1544 | tf_op jit(solution)/shard_map/ppermute | solution.py:44
  476.0 7.7 %collective-permute-start.48 = (f32[4,1,64]{2,1,0:T(1,128)S(1)}, f32[4,1,64]{2,1,0:T(1,128)S(1)}, u32[]{:S(2)}, u32[]{:S(2)}) collective-permute-start(f32[4,1,64]{2,1,0:T(1,128)S(1)} %get-tuple-element.94), channel_id=1, source_target_pairs={{0,1},{1,2},{2,3},{3,4},{4,5},{5,6},{6,7},{8,9},{9,10},{10,11},{11... | collective-permute-start | bytes 3080 | tf_op jit(solution)/shard_map/ppermute | solution.py:42
  478.8 5.5 %collective-permute-start.49 = (f32[4,1,64]{2,1,0:T(1,128)S(1)}, f32[4,1,64]{2,1,0:T(1,128)S(1)}, u32[]{:S(2)}, u32[]{:S(2)}) collective-permute-start(f32[4,1,64]{2,1,0:T(1,128)S(1)} %get-tuple-element.95), channel_id=1, source_target_pairs={{1,0},{2,1},{3,2},{4,3},{5,4},{6,5},{7,6},{9,8},{10,9},{11,10},{12... | collective-permute-start | bytes 3080 | tf_op jit(solution)/shard_map/ppermute | solution.py:44
  489.6 25.5 %copy-start.21 = (f32[1,16,512]{2,1,0:T(8,128)S(1)}, f32[1,16,512]{2,1,0:T(8,128)}, u32[]{:S(2)}) copy-start(f32[1,16,512]{2,1,0:T(8,128)} %copy-done.20) | copy-start | bytes 98308
  489.6 25.5 %copy-start.23 = (f32[512]{0:T(512)S(1)}, f32[512]{0:T(512)}, u32[]{:S(2)}) copy-start(f32[512]{0:T(512)} %copy-done.22) | copy-start | bytes 6148
  489.6 25.5 %copy-start.32 = (f32[16]{0:T(128)S(1)}, f32[16]{0:T(128)}, u32[]{:S(2)}) copy-start(f32[16]{0:T(128)} %copy-done.30) | copy-start | bytes 196
  489.6 25.5 %copy-start.35 = (f32[16]{0:T(128)S(1)}, f32[16]{0:T(128)}, u32[]{:S(2)}) copy-start(f32[16]{0:T(128)} %copy-done.33) | copy-start | bytes 196
  490.8 27.4 %copy-start.5 = (f32[16,16,512]{2,1,0:T(8,128)}, f32[16,16,512]{2,1,0:T(8,128)S(1)}, u32[]{:S(2)}) copy-start(f32[16,16,512]{2,1,0:T(8,128)S(1)} %fusion.113) | copy-start | bytes 1572868
  490.8 24.3 %copy-start.9 = (f32[16,16,512]{2,1,0:T(8,128)S(1)}, f32[16,16,512]{2,1,0:T(8,128)}, u32[]{:S(2)}) copy-start(f32[16,16,512]{2,1,0:T(8,128)} %param.9) | copy-start | bytes 1572868
  490.8 9.8 %collective-permute-start.50 = (f32[1,16,512]{2,1,0:T(8,128)S(1)}, f32[1,16,512]{2,1,0:T(8,128)S(1)}, u32[]{:S(2)}, u32[]{:S(2)}) collective-permute-start(f32[1,16,512]{2,1,0:T(8,128)S(1)} %get-tuple-element.90), channel_id=1, source_target_pairs={{8,0},{16,8},{24,16},{32,24},{40,32},{48,40},{56,48},{64,56},{72,6... | collective-permute-start | bytes 98312 | tf_op jit(solution)/shard_map/ppermute | solution.py:44
  496.7 7.6 %collective-permute-start.51 = (f32[1,16,512]{2,1,0:T(8,128)S(1)}, f32[1,16,512]{2,1,0:T(8,128)S(1)}, u32[]{:S(2)}, u32[]{:S(2)}) collective-permute-start(f32[1,16,512]{2,1,0:T(8,128)S(1)} %get-tuple-element.89), channel_id=1, source_target_pairs={{0,8},{8,16},{16,24},{24,32},{32,40},{40,48},{48,56},{56,64},{64,7... | collective-permute-start | bytes 98312 | tf_op jit(solution)/shard_map/ppermute | solution.py:42
  504.4 6.1 %collective-permute-start.52 = (f32[18,1,512]{2,1,0:T(1,128)S(1)}, f32[18,1,512]{2,1,0:T(1,128)S(1)}, u32[]{:S(2)}, u32[]{:S(2)}) collective-permute-start(f32[18,1,512]{2,1,0:T(1,128)S(1)} %get-tuple-element.85), channel_id=1, source_target_pairs={{1,0},{2,1},{3,2},{4,3},{5,4},{6,5},{7,6},{9,8},{10,9},{11,10},{12... | collective-permute-start | bytes 110600 | tf_op jit(solution)/shard_map/ppermute | solution.py:44
  508.4 6.8 %collective-permute-start.53 = (f32[18,1,512]{2,1,0:T(1,128)S(1)}, f32[18,1,512]{2,1,0:T(1,128)S(1)}, u32[]{:S(2)}, u32[]{:S(2)}) collective-permute-start(f32[18,1,512]{2,1,0:T(1,128)S(1)} %get-tuple-element.86), channel_id=1, source_target_pairs={{0,1},{1,2},{2,3},{3,4},{4,5},{5,6},{6,7},{8,9},{9,10},{10,11},{11... | collective-permute-start | bytes 110600 | tf_op jit(solution)/shard_map/ppermute | solution.py:42
  (42 other events, 318.1 us)
where the time goes:
time: 527 us; the launch traced here: 519 us
  starting transfers between devices  198 us (38%)
  local copies, waits for them, and re-layouts  160 us (30%)
  other arithmetic  86.7 us (16%)
  waiting for transfers between devices  54.3 us (10%)
  matrix products  17.1 us (3%)
    reshape x2, local copies, waits for them, and re-layouts, coarse_operator(): edge_term.reshape(2, 2, 2, size_x // 8, 8, size_z // 8, 8, size_y // 8, 8)  82.1 us
    ppermute x16, starting transfers between devices, extended_2(): lax.ppermute(head, axis, [((i + 1) % count, i) for i in range(ends)])  67.3 us
    ppermute x16, starting transfers between devices, extended_2(): lax.ppermute(tail, axis, [(i, (i + 1) % count) for i in range(ends)])  49.6 us
    reduce_sum x4, other arithmetic, body(): basis = basis / jnp.sum(basis, axis=0)  42.8 us
    ppermute x10, starting transfers between devices, extended(): lax.ppermute(last, axis, up)  40.7 us
    slice x29, local copies, waits for them, and re-layouts, apply_coarse(): coarse_op[ix, iz, iy]  33.8 us
    ppermute x10, starting transfers between devices, extended(): lax.ppermute(initial, axis, [(b, a) for a, b in up])  33.4 us
    ppermute x16, waiting for transfers between devices, extended_2(): lax.ppermute(head, axis, [((i + 1) % count, i) for i in range(ends)])  22.7 us
  transfers between devices with their start and end apart: 54, of which 23 were waited for; matrix products, arithmetic and copies ran while one was open for 11% of the time, Pallas kernels for 0%

commit v1 on v0

v1 whole, which is shorter than its diff:
```python
import jax
import jax.numpy as jnp
from jax import lax
from jax.experimental import pallas as pl
from jax.experimental.pallas import tpu as pltpu
from jax.sharding import PartitionSpec as P

COARSE_ITERS = 6
COARSE_STEP = 0.5
NT = 4
NXE = 24
NR = 32
F32 = jnp.float32
INTERPRET = False


def iota(shape, dim):
    return lax.broadcasted_iota(jnp.int32, shape, dim)


def roll(value, shift):
    return pltpu.roll(value, shift, 1)


def main_kernel(txe, tye, tze, acc, src, wcell, wrate,
                basis_out, coarse_out, rhs_out, xh_out, zh_out,
                tx_s, ty_s, tz_s, tym_s, dd_s, b0, b1, sums, sem_in, sem_out, sem_x):
    loads = []
    for t in range(NT):
        lanes = pl.ds(128 * t, 128)
        for k, (hbm, vmem) in enumerate(((txe, tx_s), (tye, ty_s), (tze, tz_s))):
            copy = pltpu.make_async_copy(hbm.at[:, :, lanes], vmem.at[:, t], sem_in.at[k * NT + t])
            copy.start()
            loads.append(copy)
    rhs_out[...] = src[...]
    lane_y = iota((1, 512), 1)
    for w in range(16):
        cell = wcell[w, 0]
        row = cell // 512
        x, z, y = row // 16, row % 16, cell % 512
        old = rhs_out[x, pl.ds(z, 1), :]
        rhs_out[x, pl.ds(z, 1), :] = old + jnp.where(lane_y == y, wrate[w, 0], 0.0)
    for copy in loads:
        copy.wait()

    sub = iota((8, 128), 0)
    lane = iota((8, 128), 1)
    yo = lane % 8
    lane_par = (lane // 8) % 2
    zero = jnp.zeros((8, 128), F32)

    def to_prev(value, left):
        return roll(jnp.where(lane == 127, left, value), 1)

    def to_next(value, right):
        return roll(jnp.where(lane == 0, right, value), 127)

    def first(index, carry):
        X, t = index // NT, index % NT
        tl = jnp.maximum(t - 1, 0)
        par = ((X + 4) // 8 + 1) % 2
        xo = (X + 4) % 8
        own_base, flip_base = par * 4, 4 - par * 4
        lo_x = (xo == 0).astype(F32)
        hi_x = (xo == 7).astype(F32)
        for r in range(3):
            R = 4 + 8 * r
            rows = pl.ds(R, 8)
            tx, txm = tx_s[X + 1, t, rows, :], tx_s[X, t, rows, :]
            tz, tzm = tz_s[X, t, rows, :], tz_s[X, t, pl.ds(R - 1, 8), :]
            ty = ty_s[X, t, rows, :]
            tym = to_prev(ty, ty_s[X, tl, rows, :])
            tym = jnp.where((lane == 0) & (t == 0), 0.0, tym)
            diag = tx + txm + tz + tzm + ty + tym
            half = diag * 0.5 + 1e-30
            tym_s[X, t, rows, :] = tym
            dd_s[X, t, rows, :] = half
            txb = lo_x * txm + hi_x * tx
            tzb = jnp.where(sub == 3, tz, jnp.where(sub == 4, tzm, 0.0))
            tyb = jnp.where(yo == 7, ty, jnp.where(yo == 0, tym, 0.0))
            own = half + (diag - txb - tzb - tyb)
            inv = 1.0 / (own + txb + tzb + tyb)
            own, vx, vz, vy = own * inv, txb * inv, tzb * inv, tyb * inv
            row_par = jnp.where(sub < 4, (r + 1) % 2, r % 2)
            for c in range(2):
                for d in range(2):
                    in_row, in_lane = row_par == c, lane_par == d
                    value = jnp.where(in_row, jnp.where(in_lane, own, vy), jnp.where(in_lane, vz, 0.0))
                    b0[own_base + 2 * c + d, X, t, rows, :] = value
                    b0[flip_base + 2 * c + d, X, t, rows, :] = jnp.where(in_row & in_lane, vx, 0.0)
                    b1[flip_base + 2 * c + d, X, t, rows, :] = zero
        return carry

    lax.fori_loop(0, NXE * NT, first, 0)

    def sweep(old, new, k):
        reach = min(k, 3)

        def block(X, t, n_slots, par):
            tl, tr = jnp.maximum(t - 1, 0), jnp.minimum(t + 1, NT - 1)
            own_base, flip_base = par * 4, 4 - par * 4
            for r in range(3):
                R = 4 + 8 * r
                rows = pl.ds(R, 8)
                tx, txm = tx_s[X + 1, t, rows, :], tx_s[X, t, rows, :]
                tz, tzm = tz_s[X, t, rows, :], tz_s[X, t, pl.ds(R - 1, 8), :]
                ty, tym = ty_s[X, t, rows, :], tym_s[X, t, rows, :]
                half = dd_s[X, t, rows, :]
                row_par = jnp.where(sub < 4, (r + 1) % 2, r % 2)
                values = []
                for cd in range(n_slots):
                    c, d = (cd // 2) % 2, cd % 2
                    s = (own_base if cd < 4 else flip_base) + cd % 4
                    b = old[s, X, t, rows, :]
                    v = half * b
                    v += tx * old[s, X + 1, t, rows, :]
                    v += txm * old[s, X - 1, t, rows, :]
                    v += tz * old[s, X, t, pl.ds(R + 1, 8), :]
                    v += tzm * old[s, X, t, pl.ds(R - 1, 8), :]
                    v += ty * to_next(b, old[s, X, tr, rows, :])
                    v += tym * to_prev(b, old[s, X, tl, rows, :])
                    if k == 4:
                        out_z = (row_par != c) & ((sub == 0) | (sub == 7))
                        out_y = (lane_par != d) & ((yo == 3) | (yo == 4))
                        v = jnp.where(out_z | out_y, 0.0, v)
                    values.append(v)
                total = values[0]
                for v in values[1:]:
                    total = total + v
                inv = 1.0 / total
                for cd in range(n_slots):
                    s = (own_base if cd < 4 else flip_base) + cd % 4
                    new[s, X, t, rows, :] = values[cd] * inv

        def step(index, carry):
            X, t = index // NT, index % NT
            par = ((X + 4) // 8 + 1) % 2
            xo = (X + 4) % 8
            dist = jnp.where(xo < 4, xo + 1, 8 - xo)

            @pl.when(dist <= reach)
            def _():
                block(X, t, 8, par)

            @pl.when(dist > reach)
            def _():
                block(X, t, 4, par)

            return carry

        lax.fori_loop((k - 1) * NT, (25 - k) * NT, step, 0)

    sweep(b0, b1, 2)
    sweep(b1, b0, 3)
    sweep(b0, b1, 4)

    stores = []
    for s in range(8):
        for t in range(NT):
            copy = pltpu.make_async_copy(b1.at[s, pl.ds(4, 16), t, pl.ds(8, 16), :],
                                         basis_out.at[s, :, :, pl.ds(128 * t, 128)], sem_out.at[s * NT + t])
            copy.start()
            stores.append(copy)
            for side, X in enumerate((3, 20)):
                copy = pltpu.make_async_copy(b1.at[s, X, t, pl.ds(8, 16), :],
                                             xh_out.at[s, side, :, pl.ds(128 * t, 128)],
                                             sem_x.at[(s * NT + t) * 2 + side])
                copy.start()
                stores.append(copy)

    flat = b1.reshape(8 * NXE * NT * NR, 128)

    def rows_of(index, carry):
        s, t = index // NT, index % NT
        lanes = pl.ds(pl.multiple_of(t * 128, 128), 128)
        for side, R in enumerate((7, 24)):
            for half in range(2):
                start = ((s * NXE + 4 + 8 * half) * NT + t) * NR + R
                zh_out[s, side, 8 * half:8 * half + 8, lanes] = flat[pl.ds(start, 8, stride=NT * NR), :]
        return carry

    lax.fori_loop(0, 8 * NT, rows_of, 0)

    for zb in range(2):
        R = 8 + 8 * zb

        def edges(index, carry):
            xb, t = index // NT, index % NT
            tl, tr = jnp.maximum(t - 1, 0), jnp.minimum(t + 1, NT - 1)
            rows = pl.ds(R, 8)
            lanes = pl.ds(pl.multiple_of(t * 128, 128), 128)
            own_base, flip_base = xb * 4, 4 - xb * 4
            groups = [[None] * 4 for _ in range(3)]
            scale = zero
            right = zero
            for xo in range(8):
                X = 4 + xb * 8 + xo
                x = xb * 8 + xo
                tz, tzm = tz_s[X, t, rows, :], tz_s[X, t, pl.ds(R - 1, 8), :]
                ty, tym = ty_s[X, t, rows, :], tym_s[X, t, rows, :]
                tzb = jnp.where(sub == 7, tz, jnp.where(sub == 0, tzm, 0.0))
                tyb = jnp.where(yo == 7, ty, jnp.where(yo == 0, tym, 0.0))
                central = acc[x, 8 * zb:8 * zb + 8, lanes] + tzb + tyb
                if xo == 0:
                    txb, xn = tx_s[X, t, rows, :], X - 1
                    central = central + txb
                if xo == 7:
                    txb, xn = tx_s[X + 1, t, rows, :], X + 1
                    central = central + txb
                scale = scale + central
                right = right + rhs_out[x, 8 * zb:8 * zb + 8, lanes]
                which = [(0, own_base)]
                if xo < 3:
                    which.append((1, flip_base))
                if xo > 4:
                    which.append((2, flip_base))
                for g, base in which:
                    for cd in range(4):
                        s = base + cd
                        b = b1[s, X, t, rows, :]
                        bz = jnp.where(sub == 7, b1[s, X, t, pl.ds(R + 1, 8), :], b1[s, X, t, pl.ds(R - 1, 8), :])
                        by = jnp.where(yo == 7, to_next(b, b1[s, X, tr, rows, :]), to_prev(b, b1[s, X, tl, rows, :]))
                        e = central * b - tzb * bz - tyb * by
                        if xo in (0, 7):
                            e = e - txb * b1[s, xn, t, rows, :]
                        groups[g][cd] = e if groups[g][cd] is None else groups[g][cd] + e
            for g in range(3):
                for cd in range(4):
                    u = xb * 12 + g * 4 + cd
                    sums[t, pl.ds(pl.multiple_of(u * 16 + 8 * zb, 8), 8), :] = groups[g][cd]
            sums[t, pl.ds(pl.multiple_of((24 + xb) * 16 + 8 * zb, 8), 8), :] = scale
            sums[t, pl.ds(pl.multiple_of((26 + xb) * 16 + 8 * zb, 8), 8), :] = right
            return carry

        lax.fori_loop(0, 2 * NT, edges, 0)

    l_y, l_j = iota((128, 128), 0), iota((128, 128), 1)
    folded = jnp.zeros((448, 128), F32)
    for t in range(NT):
        target = ((l_y % 8) // 4) * 64 + 16 * t + l_y // 8
        folded = folded + jnp.dot(sums[t], (l_j == target).astype(F32), precision=lax.Precision.HIGHEST,
                                  preferred_element_type=F32)
    o, i = iota((128, 448), 0), iota((128, 448), 1)
    pick = ((i // 16 == o % 32) & ((i % 16) // 4 == o // 32)).astype(F32)
    quarters = jnp.dot(pick, folded, precision=lax.Precision.HIGHEST, preferred_element_type=F32)

    lane1 = iota((1, 128), 1)
    odd = lane1 % 2 == 1
    low = lane1 < 64

    def unit(q, u):
        return quarters[q * 32 + u:q * 32 + u + 1, :]

    def halves(value):
        return value + roll(value, 64)

    for xb in range(2):
        for dx, g in ((0, 1), (1, 0), (2, 2)):
            for dz in range(3):
                parts = []
                for zb in range(2):
                    c = zb if dz == 1 else 1 - zb
                    vs = []
                    for d in range(2):
                        u = xb * 12 + g * 4 + c * 2 + d
                        if dz == 0:
                            vs.append(unit(2 * zb, u))
                        elif dz == 2:
                            vs.append(unit(2 * zb + 1, u))
                        else:
                            vs.append(unit(2 * zb, u) + unit(2 * zb + 1, u))
                    own = jnp.where(odd, vs[1], vs[0])
                    flip = jnp.where(odd, vs[0], vs[1])
                    turned = roll(flip, 64)
                    parts.append((flip, halves(own), turned) if zb == 0 else (turned, halves(own), flip))
                for dy in range(3):
                    k = dx * 9 + dz * 3 + dy
                    coarse_out[xb, k:k + 1, :] = jnp.where(low, parts[0][dy], parts[1][dy])
        for k, u in ((27, 26 + xb), (28, 24 + xb)):
            parts = [halves(unit(2 * zb, u) + unit(2 * zb + 1, u)) for zb in range(2)]
            coarse_out[xb, k:k + 1, :] = jnp.where(low, parts[0], parts[1])
        coarse_out[xb, 29:32, :] = jnp.zeros((3, 128), F32)

    for copy in stores:
        copy.wait()


def finish_kernel(txe, tye, tze, basis, xh, zh, c4, acc, rhs, pressure_out, residual_out,
                  tx_s, ty_s, tz_s, g_s, p_s, sem_in):
    loads = []
    for t in range(NT):
        lanes = pl.ds(128 * t, 128)
        for k, (hbm, vmem) in enumerate(((txe.at[pl.ds(4, 17)], tx_s), (tye.at[pl.ds(4, 16)], ty_s),
                                         (tze.at[pl.ds(4, 16)], tz_s))):
            copy = pltpu.make_async_copy(hbm.at[:, pl.ds(0, 24), lanes], vmem.at[:, t], sem_in.at[k * NT + t])
            copy.start()
            loads.append(copy)
    sub = iota((8, 128), 0)
    lane = iota((8, 128), 1)
    upper = sub >= 4

    j, y = iota((128, 512), 0), iota((128, 512), 1)
    block = y // 8
    side = jnp.where(y % 8 >= 4, 1, -1)
    spread = []
    for d in range(2):
        node = jnp.where(block % 2 == d, block, block + side)
        spread.append(jnp.dot(c4[...], (j == node).astype(F32), precision=lax.Precision.HIGHEST,
                              preferred_element_type=F32))
    for nx in range(4):
        for c in range(2):
            for d in range(2):
                def row(nz):
                    return spread[d][nx * 4 + nz:nx * 4 + nz + 1, :]
                if c == 0:
                    tiles = (row(1), row(1)), (row(1), row(3))
                else:
                    tiles = (row(0), row(2)), (row(2), row(2))
                for zb in range(2):
                    for t in range(NT):
                        a, b = (jnp.broadcast_to(v[:, 128 * t:128 * t + 128], (8, 128)) for v in tiles[zb])
                        g_s[nx, 2 * c + d, t, 8 * zb:8 * zb + 8, :] = jnp.where(upper, b, a)

    def plane_nodes(X):
        block_x = (X + 4) // 8 - 1
        par = (block_x + 2) % 2
        up = (X + 4) % 8 >= 4
        flip = block_x + 1 + jnp.where(up, 1, -1)
        own = block_x + 1
        return jnp.where(par == 0, own, flip), jnp.where(par == 0, flip, own)

    def prolong(read, X, t, zb):
        n0, n1 = plane_nodes(X)
        total = None
        for s in range(8):
            n = n0 if s < 4 else n1
            term = read(s) * g_s[n, s % 4, t, 8 * zb:8 * zb + 8, :]
            total = term if total is None else total + term
        return total

    def pressures(index, carry):
        x, t = index // NT, index % NT
        lanes = pl.ds(pl.multiple_of(t * 128, 128), 128)
        for zb in range(2):
            p = prolong(lambda s: basis[s, x, 8 * zb:8 * zb + 8, lanes], x + 4, t, zb)
            p_s[x + 1, t, 8 + 8 * zb:16 + 8 * zb, :] = p
            pressure_out[x, 8 * zb:8 * zb + 8, lanes] = p
        return carry

    lax.fori_loop(0, 16 * NT, pressures, 0)

    def outer(t, carry):
        lanes = pl.ds(pl.multiple_of(t * 128, 128), 128)
        for zb in range(2):
            for s_x, X, at in ((0, 3, 0), (1, 20, 17)):
                p = prolong(lambda s: xh[s, s_x, 8 * zb:8 * zb + 8, lanes], X, t, zb)
                p_s[at, t, 8 + 8 * zb:16 + 8 * zb, :] = p
        return carry

    lax.fori_loop(0, NT, outer, 0)
    flat = p_s.reshape(18 * NT * NR, 128)
    for t in range(NT):
        cols = slice(128 * t, 128 * t + 128)
        for s_z, R in ((0, 7), (1, 24)):
            for half in range(2):
                total = None
                for s in range(8):
                    a, c, d = s // 4, (s // 2) % 2, s % 2
                    nz = (1, 0)[c] if s_z == 0 else (3, 2)[c]
                    def row(nx):
                        return jnp.broadcast_to(spread[d][nx * 4 + nz:nx * 4 + nz + 1, cols], (8, 128))
                    if a == 0:
                        value = row(1) if half == 0 else jnp.where(upper, row(3), row(1))
                    else:
                        value = jnp.where(upper, row(2), row(0)) if half == 0 else row(2)
                    term = zh[s, s_z, 8 * half:8 * half + 8, cols] * value
                    total = term if total is None else total + term
                flat[pl.ds(((1 + 8 * half) * NT + t) * NR + R, 8, stride=NT * NR), :] = total
    for copy in loads:
        copy.wait()

    def to_prev(value, left):
        return roll(jnp.where(lane == 127, left, value), 1)

    def to_next(value, right):
        return roll(jnp.where(lane == 0, right, value), 127)

    def residuals(index, carry):
        x, t = index // NT, index % NT
        lanes = pl.ds(pl.multiple_of(t * 128, 128), 128)
        tl, tr = jnp.maximum(t - 1, 0), jnp.minimum(t + 1, NT - 1)
        for zb in range(2):
            R = 8 + 8 * zb
            rows = pl.ds(R, 8)
            p = p_s[x + 1, t, rows, :]
            ty = ty_s[x, t, rows, :]
            tym = jnp.where((lane == 0) & (t == 0), 0.0, to_prev(ty, ty_s[x, tl, rows, :]))
            flow = acc[x, 8 * zb:8 * zb + 8, lanes] * p
            flow += tx_s[x + 1, t, rows, :] * (p - p_s[x + 2, t, rows, :])
            flow += tx_s[x, t, rows, :] * (p - p_s[x, t, rows, :])
            flow += tz_s[x, t, rows, :] * (p - p_s[x + 1, t, pl.ds(R + 1, 8), :])
            flow += tz_s[x, t, pl.ds(R - 1, 8), :] * (p - p_s[x + 1, t, pl.ds(R - 1, 8), :])
            flow += ty * (p - to_next(p, p_s[x + 1, tr, rows, :]))
            flow += tym * (p - to_prev(p, p_s[x + 1, tl, rows, :]))
            residual_out[x, 8 * zb:8 * zb + 8, lanes] = rhs[x, 8 * zb:8 * zb + 8, lanes] - flow
        return carry

    lax.fori_loop(0, 16 * NT, residuals, 0)


VMEM_SPEC = pl.BlockSpec(memory_space=pltpu.VMEM)
SMEM_SPEC = pl.BlockSpec(memory_space=pltpu.SMEM)
ANY_SPEC = pl.BlockSpec(memory_space=pl.ANY)


def run_main(txe, tye, tze, acc, src, wcell, wrate):
    field = pltpu.VMEM((NXE, NT, NR, 128), F32)
    return pl.pallas_call(
        main_kernel,
        name="sweeps",
        out_shape=(jax.ShapeDtypeStruct((8, 16, 16, 512), F32), jax.ShapeDtypeStruct((2, 32, 128), F32),
                   jax.ShapeDtypeStruct((16, 16, 512), F32), jax.ShapeDtypeStruct((8, 2, 16, 512), F32),
                   jax.ShapeDtypeStruct((8, 2, 16, 512), F32)),
        in_specs=[ANY_SPEC] * 3 + [VMEM_SPEC] * 2 + [SMEM_SPEC] * 2,
        out_specs=(ANY_SPEC, VMEM_SPEC, VMEM_SPEC, ANY_SPEC, VMEM_SPEC),
        scratch_shapes=[
            pltpu.VMEM((NXE + 1, NT, NR, 128), F32), field, field, field, field,
            pltpu.VMEM((8, NXE, NT, NR, 128), F32), pltpu.VMEM((8, NXE, NT, NR, 128), F32),
            pltpu.VMEM((NT, 448, 128), F32),
            pltpu.SemaphoreType.DMA((3 * NT,)), pltpu.SemaphoreType.DMA((8 * NT,)),
            pltpu.SemaphoreType.DMA((16 * NT,)),
        ],
        compiler_params=pltpu.CompilerParams(vmem_limit_bytes=60 * 1024 * 1024),
        interpret=INTERPRET,
    )(txe, tye, tze, acc, src, wcell, wrate)


def run_finish(txe, tye, tze, basis, xh, zh, c4, acc, rhs):
    return pl.pallas_call(
        finish_kernel,
        name="finish",
        out_shape=(jax.ShapeDtypeStruct((16, 16, 512), F32), jax.ShapeDtypeStruct((16, 16, 512), F32)),
        in_specs=[ANY_SPEC] * 3 + [VMEM_SPEC] * 6,
        out_specs=(VMEM_SPEC, VMEM_SPEC),
        scratch_shapes=[
            pltpu.VMEM((17, NT, 24, 128), F32), pltpu.VMEM((16, NT, 24, 128), F32), pltpu.VMEM((16, NT, 24, 128), F32),
            pltpu.VMEM((4, 4, NT, 16, 128), F32), pltpu.VMEM((18, NT, NR, 128), F32),
            pltpu.SemaphoreType.DMA((3 * NT,)),
        ],
        compiler_params=pltpu.CompilerParams(vmem_limit_bytes=60 * 1024 * 1024),
        interpret=INTERPRET,
    )(txe, tye, tze, basis, xh, zh, c4, acc, rhs)


def shift_up(value, axis):
    size = lax.axis_size(axis)
    return lax.ppermute(value, axis, [(i, i + 1) for i in range(size - 1)])


def shift_down(value, axis):
    size = lax.axis_size(axis)
    return lax.ppermute(value, axis, [(i + 1, i) for i in range(size - 1)])


def extend(tx, ty, tz):
    up = jnp.concatenate([tx[:, 12:], ty[:, 12:], tz[:, 11:]], 1)
    down = jnp.concatenate([tx[:, :4], ty[:, :4], tz[:, :4]], 1)
    low, high = shift_up(up, "gz"), shift_down(down, "gz")
    fill = jnp.zeros((16, 4, 512), F32)
    txz = jnp.concatenate([low[:, :4], tx, high[:, :4]], 1)
    tyz = jnp.concatenate([low[:, 4:8], ty, high[:, 4:8]], 1)
    tzz = jnp.concatenate([low[:, 9:13], tz, high[:, 8:12]], 1)
    up = jnp.concatenate([txz[11:], tyz[12:], tzz[12:]], 0)
    down = jnp.concatenate([txz[:4], tyz[:4], tzz[:4]], 0)
    lowx, highx = shift_up(up, "tile"), shift_down(down, "tile")
    txe = jnp.pad(jnp.concatenate([lowx[:5], txz, highx[:4]], 0), ((0, 0), (4, 4), (0, 0)))
    tye = jnp.pad(jnp.concatenate([lowx[5:9], tyz, highx[4:8]], 0), ((0, 0), (4, 4), (0, 0)))
    tze = jnp.pad(jnp.concatenate([lowx[9:13], tzz, highx[8:12]], 0), ((0, 0), (4, 4), (0, 0)))
    extra = jnp.pad(low[:, 8:9], ((4, 4), (3, 28), (0, 0)))
    return txe, tye, tze + extra


def coarse_outer(value):
    for axis, dim in (("tile", 0), ("gz", 1)):
        head = lax.slice_in_dim(value, 0, 1, axis=dim)
        tail = lax.slice_in_dim(value, value.shape[dim] - 1, value.shape[dim], axis=dim)
        value = jnp.concatenate([shift_up(tail, axis), value, shift_down(head, axis)], axis=dim)
    return value


def coarse_solve(packed):
    op = packed[:, :27].reshape(2, 27, 2, 64).transpose(1, 0, 2, 3)
    right = packed[:, 27].reshape(2, 2, 64)
    scale = packed[:, 28].reshape(2, 2, 64)
    coarse = COARSE_STEP * right / scale
    for _ in range(COARSE_ITERS - 1):
        full = jnp.pad(coarse_outer(coarse), ((0, 0), (0, 0), (1, 1)))
        total = jnp.zeros((2, 2, 64), F32)
        for k in range(27):
            ix, iz, iy = k // 9, (k // 3) % 3, k % 3
            total = total + op[k] * full[ix:ix + 2, iz:iz + 2, iy:iy + 64]
        coarse = coarse + COARSE_STEP * (right - total) / scale
    return jnp.pad(coarse_outer(coarse).reshape(16, 64), ((0, 0), (0, 64)))


def body(trans_x, trans_y, trans_z, accumulation, source, well_cell, well_rate):
    last_x = lax.axis_index("tile") == lax.axis_size("tile") - 1
    last_z = lax.axis_index("gz") == lax.axis_size("gz") - 1
    tx = jnp.where((jnp.arange(16) == 15)[:, None, None] & last_x, 0.0, trans_x)
    tz = jnp.where((jnp.arange(16) == 15)[None, :, None] & last_z, 0.0, trans_z)
    ty = jnp.where((jnp.arange(512) == 511)[None, None, :], 0.0, trans_y)
    txe, tye, tze = extend(tx, ty, tz)
    basis, packed, rhs, xh, zh = run_main(txe, tye, tze, accumulation, source, well_cell, well_rate)
    c4 = coarse_solve(packed)
    pressure, residual = run_finish(txe, tye, tze, basis, xh, zh, c4, accumulation, rhs)
    return basis, pressure, residual


def solution(mesh):
    grid = P("tile", "gz", None)
    return jax.shard_map(
        body,
        mesh=mesh,
        in_specs=(grid,) * 5 + (P("tile", "gz"),) * 2,
        out_specs=(P(None, "tile", "gz", None), grid, grid),
        check_vma=False,
    )
```

time: 527 us -> 244 us (0.46)
  local copies, waits for them, and re-layouts: 160 us -> 7.36 us
  starting transfers between devices: 198 us -> 99.8 us
  other arithmetic: 86.7 us -> 7.96 us
  Pallas kernels: 0 us -> 72.5 us
  matrix products: 17.1 us -> 0 us
    ppermute x54 -> x28, starting transfers between devices: 198 us -> 99.8 us  [the longest x14 55 us: shift_down(): return lax.ppermute(value, axis, [(i + 1, i) for i in range(size - 1)])]
    reshape x4 -> x1, local copies, waits for them, and re-layouts: 91 us -> 0.11 us  [coarse_solve(): op = packed[:, :27].reshape(2, 27, 2, 64).transpose(1, 0, 2, 3)]
    pallas_call x0 -> x2, Pallas kernels: none -> 72.5 us  [the longest x1 60.5 us: run_main(): pl.pallas_call(main_kernel, name='sweeps', out_shape=(jax.ShapeDtypeStruc...]
    reduce_sum x7 -> x0, other arithmetic: 52.5 us -> none  [the longest x4 42.8 us: body(): basis = basis / jnp.sum(basis, axis=0)]
    slice x72 -> x23, local copies, waits for them, and re-layouts: 51.5 us -> 5.12 us  [the longest x1 1.15 us: extend(): highx[8:12]]
    add x27 -> x6, other arithmetic: 19.2 us -> 2 us  [the longest x1 1.46 us: extend(): return (txe, tye, tze + extra)]
    dot_general x6 -> x0, matrix products: 17.1 us -> none  [the longest x3 14.1 us: coarse_operator(): jnp.einsum('abcIiKkJj,aIix,bKkz,cJjy->xzyIKJ', shaped, one_hot_offsets(of...]
    another operation x12 -> x2, local copies, waits for them, and re-layouts: 6.99 us -> 0.16 us  [the longest x1 0.08 us: coarse_solve(): right = packed[:, 27].reshape(2, 2, 64)]
  transfers between devices with their start and end apart: 54 -> 28, of which waited for: 23 -> 16; matrix products, arithmetic and copies ran while one was open for 11% -> 2% of each run, Pallas kernels for 0% -> 0%
where the time goes in v1:
time: 244 us; the launch traced here: 240 us
  starting transfers between devices  99.8 us (41%)
  Pallas kernels  72.5 us (30%)
  waiting for transfers between devices  51.4 us (21%)
  other arithmetic  7.96 us (3%)
  local copies, waits for them, and re-layouts  7.36 us (3%)
    pallas_call x1, Pallas kernels, run_main(): pl.pallas_call(main_kernel, name='sweeps', out_shape=(jax.ShapeDtypeStruc...  60.5 us
    ppermute x14, starting transfers between devices, shift_down(): return lax.ppermute(value, axis, [(i + 1, i) for i in range(size - 1)])  55 us
    ppermute x14, starting transfers between devices, shift_up(): return lax.ppermute(value, axis, [(i, i + 1) for i in range(size - 1)])  44.8 us
    ppermute x14, waiting for transfers between devices, shift_down(): return lax.ppermute(value, axis, [(i + 1, i) for i in range(size - 1)])  36.2 us
    ppermute x14, waiting for transfers between devices, shift_up(): return lax.ppermute(value, axis, [(i, i + 1) for i in range(size - 1)])  15.2 us
    pallas_call x1, Pallas kernels, run_finish(): pl.pallas_call(finish_kernel, name='finish', out_shape=(jax.ShapeDtypeStr...  11.9 us
  transfers between devices with their start and end apart: 28, of which 16 were waited for; matrix products, arithmetic and copies ran while one was open for 2% of the time, Pallas kernels for 0%

profile of v1, /device:TPU:36, one launch (start us, length us, event | category | flops | bytes accessed | tf_op | source)
XLA Modules:
  0.0 240.1 jit_solution(17394031991482166965)
XLA Ops:
  0.7 1.2 broadcast_select_fusion
  2.2 0.1 fusion.184
  2.4 3.0 %collective-permute-start.1 = (f32[16,12,512]{2,1,0:T(8,128)S(1)}, f32[16,12,512]{2,1,0:T(8,128)S(1)}, u32[]{:S(2)}, u32[]{:S(2)}) collective-permute-start(f32[16,12,512]{2,1,0:T(8,128)S(1)} %pad_maximum_fusion.5), channel_id=1, source_target_pairs={{1,0},{2,1},{3,2},{4,3},{5,4},{6,5},{7,6},{9,8},{10,9},{11,10},{12... | collective-permute-start | bytes 1179656 | tf_op jit(solution)/shard_map/ppermute | solution.py:462
  5.6 2.8 %collective-permute-start = (f32[16,13,512]{2,1,0:T(8,128)S(1)}, f32[16,13,512]{2,1,0:T(8,128)S(1)}, u32[]{:S(2)}, u32[]{:S(2)}) collective-permute-start(f32[16,13,512]{2,1,0:T(8,128)S(1)} %pad_maximum_fusion.4), channel_id=1, source_target_pairs={{0,1},{1,2},{2,3},{3,4},{4,5},{5,6},{6,7},{8,9},{9,10},{10,11},{11... | collective-permute-start | bytes 1277960 | tf_op jit(solution)/shard_map/ppermute | solution.py:457
  8.4 10.7 %collective-permute-done.1 = f32[16,12,512]{2,1,0:T(8,128)S(1)} collective-permute-done((f32[16,12,512]{2,1,0:T(8,128)S(1)}, f32[16,12,512]{2,1,0:T(8,128)S(1)}, u32[]{:S(2)}, u32[]{:S(2)}) %collective-permute-start.1) | collective-permute-done | bytes 393248 | tf_op jit(solution)/shard_map/ppermute | solution.py:462
  19.1 9.6 %collective-permute-done = f32[16,13,512]{2,1,0:T(8,128)S(1)} collective-permute-done((f32[16,13,512]{2,1,0:T(8,128)S(1)}, f32[16,13,512]{2,1,0:T(8,128)S(1)}, u32[]{:S(2)}, u32[]{:S(2)}) %collective-permute-start) | collective-permute-done | bytes 426016 | tf_op jit(solution)/shard_map/ppermute | solution.py:457
  28.8 0.9 fusion.6
  29.7 3.8 %collective-permute-start.3 = (f32[12,24,512]{2,1,0:T(8,128)}, f32[12,24,512]{2,1,0:T(8,128)}, u32[]{:S(2)}, u32[]{:S(2)}) collective-permute-start(f32[12,24,512]{2,1,0:T(8,128)} %fusion.6), channel_id=1, source_target_pairs={{8,0},{16,8},{24,16},{32,24},{40,32},{48,40},{56,48},{64,56},{72,6... | collective-permute-start | bytes 1769480 | tf_op jit(solution)/shard_map/ppermute | solution.py:462
  33.6 1.9 collective-permute-start.2
  35.6 0.7 copy.13.wcell
  36.2 0.7 copy.14.wrate
  36.9 4.3 %collective-permute-done.3 = f32[12,24,512]{2,1,0:T(8,128)} collective-permute-done((f32[12,24,512]{2,1,0:T(8,128)}, f32[12,24,512]{2,1,0:T(8,128)}, u32[]{:S(2)}, u32[]{:S(2)}) %collective-permute-start.3) | collective-permute-done | bytes 589856 | tf_op jit(solution)/shard_map/ppermute | solution.py:462
  41.2 1.2 fusion.181
  42.4 5.6 %collective-permute-done.2 = f32[13,24,512]{2,1,0:T(8,128)} collective-permute-done((f32[13,24,512]{2,1,0:T(8,128)S(1)}, f32[13,24,512]{2,1,0:T(8,128)}, u32[]{:S(2)}, u32[]{:S(2)}) %collective-permute-start.2) | collective-permute-done | bytes 639008 | tf_op jit(solution)/shard_map/ppermute | solution.py:457
  48.0 1.0 slice.1061
  48.9 1.5 select_maximum_fusion.txe
  50.4 1.0 fusion.180
  51.4 1.4 select_maximum_fusion.8.tye
  52.9 1.5 fusion.1.tze
  54.3 60.5 %sweeps.1 = (f32[8,16,16,512]{3,2,1,0:T(8,128)}, f32[2,32,128]{2,1,0:T(8,128)}, f32[16,16,512]{2,1,0:T(8,128)}, f32[8,2,16,512]{3,2,1,0:T(8,128)}, f32[8,2,16,512]{3,2,1,0:T(8,128)}) custom-call(f32[25,32,512]{2,1,0:T(8,128)} %select_maximum_fusion.txe, f32[24,32,512]{2,1,0:T(8,128)} %select_maximum_fusion.8.tye, f32[24,32,512]{2,1,0:T(8,128)} %fusion.1.tze, ...), custom_call_target="tpu_custom_call" | custom-call | tf_op jit(solution)/shard_map/sweeps/pallas_call | solution.py:418
  114.9 0.8 slice_reduce_fusion.1
  115.8 4.9 %collective-permute-start.4 = (f32[1,2,64]{2,1,0:T(2,128)S(1)}, f32[1,2,64]{2,1,0:T(2,128)S(1)}, u32[]{:S(2)}, u32[]{:S(2)}) collective-permute-start(f32[1,2,64]{2,1,0:T(2,128)S(1)} %get-tuple-element.56), channel_id=1, source_target_pairs={{0,8},{8,16},{16,24},{24,32},{32,40},{40,48},{48,56},{56,64},{64,7... | collective-permute-start | bytes 1544 | tf_op jit(solution)/shard_map/ppermute | solution.py:457
  120.7 3.1 %collective-permute-start.5 = (f32[1,2,64]{2,1,0:T(2,128)S(1)}, f32[1,2,64]{2,1,0:T(2,128)S(1)}, u32[]{:S(2)}, u32[]{:S(2)}) collective-permute-start(f32[1,2,64]{2,1,0:T(2,128)S(1)} %get-tuple-element.57), channel_id=1, source_target_pairs={{8,0},{16,8},{24,16},{32,24},{40,32},{48,40},{56,48},{64,56},{72,6... | collective-permute-start | bytes 1544 | tf_op jit(solution)/shard_map/ppermute | solution.py:462
  123.8 1.6 collective-permute-done.5
  125.4 2.6 %collective-permute-start.6 = (f32[4,1,64]{2,1,0:T(1,128)S(1)}, f32[4,1,64]{2,1,0:T(1,128)S(1)}, u32[]{:S(2)}, u32[]{:S(2)}) collective-permute-start(f32[4,1,64]{2,1,0:T(1,128)S(1)} %get-tuple-element.44), channel_id=1, source_target_pairs={{0,1},{1,2},{2,3},{3,4},{4,5},{5,6},{6,7},{8,9},{9,10},{10,11},{11... | collective-permute-start | bytes 3080 | tf_op jit(solution)/shard_map/ppermute | solution.py:457
  128.0 4.2 %collective-permute-start.7 = (f32[4,1,64]{2,1,0:T(1,128)S(1)}, f32[4,1,64]{2,1,0:T(1,128)S(1)}, u32[]{:S(2)}, u32[]{:S(2)}) collective-permute-start(f32[4,1,64]{2,1,0:T(1,128)S(1)} %get-tuple-element.45), channel_id=1, source_target_pairs={{1,0},{2,1},{3,2},{4,3},{5,4},{6,5},{7,6},{9,8},{10,9},{11,10},{12... | collective-permute-start | bytes 3080 | tf_op jit(solution)/shard_map/ppermute | solution.py:462
  132.2 0.8 copy.15
  133.0 0.1 reshape.28
  133.1 1.1 collective-permute-done.7
  134.3 0.1 fusion.152
  134.4 4.6 %collective-permute-start.8 = (f32[1,2,64]{2,1,0:T(2,128)S(1)}, f32[1,2,64]{2,1,0:T(2,128)S(1)}, u32[]{:S(2)}, u32[]{:S(2)}) collective-permute-start(f32[1,2,64]{2,1,0:T(2,128)S(1)} %get-tuple-element.54), channel_id=1, source_target_pairs={{0,8},{8,16},{16,24},{24,32},{32,40},{40,48},{48,56},{56,64},{64,7... | collective-permute-start | bytes 1544 | tf_op jit(solution)/shard_map/ppermute | solution.py:457
  139.0 3.4 %collective-permute-start.9 = (f32[1,2,64]{2,1,0:T(2,128)S(1)}, f32[1,2,64]{2,1,0:T(2,128)S(1)}, u32[]{:S(2)}, u32[]{:S(2)}) collective-permute-start(f32[1,2,64]{2,1,0:T(2,128)S(1)} %get-tuple-element.55), channel_id=1, source_target_pairs={{8,0},{16,8},{24,16},{32,24},{40,32},{48,40},{56,48},{64,56},{72,6... | collective-permute-start | bytes 1544 | tf_op jit(solution)/shard_map/ppermute | solution.py:462
  142.4 1.3 collective-permute-done.9
  143.7 4.8 %collective-permute-start.10 = (f32[4,1,64]{2,1,0:T(1,128)S(1)}, f32[4,1,64]{2,1,0:T(1,128)S(1)}, u32[]{:S(2)}, u32[]{:S(2)}) collective-permute-start(f32[4,1,64]{2,1,0:T(1,128)S(1)} %get-tuple-element.42), channel_id=1, source_target_pairs={{0,1},{1,2},{2,3},{3,4},{4,5},{5,6},{6,7},{8,9},{9,10},{10,11},{11... | collective-permute-start | bytes 3080 | tf_op jit(solution)/shard_map/ppermute | solution.py:457
  148.5 1.9 collective-permute-start.11
  150.4 3.5 %collective-permute-done.11 = f32[4,1,64]{2,1,0:T(1,128)S(1)} collective-permute-done((f32[4,1,64]{2,1,0:T(1,128)S(1)}, f32[4,1,64]{2,1,0:T(1,128)S(1)}, u32[]{:S(2)}, u32[]{:S(2)}) %collective-permute-start.11) | collective-permute-done | bytes 1056 | tf_op jit(solution)/shard_map/ppermute | solution.py:462
  154.1 0.1 fusion.118
  154.2 2.8 %collective-permute-start.12 = (f32[1,2,64]{2,1,0:T(2,128)S(1)}, f32[1,2,64]{2,1,0:T(2,128)S(1)}, u32[]{:S(2)}, u32[]{:S(2)}) collective-permute-start(f32[1,2,64]{2,1,0:T(2,128)S(1)} %get-tuple-element.52), channel_id=1, source_target_pairs={{0,8},{8,16},{16,24},{24,32},{32,40},{40,48},{48,56},{56,64},{64,7... | collective-permute-start | bytes 1544 | tf_op jit(solution)/shard_map/ppermute | solution.py:457
  157.0 5.2 %collective-permute-start.13 = (f32[1,2,64]{2,1,0:T(2,128)S(1)}, f32[1,2,64]{2,1,0:T(2,128)S(1)}, u32[]{:S(2)}, u32[]{:S(2)}) collective-permute-start(f32[1,2,64]{2,1,0:T(2,128)S(1)} %get-tuple-element.53), channel_id=1, source_target_pairs={{8,0},{16,8},{24,16},{32,24},{40,32},{48,40},{56,48},{64,56},{72,6... | collective-permute-start | bytes 1544 | tf_op jit(solution)/shard_map/ppermute | solution.py:462
  162.2 1.3 collective-permute-done.13
  163.5 3.3 %collective-permute-start.14 = (f32[4,1,64]{2,1,0:T(1,128)S(1)}, f32[4,1,64]{2,1,0:T(1,128)S(1)}, u32[]{:S(2)}, u32[]{:S(2)}) collective-permute-start(f32[4,1,64]{2,1,0:T(1,128)S(1)} %get-tuple-element.40), channel_id=1, source_target_pairs={{0,1},{1,2},{2,3},{3,4},{4,5},{5,6},{6,7},{8,9},{9,10},{10,11},{11... | collective-permute-start | bytes 3080 | tf_op jit(solution)/shard_map/ppermute | solution.py:457
  166.7 3.5 %collective-permute-start.15 = (f32[4,1,64]{2,1,0:T(1,128)S(1)}, f32[4,1,64]{2,1,0:T(1,128)S(1)}, u32[]{:S(2)}, u32[]{:S(2)}) collective-permute-start(f32[4,1,64]{2,1,0:T(1,128)S(1)} %get-tuple-element.41), channel_id=1, source_target_pairs={{1,0},{2,1},{3,2},{4,3},{5,4},{6,5},{7,6},{9,8},{10,9},{11,10},{12... | collective-permute-start | bytes 3080 | tf_op jit(solution)/shard_map/ppermute | solution.py:462
  170.2 2.0 collective-permute-done.15
  172.4 2.8 %collective-permute-start.16 = (f32[1,2,64]{2,1,0:T(2,128)S(1)}, f32[1,2,64]{2,1,0:T(2,128)S(1)}, u32[]{:S(2)}, u32[]{:S(2)}) collective-permute-start(f32[1,2,64]{2,1,0:T(2,128)S(1)} %get-tuple-element.50), channel_id=1, source_target_pairs={{0,8},{8,16},{16,24},{24,32},{32,40},{40,48},{48,56},{56,64},{64,7... | collective-permute-start | bytes 1544 | tf_op jit(solution)/shard_map/ppermute | solution.py:457
  175.2 5.2 %collective-permute-start.17 = (f32[1,2,64]{2,1,0:T(2,128)S(1)}, f32[1,2,64]{2,1,0:T(2,128)S(1)}, u32[]{:S(2)}, u32[]{:S(2)}) collective-permute-start(f32[1,2,64]{2,1,0:T(2,128)S(1)} %get-tuple-element.51), channel_id=1, source_target_pairs={{8,0},{16,8},{24,16},{32,24},{40,32},{48,40},{56,48},{64,56},{72,6... | collective-permute-start | bytes 1544 | tf_op jit(solution)/shard_map/ppermute | solution.py:462
  180.4 1.3 collective-permute-done.17
  181.7 4.8 %collective-permute-start.18 = (f32[4,1,64]{2,1,0:T(1,128)S(1)}, f32[4,1,64]{2,1,0:T(1,128)S(1)}, u32[]{:S(2)}, u32[]{:S(2)}) collective-permute-start(f32[4,1,64]{2,1,0:T(1,128)S(1)} %get-tuple-element.38), channel_id=1, source_target_pairs={{0,1},{1,2},{2,3},{3,4},{4,5},{5,6},{6,7},{8,9},{9,10},{10,11},{11... | collective-permute-start | bytes 3080 | tf_op jit(solution)/shard_map/ppermute | solution.py:457
  186.5 1.9 collective-permute-start.19
  188.5 3.5 %collective-permute-done.19 = f32[4,1,64]{2,1,0:T(1,128)S(1)} collective-permute-done((f32[4,1,64]{2,1,0:T(1,128)S(1)}, f32[4,1,64]{2,1,0:T(1,128)S(1)}, u32[]{:S(2)}, u32[]{:S(2)}) %collective-permute-start.19) | collective-permute-done | bytes 1056 | tf_op jit(solution)/shard_map/ppermute | solution.py:462
  192.2 1.9 collective-permute-start.20
  194.1 6.0 %collective-permute-start.21 = (f32[1,2,64]{2,1,0:T(2,128)S(1)}, f32[1,2,64]{2,1,0:T(2,128)S(1)}, u32[]{:S(2)}, u32[]{:S(2)}) collective-permute-start(f32[1,2,64]{2,1,0:T(2,128)S(1)} %get-tuple-element.49), channel_id=1, source_target_pairs={{8,0},{16,8},{24,16},{32,24},{40,32},{48,40},{56,48},{64,56},{72,6... | collective-permute-start | bytes 1544 | tf_op jit(solution)/shard_map/ppermute | solution.py:462
  200.2 1.3 collective-permute-done.21
  201.5 2.8 %collective-permute-start.22 = (f32[4,1,64]{2,1,0:T(1,128)S(1)}, f32[4,1,64]{2,1,0:T(1,128)S(1)}, u32[]{:S(2)}, u32[]{:S(2)}) collective-permute-start(f32[4,1,64]{2,1,0:T(1,128)S(1)} %get-tuple-element.36), channel_id=1, source_target_pairs={{0,1},{1,2},{2,3},{3,4},{4,5},{5,6},{6,7},{8,9},{9,10},{10,11},{11... | collective-permute-start | bytes 3080 | tf_op jit(solution)/shard_map/ppermute | solution.py:457
  204.3 3.9 %collective-permute-start.23 = (f32[4,1,64]{2,1,0:T(1,128)S(1)}, f32[4,1,64]{2,1,0:T(1,128)S(1)}, u32[]{:S(2)}, u32[]{:S(2)}) collective-permute-start(f32[4,1,64]{2,1,0:T(1,128)S(1)} %get-tuple-element.37), channel_id=1, source_target_pairs={{1,0},{2,1},{3,2},{4,3},{5,4},{6,5},{7,6},{9,8},{10,9},{11,10},{12... | collective-permute-start | bytes 3080 | tf_op jit(solution)/shard_map/ppermute | solution.py:462
  208.2 1.5 collective-permute-done.23
  209.9 0.1 fusion.16
  210.0 1.9 collective-permute-start.24
  211.9 6.0 %collective-permute-start.25 = (f32[1,2,64]{2,1,0:T(2,128)S(1)}, f32[1,2,64]{2,1,0:T(2,128)S(1)}, u32[]{:S(2)}, u32[]{:S(2)}) collective-permute-start(f32[1,2,64]{2,1,0:T(2,128)S(1)} %get-tuple-element.47), channel_id=1, source_target_pairs={{8,0},{16,8},{24,16},{32,24},{40,32},{48,40},{56,48},{64,56},{72,6... | collective-permute-start | bytes 1544 | tf_op jit(solution)/shard_map/ppermute | solution.py:462
  218.0 1.3 collective-permute-done.25
  219.3 2.8 %collective-permute-start.26 = (f32[4,1,64]{2,1,0:T(1,128)S(1)}, f32[4,1,64]{2,1,0:T(1,128)S(1)}, u32[]{:S(2)}, u32[]{:S(2)}) collective-permute-start(f32[4,1,64]{2,1,0:T(1,128)S(1)} %get-tuple-element.34), channel_id=1, source_target_pairs={{0,1},{1,2},{2,3},{3,4},{4,5},{5,6},{6,7},{8,9},{9,10},{10,11},{11... | collective-permute-start | bytes 3080 | tf_op jit(solution)/shard_map/ppermute | solution.py:457
  222.1 3.9 %collective-permute-start.27 = (f32[4,1,64]{2,1,0:T(1,128)S(1)}, f32[4,1,64]{2,1,0:T(1,128)S(1)}, u32[]{:S(2)}, u32[]{:S(2)}) collective-permute-start(f32[4,1,64]{2,1,0:T(1,128)S(1)} %get-tuple-element.35), channel_id=1, source_target_pairs={{1,0},{2,1},{3,2},{4,3},{5,4},{6,5},{7,6},{9,8},{10,9},{11,10},{12... | collective-permute-start | bytes 3080 | tf_op jit(solution)/shard_map/ppermute | solution.py:462
  226.0 1.5 collective-permute-done.27
  227.6 0.6 pad.44.c4
  228.2 11.9 %finish.1 = (f32[16,16,512]{2,1,0:T(8,128)}, f32[16,16,512]{2,1,0:T(8,128)}) custom-call(f32[25,32,512]{2,1,0:T(8,128)} %select_maximum_fusion.txe, f32[24,32,512]{2,1,0:T(8,128)} %select_maximum_fusion.8.tye, f32[24,32,512]{2,1,0:T(8,128)} %fusion.1.tze, f32[8,16,16,512]{3,2,1,0:T(8,128)} %get-tuple-element.7.basis, ...), custom_call_target="tpu_custom_call" | custom-call | tf_op jit(solution)/shard_map/finish/pallas_call | solution.py:439
  (62 shorter events, 1.6 us)
Async XLA Ops:
  0.6 1.4 copy-start
  0.6 1.4 copy-start.1
  2.4 16.7 %collective-permute-start.1 = (f32[16,12,512]{2,1,0:T(8,128)S(1)}, f32[16,12,512]{2,1,0:T(8,128)S(1)}, u32[]{:S(2)}, u32[]{:S(2)}) collective-permute-start(f32[16,12,512]{2,1,0:T(8,128)S(1)} %pad_maximum_fusion.5), channel_id=1, source_target_pairs={{1,0},{2,1},{3,2},{4,3},{5,4},{6,5},{7,6},{9,8},{10,9},{11,10},{12... | collective-permute-start | bytes 1179656 | tf_op jit(solution)/shard_map/ppermute | solution.py:462
  5.6 23.2 %collective-permute-start = (f32[16,13,512]{2,1,0:T(8,128)S(1)}, f32[16,13,512]{2,1,0:T(8,128)S(1)}, u32[]{:S(2)}, u32[]{:S(2)}) collective-permute-start(f32[16,13,512]{2,1,0:T(8,128)S(1)} %pad_maximum_fusion.4), channel_id=1, source_target_pairs={{0,1},{1,2},{2,3},{3,4},{4,5},{5,6},{6,7},{8,9},{9,10},{10,11},{11... | collective-permute-start | bytes 1277960 | tf_op jit(solution)/shard_map/ppermute | solution.py:457
  29.7 5.8 %copy-start.2 = (s32[16,1]{0,1:T(1,128)S(1)}, s32[16,1]{0,1:T(1,128)}, u32[]{:S(2)}) copy-start(s32[16,1]{0,1:T(1,128)} %param.12) | copy-start | bytes 196
  29.7 6.5 %copy-start.3 = (f32[16,1]{0,1:T(1,128)S(1)}, f32[16,1]{0,1:T(1,128)}, u32[]{:S(2)}) copy-start(f32[16,1]{0,1:T(1,128)} %param.13) | copy-start | bytes 196
  29.7 11.5 %collective-permute-start.3 = (f32[12,24,512]{2,1,0:T(8,128)}, f32[12,24,512]{2,1,0:T(8,128)}, u32[]{:S(2)}, u32[]{:S(2)}) collective-permute-start(f32[12,24,512]{2,1,0:T(8,128)} %fusion.6), channel_id=1, source_target_pairs={{8,0},{16,8},{24,16},{32,24},{40,32},{48,40},{56,48},{64,56},{72,6... | collective-permute-start | bytes 1769480 | tf_op jit(solution)/shard_map/ppermute | solution.py:462
  33.6 14.3 %collective-permute-start.2 = (f32[13,24,512]{2,1,0:T(8,128)S(1)}, f32[13,24,512]{2,1,0:T(8,128)}, u32[]{:S(2)}, u32[]{:S(2)}) collective-permute-start(f32[13,24,512]{2,1,0:T(8,128)S(1)} %fusion.3), channel_id=1, source_target_pairs={{0,8},{8,16},{16,24},{24,32},{32,40},{40,48},{48,56},{56,64},{64,7... | collective-permute-start | bytes 1916936 | tf_op jit(solution)/shard_map/ppermute | solution.py:457
  115.8 8.0 %collective-permute-start.4 = (f32[1,2,64]{2,1,0:T(2,128)S(1)}, f32[1,2,64]{2,1,0:T(2,128)S(1)}, u32[]{:S(2)}, u32[]{:S(2)}) collective-permute-start(f32[1,2,64]{2,1,0:T(2,128)S(1)} %get-tuple-element.56), channel_id=1, source_target_pairs={{0,8},{8,16},{16,24},{24,32},{32,40},{40,48},{48,56},{56,64},{64,7... | collective-permute-start | bytes 1544 | tf_op jit(solution)/shard_map/ppermute | solution.py:457
  120.7 4.7 %collective-permute-start.5 = (f32[1,2,64]{2,1,0:T(2,128)S(1)}, f32[1,2,64]{2,1,0:T(2,128)S(1)}, u32[]{:S(2)}, u32[]{:S(2)}) collective-permute-start(f32[1,2,64]{2,1,0:T(2,128)S(1)} %get-tuple-element.57), channel_id=1, source_target_pairs={{8,0},{16,8},{24,16},{32,24},{40,32},{48,40},{56,48},{64,56},{72,6... | collective-permute-start | bytes 1544 | tf_op jit(solution)/shard_map/ppermute | solution.py:462
  125.4 7.7 %collective-permute-start.6 = (f32[4,1,64]{2,1,0:T(1,128)S(1)}, f32[4,1,64]{2,1,0:T(1,128)S(1)}, u32[]{:S(2)}, u32[]{:S(2)}) collective-permute-start(f32[4,1,64]{2,1,0:T(1,128)S(1)} %get-tuple-element.44), channel_id=1, source_target_pairs={{0,1},{1,2},{2,3},{3,4},{4,5},{5,6},{6,7},{8,9},{9,10},{10,11},{11... | collective-permute-start | bytes 3080 | tf_op jit(solution)/shard_map/ppermute | solution.py:457
  128.0 6.2 %collective-permute-start.7 = (f32[4,1,64]{2,1,0:T(1,128)S(1)}, f32[4,1,64]{2,1,0:T(1,128)S(1)}, u32[]{:S(2)}, u32[]{:S(2)}) collective-permute-start(f32[4,1,64]{2,1,0:T(1,128)S(1)} %get-tuple-element.45), channel_id=1, source_target_pairs={{1,0},{2,1},{3,2},{4,3},{5,4},{6,5},{7,6},{9,8},{10,9},{11,10},{12... | collective-permute-start | bytes 3080 | tf_op jit(solution)/shard_map/ppermute | solution.py:462
  134.4 8.0 %collective-permute-start.8 = (f32[1,2,64]{2,1,0:T(2,128)S(1)}, f32[1,2,64]{2,1,0:T(2,128)S(1)}, u32[]{:S(2)}, u32[]{:S(2)}) collective-permute-start(f32[1,2,64]{2,1,0:T(2,128)S(1)} %get-tuple-element.54), channel_id=1, source_target_pairs={{0,8},{8,16},{16,24},{24,32},{32,40},{40,48},{48,56},{56,64},{64,7... | collective-permute-start | bytes 1544 | tf_op jit(solution)/shard_map/ppermute | solution.py:457
  139.0 4.7 %collective-permute-start.9 = (f32[1,2,64]{2,1,0:T(2,128)S(1)}, f32[1,2,64]{2,1,0:T(2,128)S(1)}, u32[]{:S(2)}, u32[]{:S(2)}) collective-permute-start(f32[1,2,64]{2,1,0:T(2,128)S(1)} %get-tuple-element.55), channel_id=1, source_target_pairs={{8,0},{16,8},{24,16},{32,24},{40,32},{48,40},{56,48},{64,56},{72,6... | collective-permute-start | bytes 1544 | tf_op jit(solution)/shard_map/ppermute | solution.py:462
  143.7 6.8 %collective-permute-start.10 = (f32[4,1,64]{2,1,0:T(1,128)S(1)}, f32[4,1,64]{2,1,0:T(1,128)S(1)}, u32[]{:S(2)}, u32[]{:S(2)}) collective-permute-start(f32[4,1,64]{2,1,0:T(1,128)S(1)} %get-tuple-element.42), channel_id=1, source_target_pairs={{0,1},{1,2},{2,3},{3,4},{4,5},{5,6},{6,7},{8,9},{9,10},{10,11},{11... | collective-permute-start | bytes 3080 | tf_op jit(solution)/shard_map/ppermute | solution.py:457
  148.5 5.5 %collective-permute-start.11 = (f32[4,1,64]{2,1,0:T(1,128)S(1)}, f32[4,1,64]{2,1,0:T(1,128)S(1)}, u32[]{:S(2)}, u32[]{:S(2)}) collective-permute-start(f32[4,1,64]{2,1,0:T(1,128)S(1)} %get-tuple-element.43), channel_id=1, source_target_pairs={{1,0},{2,1},{3,2},{4,3},{5,4},{6,5},{7,6},{9,8},{10,9},{11,10},{12... | collective-permute-start | bytes 3080 | tf_op jit(solution)/shard_map/ppermute | solution.py:462
  154.2 8.0 %collective-permute-start.12 = (f32[1,2,64]{2,1,0:T(2,128)S(1)}, f32[1,2,64]{2,1,0:T(2,128)S(1)}, u32[]{:S(2)}, u32[]{:S(2)}) collective-permute-start(f32[1,2,64]{2,1,0:T(2,128)S(1)} %get-tuple-element.52), channel_id=1, source_target_pairs={{0,8},{8,16},{16,24},{24,32},{32,40},{40,48},{48,56},{56,64},{64,7... | collective-permute-start | bytes 1544 | tf_op jit(solution)/shard_map/ppermute | solution.py:457
  157.0 6.4 %collective-permute-start.13 = (f32[1,2,64]{2,1,0:T(2,128)S(1)}, f32[1,2,64]{2,1,0:T(2,128)S(1)}, u32[]{:S(2)}, u32[]{:S(2)}) collective-permute-start(f32[1,2,64]{2,1,0:T(2,128)S(1)} %get-tuple-element.53), channel_id=1, source_target_pairs={{8,0},{16,8},{24,16},{32,24},{40,32},{48,40},{56,48},{64,56},{72,6... | collective-permute-start | bytes 1544 | tf_op jit(solution)/shard_map/ppermute | solution.py:462
  163.5 6.8 %collective-permute-start.14 = (f32[4,1,64]{2,1,0:T(1,128)S(1)}, f32[4,1,64]{2,1,0:T(1,128)S(1)}, u32[]{:S(2)}, u32[]{:S(2)}) collective-permute-start(f32[4,1,64]{2,1,0:T(1,128)S(1)} %get-tuple-element.40), channel_id=1, source_target_pairs={{0,1},{1,2},{2,3},{3,4},{4,5},{5,6},{6,7},{8,9},{9,10},{10,11},{11... | collective-permute-start | bytes 3080 | tf_op jit(solution)/shard_map/ppermute | solution.py:457
  166.7 5.5 %collective-permute-start.15 = (f32[4,1,64]{2,1,0:T(1,128)S(1)}, f32[4,1,64]{2,1,0:T(1,128)S(1)}, u32[]{:S(2)}, u32[]{:S(2)}) collective-permute-start(f32[4,1,64]{2,1,0:T(1,128)S(1)} %get-tuple-element.41), channel_id=1, source_target_pairs={{1,0},{2,1},{3,2},{4,3},{5,4},{6,5},{7,6},{9,8},{10,9},{11,10},{12... | collective-permute-start | bytes 3080 | tf_op jit(solution)/shard_map/ppermute | solution.py:462
  172.4 8.0 %collective-permute-start.16 = (f32[1,2,64]{2,1,0:T(2,128)S(1)}, f32[1,2,64]{2,1,0:T(2,128)S(1)}, u32[]{:S(2)}, u32[]{:S(2)}) collective-permute-start(f32[1,2,64]{2,1,0:T(2,128)S(1)} %get-tuple-element.50), channel_id=1, source_target_pairs={{0,8},{8,16},{16,24},{24,32},{32,40},{40,48},{48,56},{56,64},{64,7... | collective-permute-start | bytes 1544 | tf_op jit(solution)/shard_map/ppermute | solution.py:457
  175.2 6.5 %collective-permute-start.17 = (f32[1,2,64]{2,1,0:T(2,128)S(1)}, f32[1,2,64]{2,1,0:T(2,128)S(1)}, u32[]{:S(2)}, u32[]{:S(2)}) collective-permute-start(f32[1,2,64]{2,1,0:T(2,128)S(1)} %get-tuple-element.51), channel_id=1, source_target_pairs={{8,0},{16,8},{24,16},{32,24},{40,32},{48,40},{56,48},{64,56},{72,6... | collective-permute-start | bytes 1544 | tf_op jit(solution)/shard_map/ppermute | solution.py:462
  181.7 6.8 %collective-permute-start.18 = (f32[4,1,64]{2,1,0:T(1,128)S(1)}, f32[4,1,64]{2,1,0:T(1,128)S(1)}, u32[]{:S(2)}, u32[]{:S(2)}) collective-permute-start(f32[4,1,64]{2,1,0:T(1,128)S(1)} %get-tuple-element.38), channel_id=1, source_target_pairs={{0,1},{1,2},{2,3},{3,4},{4,5},{5,6},{6,7},{8,9},{9,10},{10,11},{11... | collective-permute-start | bytes 3080 | tf_op jit(solution)/shard_map/ppermute | solution.py:457
  186.5 5.5 %collective-permute-start.19 = (f32[4,1,64]{2,1,0:T(1,128)S(1)}, f32[4,1,64]{2,1,0:T(1,128)S(1)}, u32[]{:S(2)}, u32[]{:S(2)}) collective-permute-start(f32[4,1,64]{2,1,0:T(1,128)S(1)} %get-tuple-element.39), channel_id=1, source_target_pairs={{1,0},{2,1},{3,2},{4,3},{5,4},{6,5},{7,6},{9,8},{10,9},{11,10},{12... | collective-permute-start | bytes 3080 | tf_op jit(solution)/shard_map/ppermute | solution.py:462
  192.2 8.0 %collective-permute-start.20 = (f32[1,2,64]{2,1,0:T(2,128)S(1)}, f32[1,2,64]{2,1,0:T(2,128)S(1)}, u32[]{:S(2)}, u32[]{:S(2)}) collective-permute-start(f32[1,2,64]{2,1,0:T(2,128)S(1)} %get-tuple-element.48), channel_id=1, source_target_pairs={{0,8},{8,16},{16,24},{24,32},{32,40},{40,48},{48,56},{56,64},{64,7... | collective-permute-start | bytes 1544 | tf_op jit(solution)/shard_map/ppermute | solution.py:457
  194.1 7.3 %collective-permute-start.21 = (f32[1,2,64]{2,1,0:T(2,128)S(1)}, f32[1,2,64]{2,1,0:T(2,128)S(1)}, u32[]{:S(2)}, u32[]{:S(2)}) collective-permute-start(f32[1,2,64]{2,1,0:T(2,128)S(1)} %get-tuple-element.49), channel_id=1, source_target_pairs={{8,0},{16,8},{24,16},{32,24},{40,32},{48,40},{56,48},{64,56},{72,6... | collective-permute-start | bytes 1544 | tf_op jit(solution)/shard_map/ppermute | solution.py:462
  201.5 6.8 %collective-permute-start.22 = (f32[4,1,64]{2,1,0:T(1,128)S(1)}, f32[4,1,64]{2,1,0:T(1,128)S(1)}, u32[]{:S(2)}, u32[]{:S(2)}) collective-permute-start(f32[4,1,64]{2,1,0:T(1,128)S(1)} %get-tuple-element.36), channel_id=1, source_target_pairs={{0,1},{1,2},{2,3},{3,4},{4,5},{5,6},{6,7},{8,9},{9,10},{10,11},{11... | collective-permute-start | bytes 3080 | tf_op jit(solution)/shard_map/ppermute | solution.py:457
  204.3 5.5 %collective-permute-start.23 = (f32[4,1,64]{2,1,0:T(1,128)S(1)}, f32[4,1,64]{2,1,0:T(1,128)S(1)}, u32[]{:S(2)}, u32[]{:S(2)}) collective-permute-start(f32[4,1,64]{2,1,0:T(1,128)S(1)} %get-tuple-element.37), channel_id=1, source_target_pairs={{1,0},{2,1},{3,2},{4,3},{5,4},{6,5},{7,6},{9,8},{10,9},{11,10},{12... | collective-permute-start | bytes 3080 | tf_op jit(solution)/shard_map/ppermute | solution.py:462
  210.0 8.0 %collective-permute-start.24 = (f32[1,2,64]{2,1,0:T(2,128)S(1)}, f32[1,2,64]{2,1,0:T(2,128)S(1)}, u32[]{:S(2)}, u32[]{:S(2)}) collective-permute-start(f32[1,2,64]{2,1,0:T(2,128)S(1)} %get-tuple-element.46), channel_id=1, source_target_pairs={{0,8},{8,16},{16,24},{24,32},{32,40},{40,48},{48,56},{56,64},{64,7... | collective-permute-start | bytes 1544 | tf_op jit(solution)/shard_map/ppermute | solution.py:457
  211.9 7.3 %collective-permute-start.25 = (f32[1,2,64]{2,1,0:T(2,128)S(1)}, f32[1,2,64]{2,1,0:T(2,128)S(1)}, u32[]{:S(2)}, u32[]{:S(2)}) collective-permute-start(f32[1,2,64]{2,1,0:T(2,128)S(1)} %get-tuple-element.47), channel_id=1, source_target_pairs={{8,0},{16,8},{24,16},{32,24},{40,32},{48,40},{56,48},{64,56},{72,6... | collective-permute-start | bytes 1544 | tf_op jit(solution)/shard_map/ppermute | solution.py:462
  219.3 6.8 %collective-permute-start.26 = (f32[4,1,64]{2,1,0:T(1,128)S(1)}, f32[4,1,64]{2,1,0:T(1,128)S(1)}, u32[]{:S(2)}, u32[]{:S(2)}) collective-permute-start(f32[4,1,64]{2,1,0:T(1,128)S(1)} %get-tuple-element.34), channel_id=1, source_target_pairs={{0,1},{1,2},{2,3},{3,4},{4,5},{5,6},{6,7},{8,9},{9,10},{10,11},{11... | collective-permute-start | bytes 3080 | tf_op jit(solution)/shard_map/ppermute | solution.py:457
  222.1 5.5 %collective-permute-start.27 = (f32[4,1,64]{2,1,0:T(1,128)S(1)}, f32[4,1,64]{2,1,0:T(1,128)S(1)}, u32[]{:S(2)}, u32[]{:S(2)}) collective-permute-start(f32[4,1,64]{2,1,0:T(1,128)S(1)} %get-tuple-element.35), channel_id=1, source_target_pairs={{1,0},{2,1},{3,2},{4,3},{5,4},{6,5},{7,6},{9,8},{10,9},{11,10},{12... | collective-permute-start | bytes 3080 | tf_op jit(solution)/shard_map/ppermute | solution.py:462

commit v2 on v1

--- a/solution.py
+++ b/solution.py
@@ -5,13 +5,13 @@
 from jax.experimental.pallas import tpu as pltpu
 from jax.sharding import PartitionSpec as P
 
-COARSE_ITERS = 6
 COARSE_STEP = 0.5
 NT = 4
 NXE = 24
 NR = 32
 F32 = jnp.float32
 INTERPRET = False
+COMM_INTERPRET = False
 
 
 def iota(shape, dim):
@@ -311,7 +311,7 @@
         for c in range(2):
             for d in range(2):
                 def row(nz):
-                    return spread[d][nx * 4 + nz:nx * 4 + nz + 1, :]
+                    return spread[d][nz * 8 + nx + 1:nz * 8 + nx + 2, :]
                 if c == 0:
                     tiles = (row(1), row(1)), (row(1), row(3))
                 else:
@@ -368,7 +368,7 @@
                     a, c, d = s // 4, (s // 2) % 2, s % 2
                     nz = (1, 0)[c] if s_z == 0 else (3, 2)[c]
                     def row(nx):
-                        return jnp.broadcast_to(spread[d][nx * 4 + nz:nx * 4 + nz + 1, cols], (8, 128))
+                        return jnp.broadcast_to(spread[d][nz * 8 + nx + 1:nz * 8 + nx + 2, cols], (8, 128))
                     if a == 0:
                         value = row(1) if half == 0 else jnp.where(upper, row(3), row(1))
                     else:
@@ -452,6 +452,157 @@
     )(txe, tye, tze, basis, xh, zh, c4, acc, rhs)
 
 
+NEAR = [(dt, dg) for dt in (-1, 0, 1) for dg in (-1, 0, 1) if (dt, dg) != (0, 0)]
+
+
+def slot_of(dt, dg):
+    return (dt + 1) * 3 + dg + 1
+
+
+def neighbours():
+    tile, gz = lax.axis_index("tile"), lax.axis_index("gz")
+    tiles, layers = lax.axis_size("tile"), lax.axis_size("gz")
+    found = []
+    for dt, dg in NEAR:
+        here = (tile + dt >= 0) & (tile + dt < tiles) & (gz + dg >= 0) & (gz + dg < layers)
+        found.append((dt, dg, here, (tile + dt, gz + dg)))
+    return found
+
+
+def greet(near):
+    barrier = pltpu.get_barrier_semaphore()
+    count = 0
+    for dt, dg, here, device in near:
+        @pl.when(here)
+        def _():
+            pl.semaphore_signal(barrier, inc=1, device_id=device, device_id_type=pl.DeviceIdType.MESH)
+        count = count + here.astype(jnp.int32)
+    pl.semaphore_wait(barrier, count)
+
+
+def coarse_kernel(packed, c_out, ops, got, mine, op_send, op_recv, c_send, c_recv):
+    near = neighbours()
+    ops[...] = jnp.zeros(ops.shape, F32)
+    got[...] = jnp.zeros(got.shape, F32)
+    greet(near)
+
+    def op_copies(dt, dg, device):
+        made = []
+        for n, xb in enumerate({1: (1,), -1: (0,), 0: (0, 1)}[dt]):
+            made.append(pltpu.make_async_remote_copy(
+                src_ref=packed.at[xb], dst_ref=ops.at[2 * (1 - dt) + xb, 1 - dg],
+                send_sem=op_send.at[slot_of(dt, dg), n], recv_sem=op_recv.at[slot_of(-dt, -dg), n],
+                device_id=device, device_id_type=pl.DeviceIdType.MESH))
+        return made
+
+    def c_copy(r, dt, dg, device):
+        return pltpu.make_async_remote_copy(
+            src_ref=mine.at[r], dst_ref=got.at[r, slot_of(-dt, -dg)],
+            send_sem=c_send.at[r, slot_of(dt, dg)], recv_sem=c_recv.at[r, slot_of(-dt, -dg)],
+            device_id=device, device_id_type=pl.DeviceIdType.MESH)
+
+    def each(act):
+        for dt, dg, here, device in near:
+            @pl.when(here)
+            def _():
+                act(dt, dg, device)
+
+    def send(r):
+        each(lambda dt, dg, device: c_copy(r, dt, dg, device).start())
+
+    def arrive(r):
+        each(lambda dt, dg, device: c_copy(r, -dt, -dg, device).wait_recv())
+
+    for xb in range(2):
+        mine[0, xb:xb + 1, :] = COARSE_STEP * packed[xb, 27:28, :] / packed[xb, 28:29, :]
+        ops[2 + xb, 1] = packed[xb]
+    send(0)
+    each(lambda dt, dg, device: [c.start() for c in op_copies(dt, dg, device)])
+
+    lane = iota((8, 128), 1)
+    row = iota((8, 128), 0)
+    table = ops.reshape(8 * 3 * 32, 128)
+
+    def entry(g, k):
+        return table[pl.ds(g * 32 + k, 8, stride=96), :]
+
+    def gather(r):
+        fields = []
+        for g in range(3):
+            parts = []
+            for dt in (-1, 0, 1):
+                parts.append(mine[r, 0:2, :] if (dt, g) == (0, 1) else got[r, slot_of(dt, g - 1), 0:2, :])
+            fields.append(jnp.concatenate(parts + [jnp.zeros((2, 128), F32)], 0))
+        return fields
+
+    def lanes_from(fields, g, by):
+        if by == 0:
+            return fields[g]
+        if by > 0:
+            after = fields[min(g + 1, 2)]
+            return jnp.where(lane < 128 - by, roll(fields[g], 128 - by), roll(after, 128 - by))
+        before = fields[max(g - 1, 0)]
+        return jnp.where(lane >= -by, roll(fields[g], -by), roll(before, -by))
+
+    def iterate(fields):
+        totals = [None] * 3
+        for dx in (-1, 0, 1):
+            moved = fields if dx == 0 else [pltpu.roll(f, 1 if dx == -1 else 7, 0) for f in fields]
+            for dz in (-1, 0, 1):
+                for dy in (-1, 0, 1):
+                    k = (dx + 1) * 9 + (dz + 1) * 3 + dy + 1
+                    for g in range(3):
+                        term = entry(g, k) * lanes_from(moved, g, 64 * dz + dy)
+                        totals[g] = term if totals[g] is None else totals[g] + term
+        result = []
+        for g in range(3):
+            scale = entry(g, 28)
+            safe = jnp.where(scale > 0.0, scale, 1.0)
+            value = fields[g] + COARSE_STEP * (entry(g, 27) - totals[g]) / safe
+            result.append(jnp.where(scale > 0.0, value, 0.0))
+        return result
+
+    arrive(0)
+    each(lambda dt, dg, device: [c.wait_recv() for c in op_copies(-dt, -dg, device)])
+    for r in range(3):
+        if r:
+            arrive(r)
+        fields = iterate(gather(r))
+        if r < 2:
+            fields = iterate(fields)
+            mine[r + 1, 0:2, :] = fields[1][2:4]
+            send(r + 1)
+    c_out[0:8, :] = roll(fields[0], 64)
+    c_out[8:16, :] = fields[1]
+    c_out[16:24, :] = roll(fields[1], 64)
+    c_out[24:32, :] = fields[2]
+
+    def drain(dt, dg, device):
+        for copy in op_copies(dt, dg, device):
+            copy.wait_send()
+        for r in range(3):
+            c_copy(r, dt, dg, device).wait_send()
+
+    each(drain)
+
+
+def run_coarse(packed):
+    return pl.pallas_call(
+        coarse_kernel,
+        name="coarse",
+        out_shape=jax.ShapeDtypeStruct((32, 128), F32),
+        in_specs=[VMEM_SPEC],
+        out_specs=VMEM_SPEC,
+        scratch_shapes=[
+            pltpu.VMEM((8, 3, 32, 128), F32), pltpu.VMEM((3, 9, 8, 128), F32), pltpu.VMEM((3, 8, 128), F32),
+            pltpu.SemaphoreType.DMA((9, 2)), pltpu.SemaphoreType.DMA((9, 2)),
+            pltpu.SemaphoreType.DMA((3, 9)), pltpu.SemaphoreType.DMA((3, 9)),
+        ],
+        compiler_params=pltpu.CompilerParams(collective_id=1, has_side_effects=True),
+        interpret=COMM_INTERPRET,
+    )(packed)
+
+
 def shift_up(value, axis):
     size = lax.axis_size(axis)
     return lax.ppermute(value, axis, [(i, i + 1) for i in range(size - 1)])
@@ -480,29 +631,6 @@
     return txe, tye, tze + extra
 
 
-def coarse_outer(value):
-    for axis, dim in (("tile", 0), ("gz", 1)):
-        head = lax.slice_in_dim(value, 0, 1, axis=dim)
-        tail = lax.slice_in_dim(value, value.shape[dim] - 1, value.shape[dim], axis=dim)
-        value = jnp.concatenate([shift_up(tail, axis), value, shift_down(head, axis)], axis=dim)
-    return value
-
-
-def coarse_solve(packed):
-    op = packed[:, :27].reshape(2, 27, 2, 64).transpose(1, 0, 2, 3)
-    right = packed[:, 27].reshape(2, 2, 64)
-    scale = packed[:, 28].reshape(2, 2, 64)
-    coarse = COARSE_STEP * right / scale
-    for _ in range(COARSE_ITERS - 1):
-        full = jnp.pad(coarse_outer(coarse), ((0, 0), (0, 0), (1, 1)))
-        total = jnp.zeros((2, 2, 64), F32)
-        for k in range(27):
-            ix, iz, iy = k // 9, (k // 3) % 3, k % 3
-            total = total + op[k] * full[ix:ix + 2, iz:iz + 2, iy:iy + 64]
-        coarse = coarse + COARSE_STEP * (right - total) / scale
-    return jnp.pad(coarse_outer(coarse).reshape(16, 64), ((0, 0), (0, 64)))
-
-
 def body(trans_x, trans_y, trans_z, accumulation, source, well_cell, well_rate):
     last_x = lax.axis_index("tile") == lax.axis_size("tile") - 1
     last_z = lax.axis_index("gz") == lax.axis_size("gz") - 1
@@ -511,7 +639,7 @@
     ty = jnp.where((jnp.arange(512) == 511)[None, None, :], 0.0, trans_y)
     txe, tye, tze = extend(tx, ty, tz)
     basis, packed, rhs, xh, zh = run_main(txe, tye, tze, accumulation, source, well_cell, well_rate)
-    c4 = coarse_solve(packed)
+    c4 = run_coarse(packed)
     pressure, residual = run_finish(txe, tye, tze, basis, xh, zh, c4, accumulation, rhs)
     return basis, pressure, residual
 

time: 244 us -> 148 us (0.61); the launches traced: 240 us -> 147 us
  starting transfers between devices: 99.8 us -> 11.5 us
  waiting for transfers between devices: 51.4 us -> 30.2 us
  Pallas kernels: 72.5 us -> 93 us
  local copies, waits for them, and re-layouts: 7.36 us -> 4.82 us
    ppermute x14 -> x2, starting transfers between devices: 55 us -> 6.81 us  [shift_down(): return lax.ppermute(value, axis, [(i + 1, i) for i in range(size - 1)])]
    ppermute x14 -> x2, starting transfers between devices: 44.8 us -> 4.73 us  [shift_up(): return lax.ppermute(value, axis, [(i, i + 1) for i in range(size - 1)])]
    ppermute x14 -> x2, waiting for transfers between devices: 36.2 us -> 15 us  [shift_down(): return lax.ppermute(value, axis, [(i + 1, i) for i in range(size - 1)])]
    pallas_call x0 -> x1, Pallas kernels: none -> 20.4 us  [run_coarse(): pl.pallas_call(coarse_kernel, name='coarse', out_shape=jax.ShapeDtypeStru...]
    ppermute x14 -> x2, waiting for transfers between devices: 15.2 us -> 15.1 us  [shift_up(): return lax.ppermute(value, axis, [(i, i + 1) for i in range(size - 1)])]
  transfers between devices with their start and end apart: 28 -> 4, of which waited for: 16 -> 4; matrix products, arithmetic and copies ran while one was open for 2% -> 2% of each run, Pallas kernels for 0% -> 0%
where the time goes in v2:
time: 148 us; the launch traced here: 147 us
  Pallas kernels  93 us (63%)
  waiting for transfers between devices  30.2 us (20%)
  starting transfers between devices  11.5 us (8%)
  other arithmetic  6.93 us (5%)
  local copies, waits for them, and re-layouts  4.82 us (3%)
    pallas_call x1, Pallas kernels, run_main(): pl.pallas_call(main_kernel, name='sweeps', out_shape=(jax.ShapeDtypeStruc...  60.6 us
    pallas_call x1, Pallas kernels, run_coarse(): pl.pallas_call(coarse_kernel, name='coarse', out_shape=jax.ShapeDtypeStru...  20.4 us
    ppermute x2, waiting for transfers between devices, shift_up(): return lax.ppermute(value, axis, [(i, i + 1) for i in range(size - 1)])  15.1 us
    ppermute x2, waiting for transfers between devices, shift_down(): return lax.ppermute(value, axis, [(i + 1, i) for i in range(size - 1)])  15 us
    pallas_call x1, Pallas kernels, run_finish(): pl.pallas_call(finish_kernel, name='finish', out_shape=(jax.ShapeDtypeStr...  12 us
    ppermute x2, starting transfers between devices, shift_down(): return lax.ppermute(value, axis, [(i + 1, i) for i in range(size - 1)])  6.81 us
    ppermute x2, starting transfers between devices, shift_up(): return lax.ppermute(value, axis, [(i, i + 1) for i in range(size - 1)])  4.73 us
  transfers between devices with their start and end apart: 4, of which 4 were waited for; matrix products, arithmetic and copies ran while one was open for 2% of the time, Pallas kernels for 0%

profile of v2, /device:TPU:36, one launch (start us, length us, event | category | flops | bytes accessed | tf_op | source)
XLA Modules:
  0.0 147.3 jit_solution(6510646818784127309)
XLA Ops:
  0.6 0.0 copy-start
  0.6 0.0 copy-start.1
  0.7 1.2 broadcast_select_fusion
  2.0 0.0 copy-done
  2.0 0.0 copy-done.1
  2.1 0.1 broadcast_select_fusion.2
  2.2 0.1 fusion.13
  2.3 0.1 pad_maximum_fusion.5
  2.4 3.0 %collective-permute-start.1 = (f32[16,12,512]{2,1,0:T(8,128)S(1)}, f32[16,12,512]{2,1,0:T(8,128)S(1)}, u32[]{:S(2)}, u32[]{:S(2)}) collective-permute-start(f32[16,12,512]{2,1,0:T(8,128)S(1)} %pad_maximum_fusion.5), channel_id=1, source_target_pairs={{1,0},{2,1},{3,2},{4,3},{5,4},{6,5},{7,6},{9,8},{10,9},{11,10},{12... | collective-permute-start | bytes 1179656 | tf_op jit(solution)/shard_map/ppermute | solution.py:613
  5.5 0.1 pad_maximum_fusion.4
  5.6 2.8 %collective-permute-start = (f32[16,13,512]{2,1,0:T(8,128)S(1)}, f32[16,13,512]{2,1,0:T(8,128)S(1)}, u32[]{:S(2)}, u32[]{:S(2)}) collective-permute-start(f32[16,13,512]{2,1,0:T(8,128)S(1)} %pad_maximum_fusion.4), channel_id=1, source_target_pairs={{0,1},{1,2},{2,3},{3,4},{4,5},{5,6},{6,7},{8,9},{9,10},{10,11},{11... | collective-permute-start | bytes 1277960 | tf_op jit(solution)/shard_map/ppermute | solution.py:608
  8.4 10.7 %collective-permute-done.1 = f32[16,12,512]{2,1,0:T(8,128)S(1)} collective-permute-done((f32[16,12,512]{2,1,0:T(8,128)S(1)}, f32[16,12,512]{2,1,0:T(8,128)S(1)}, u32[]{:S(2)}, u32[]{:S(2)}) %collective-permute-start.1) | collective-permute-done | bytes 393248 | tf_op jit(solution)/shard_map/ppermute | solution.py:613
  19.1 0.1 fusion.12
  19.1 9.6 %collective-permute-done = f32[16,13,512]{2,1,0:T(8,128)S(1)} collective-permute-done((f32[16,13,512]{2,1,0:T(8,128)S(1)}, f32[16,13,512]{2,1,0:T(8,128)S(1)}, u32[]{:S(2)}, u32[]{:S(2)}) %collective-permute-start) | collective-permute-done | bytes 426016 | tf_op jit(solution)/shard_map/ppermute | solution.py:608
  28.7 0.1 fusion.11
  28.8 0.9 fusion.6
  29.7 0.0 copy-start.2
  29.7 0.0 copy-start.3
  29.7 3.8 %collective-permute-start.3 = (f32[12,24,512]{2,1,0:T(8,128)}, f32[12,24,512]{2,1,0:T(8,128)}, u32[]{:S(2)}, u32[]{:S(2)}) collective-permute-start(f32[12,24,512]{2,1,0:T(8,128)} %fusion.6), channel_id=1, source_target_pairs={{8,0},{16,8},{24,16},{32,24},{40,32},{48,40},{56,48},{64,56},{72,6... | collective-permute-start | bytes 1769480 | tf_op jit(solution)/shard_map/ppermute | solution.py:613
  33.5 0.1 fusion.3
  33.6 1.9 %collective-permute-start.2 = (f32[13,24,512]{2,1,0:T(8,128)S(1)}, f32[13,24,512]{2,1,0:T(8,128)}, u32[]{:S(2)}, u32[]{:S(2)}) collective-permute-start(f32[13,24,512]{2,1,0:T(8,128)S(1)} %fusion.3), channel_id=1, source_target_pairs={{0,8},{8,16},{16,24},{24,32},{32,40},{40,48},{48,56},{56,64},{64,7... | collective-permute-start | bytes 1916936 | tf_op jit(solution)/shard_map/ppermute | solution.py:608
  35.6 0.0 copy-done.2
  35.6 0.7 copy.10.wcell
  36.2 0.0 copy-done.3
  36.2 0.7 copy.11.wrate
  36.9 4.3 %collective-permute-done.3 = f32[12,24,512]{2,1,0:T(8,128)} collective-permute-done((f32[12,24,512]{2,1,0:T(8,128)}, f32[12,24,512]{2,1,0:T(8,128)}, u32[]{:S(2)}, u32[]{:S(2)}) %collective-permute-start.3) | collective-permute-done | bytes 589856 | tf_op jit(solution)/shard_map/ppermute | solution.py:613
  41.2 1.2 fusion.10
  42.4 5.6 %collective-permute-done.2 = f32[13,24,512]{2,1,0:T(8,128)} collective-permute-done((f32[13,24,512]{2,1,0:T(8,128)S(1)}, f32[13,24,512]{2,1,0:T(8,128)}, u32[]{:S(2)}, u32[]{:S(2)}) %collective-permute-start.2) | collective-permute-done | bytes 639008 | tf_op jit(solution)/shard_map/ppermute | solution.py:608
  48.0 1.0 slice.112
  48.9 1.5 select_maximum_fusion.txe
  50.4 1.0 fusion.9
  51.4 1.4 select_maximum_fusion.8.tye
  52.8 1.5 fusion.1.tze
  54.3 60.6 %sweeps.1 = (f32[8,16,16,512]{3,2,1,0:T(8,128)}, f32[2,32,128]{2,1,0:T(8,128)}, f32[16,16,512]{2,1,0:T(8,128)}, f32[8,2,16,512]{3,2,1,0:T(8,128)}, f32[8,2,16,512]{3,2,1,0:T(8,128)}) custom-call(f32[25,32,512]{2,1,0:T(8,128)} %select_maximum_fusion.txe, f32[24,32,512]{2,1,0:T(8,128)} %select_maximum_fusion.8.tye, f32[24,32,512]{2,1,0:T(8,128)} %fusion.1.tze, ...), custom_call_target="tpu_custom_call" | custom-call | tf_op jit(solution)/shard_map/sweeps/pallas_call | solution.py:418
  114.8 20.4 %coarse.1.c4 = f32[32,128]{1,0:T(8,128)} custom-call(f32[2,32,128]{2,1,0:T(8,128)} %get-tuple-element.13.packed), custom_call_target="tpu_custom_call" | custom-call | tf_op jit(solution)/shard_map/coarse/pallas_call | solution.py:590
  135.3 12.0 %finish.1 = (f32[16,16,512]{2,1,0:T(8,128)}, f32[16,16,512]{2,1,0:T(8,128)}) custom-call(f32[25,32,512]{2,1,0:T(8,128)} %select_maximum_fusion.txe, f32[24,32,512]{2,1,0:T(8,128)} %select_maximum_fusion.8.tye, f32[24,32,512]{2,1,0:T(8,128)} %fusion.1.tze, f32[8,16,16,512]{3,2,1,0:T(8,128)} %get-tuple-element.7.basis, ...), custom_call_target="tpu_custom_call" | custom-call | tf_op jit(solution)/shard_map/finish/pallas_call | solution.py:439
  (7 shorter events, 0.1 us)
Async XLA Ops:
  0.6 1.4 copy-start
  0.6 1.4 copy-start.1
  2.4 16.7 %collective-permute-start.1 = (f32[16,12,512]{2,1,0:T(8,128)S(1)}, f32[16,12,512]{2,1,0:T(8,128)S(1)}, u32[]{:S(2)}, u32[]{:S(2)}) collective-permute-start(f32[16,12,512]{2,1,0:T(8,128)S(1)} %pad_maximum_fusion.5), channel_id=1, source_target_pairs={{1,0},{2,1},{3,2},{4,3},{5,4},{6,5},{7,6},{9,8},{10,9},{11,10},{12... | collective-permute-start | bytes 1179656 | tf_op jit(solution)/shard_map/ppermute | solution.py:613
  5.6 23.2 %collective-permute-start = (f32[16,13,512]{2,1,0:T(8,128)S(1)}, f32[16,13,512]{2,1,0:T(8,128)S(1)}, u32[]{:S(2)}, u32[]{:S(2)}) collective-permute-start(f32[16,13,512]{2,1,0:T(8,128)S(1)} %pad_maximum_fusion.4), channel_id=1, source_target_pairs={{0,1},{1,2},{2,3},{3,4},{4,5},{5,6},{6,7},{8,9},{9,10},{10,11},{11... | collective-permute-start | bytes 1277960 | tf_op jit(solution)/shard_map/ppermute | solution.py:608
  29.7 5.8 %copy-start.2 = (s32[16,1]{0,1:T(1,128)S(1)}, s32[16,1]{0,1:T(1,128)}, u32[]{:S(2)}) copy-start(s32[16,1]{0,1:T(1,128)} %param.12) | copy-start | bytes 196
  29.7 6.5 %copy-start.3 = (f32[16,1]{0,1:T(1,128)S(1)}, f32[16,1]{0,1:T(1,128)}, u32[]{:S(2)}) copy-start(f32[16,1]{0,1:T(1,128)} %param.13) | copy-start | bytes 196
  29.7 11.5 %collective-permute-start.3 = (f32[12,24,512]{2,1,0:T(8,128)}, f32[12,24,512]{2,1,0:T(8,128)}, u32[]{:S(2)}, u32[]{:S(2)}) collective-permute-start(f32[12,24,512]{2,1,0:T(8,128)} %fusion.6), channel_id=1, source_target_pairs={{8,0},{16,8},{24,16},{32,24},{40,32},{48,40},{56,48},{64,56},{72,6... | collective-permute-start | bytes 1769480 | tf_op jit(solution)/shard_map/ppermute | solution.py:613
  33.6 14.3 %collective-permute-start.2 = (f32[13,24,512]{2,1,0:T(8,128)S(1)}, f32[13,24,512]{2,1,0:T(8,128)}, u32[]{:S(2)}, u32[]{:S(2)}) collective-permute-start(f32[13,24,512]{2,1,0:T(8,128)S(1)} %fusion.3), channel_id=1, source_target_pairs={{0,8},{8,16},{16,24},{24,32},{32,40},{40,48},{48,56},{56,64},{64,7... | collective-permute-start | bytes 1916936 | tf_op jit(solution)/shard_map/ppermute | solution.py:608

commit v3 on v2

--- a/solution.py
+++ b/solution.py
@@ -22,16 +22,49 @@
     return pltpu.roll(value, shift, 1)
 
 
-def main_kernel(txe, tye, tze, acc, src, wcell, wrate,
+def select_dot(table, value):
+    total = None
+    for _ in range(3):
+        part = value.astype(jnp.bfloat16)
+        value = value - part.astype(F32)
+        term = jnp.dot(*table(part), preferred_element_type=F32)
+        total = term if total is None else total + term
+    return total
+
+
+LO_SPANS = (4, 4, 5)
+HI_SPANS = (4, 4, 4)
+ZROWS = 216
+
+
+def z_row(x):
+    return 13 * x + 4 * (x >= 4)
+
+
+def main_kernel(tx_in, ty_in, tz_in, xlo, xhi, zlo, zhi, corners, acc, src, wcell, wrate,
                 basis_out, coarse_out, rhs_out, xh_out, zh_out,
                 tx_s, ty_s, tz_s, tym_s, dd_s, b0, b1, sums, sem_in, sem_out, sem_x):
     loads = []
+    pieces = ((tx_in, 0, 16, tx_s, 5), (xlo, 0, 5, tx_s, 0), (xhi, 0, 4, tx_s, 21),
+              (ty_in, 0, 16, ty_s, 4), (xlo, 5, 4, ty_s, 0), (xhi, 4, 4, ty_s, 20),
+              (tz_in, 0, 16, tz_s, 4), (xlo, 9, 4, tz_s, 0), (xhi, 8, 4, tz_s, 20))
     for t in range(NT):
-        lanes = pl.ds(128 * t, 128)
-        for k, (hbm, vmem) in enumerate(((txe, tx_s), (tye, ty_s), (tze, tz_s))):
-            copy = pltpu.make_async_copy(hbm.at[:, :, lanes], vmem.at[:, t], sem_in.at[k * NT + t])
+        for k, (hbm, first_in, count, vmem, first_out) in enumerate(pieces):
+            copy = pltpu.make_async_copy(hbm.at[pl.ds(first_in, count), :, pl.ds(128 * t, 128)],
+                                         vmem.at[pl.ds(first_out, count), t, pl.ds(8, 16), :],
+                                         sem_in.at[k * NT + t])
             copy.start()
             loads.append(copy)
+    for x in range(-4, 20):
+        for side, top, spans in ((0, 4, LO_SPANS), (1, 24, HI_SPANS)):
+            for t in range(NT):
+                if 0 <= x < 16:
+                    piece, base = (zlo, zhi)[side], z_row(x)
+                else:
+                    piece, base = corners.at[2 * (x >= 16) + side], 13 * (x % 16) - 156 * (x < 0)
+                for at, count, ref, shift in zip((0, 4, 8), spans, (tx_s, ty_s, tz_s), (5, 4, 4)):
+                    row = top - (count - 4)
+                    ref[x + shift, t, row:row + count, :] = piece[t, base + at:base + at + count, :]
     rhs_out[...] = src[...]
     lane_y = iota((1, 512), 1)
     for w in range(16):
@@ -43,6 +76,17 @@
     for copy in loads:
         copy.wait()
 
+    @pl.when(lax.axis_index("tile") == lax.axis_size("tile") - 1)
+    def _():
+        for t in range(NT):
+            tx_s[20, t, 0:32, :] = jnp.zeros((NR, 128), F32)
+
+    @pl.when(lax.axis_index("gz") == lax.axis_size("gz") - 1)
+    def _():
+        for X in range(NXE):
+            for t in range(NT):
+                tz_s[X, t, 23:24, :] = jnp.zeros((1, 128), F32)
+
     sub = iota((8, 128), 0)
     lane = iota((8, 128), 1)
     yo = lane % 8
@@ -55,9 +99,13 @@
     def to_next(value, right):
         return roll(jnp.where(lane == 0, right, value), 127)
 
-    def first(index, carry):
-        X, t = index // NT, index % NT
-        tl = jnp.maximum(t - 1, 0)
+    def first(X, carry):
+        for t in range(NT):
+            first_tile(X, t)
+        return carry
+
+    def first_tile(X, t):
+        tl = max(t - 1, 0)
         par = ((X + 4) // 8 + 1) % 2
         xo = (X + 4) % 8
         own_base, flip_base = par * 4, 4 - par * 4
@@ -69,8 +117,12 @@
             tx, txm = tx_s[X + 1, t, rows, :], tx_s[X, t, rows, :]
             tz, tzm = tz_s[X, t, rows, :], tz_s[X, t, pl.ds(R - 1, 8), :]
             ty = ty_s[X, t, rows, :]
+            if t == NT - 1:
+                ty = jnp.where(lane == 127, 0.0, ty)
+                ty_s[X, t, rows, :] = ty
             tym = to_prev(ty, ty_s[X, tl, rows, :])
-            tym = jnp.where((lane == 0) & (t == 0), 0.0, tym)
+            if t == 0:
+                tym = jnp.where(lane == 0, 0.0, tym)
             diag = tx + txm + tz + tzm + ty + tym
             half = diag * 0.5 + 1e-30
             tym_s[X, t, rows, :] = tym
@@ -89,15 +141,14 @@
                     b0[own_base + 2 * c + d, X, t, rows, :] = value
                     b0[flip_base + 2 * c + d, X, t, rows, :] = jnp.where(in_row & in_lane, vx, 0.0)
                     b1[flip_base + 2 * c + d, X, t, rows, :] = zero
-        return carry
-
-    lax.fori_loop(0, NXE * NT, first, 0)
+
+    lax.fori_loop(0, NXE, first, 0)
 
     def sweep(old, new, k):
         reach = min(k, 3)
 
         def block(X, t, n_slots, par):
-            tl, tr = jnp.maximum(t - 1, 0), jnp.minimum(t + 1, NT - 1)
+            tl, tr = max(t - 1, 0), min(t + 1, NT - 1)
             own_base, flip_base = par * 4, 4 - par * 4
             for r in range(3):
                 R = 4 + 8 * r
@@ -132,23 +183,24 @@
                     s = (own_base if cd < 4 else flip_base) + cd % 4
                     new[s, X, t, rows, :] = values[cd] * inv
 
-        def step(index, carry):
-            X, t = index // NT, index % NT
+        def step(X, carry):
             par = ((X + 4) // 8 + 1) % 2
             xo = (X + 4) % 8
             dist = jnp.where(xo < 4, xo + 1, 8 - xo)
 
             @pl.when(dist <= reach)
             def _():
-                block(X, t, 8, par)
+                for t in range(NT):
+                    block(X, t, 8, par)
 
             @pl.when(dist > reach)
             def _():
-                block(X, t, 4, par)
+                for t in range(NT):
+                    block(X, t, 4, par)
 
             return carry
 
-        lax.fori_loop((k - 1) * NT, (25 - k) * NT, step, 0)
+        lax.fori_loop(k - 1, 25 - k, step, 0)
 
     sweep(b0, b1, 2)
     sweep(b1, b0, 3)
@@ -238,11 +290,11 @@
     folded = jnp.zeros((448, 128), F32)
     for t in range(NT):
         target = ((l_y % 8) // 4) * 64 + 16 * t + l_y // 8
-        folded = folded + jnp.dot(sums[t], (l_j == target).astype(F32), precision=lax.Precision.HIGHEST,
-                                  preferred_element_type=F32)
+        chosen = (l_j == target).astype(jnp.bfloat16)
+        folded = folded + select_dot(lambda part: (part, chosen), sums[t])
     o, i = iota((128, 448), 0), iota((128, 448), 1)
-    pick = ((i // 16 == o % 32) & ((i % 16) // 4 == o // 32)).astype(F32)
-    quarters = jnp.dot(pick, folded, precision=lax.Precision.HIGHEST, preferred_element_type=F32)
+    pick = ((i // 16 == o % 32) & ((i % 16) // 4 == o // 32)).astype(jnp.bfloat16)
+    quarters = select_dot(lambda part: (pick, part), folded)
 
     lane1 = iota((1, 128), 1)
     odd = lane1 % 2 == 1
@@ -285,16 +337,19 @@
         copy.wait()
 
 
-def finish_kernel(txe, tye, tze, basis, xh, zh, c4, acc, rhs, pressure_out, residual_out,
+def finish_kernel(tx_in, ty_in, tz_in, xlo, zlo, basis, xh, zh, c4, acc, rhs, pressure_out, residual_out,
                   tx_s, ty_s, tz_s, g_s, p_s, sem_in):
     loads = []
+    pieces = ((tx_in, 0, 16, tx_s, 1), (xlo, 4, 1, tx_s, 0), (ty_in, 0, 16, ty_s, 0), (tz_in, 0, 16, tz_s, 0))
     for t in range(NT):
-        lanes = pl.ds(128 * t, 128)
-        for k, (hbm, vmem) in enumerate(((txe.at[pl.ds(4, 17)], tx_s), (tye.at[pl.ds(4, 16)], ty_s),
-                                         (tze.at[pl.ds(4, 16)], tz_s))):
-            copy = pltpu.make_async_copy(hbm.at[:, pl.ds(0, 24), lanes], vmem.at[:, t], sem_in.at[k * NT + t])
+        for k, (hbm, first_in, count, vmem, first_out) in enumerate(pieces):
+            copy = pltpu.make_async_copy(hbm.at[pl.ds(first_in, count), :, pl.ds(128 * t, 128)],
+                                         vmem.at[pl.ds(first_out, count), t, pl.ds(8, 16), :],
+                                         sem_in.at[k * NT + t])
             copy.start()
             loads.append(copy)
+        for x in range(16):
+            tz_s[x, t, 7:8, :] = zlo[t, z_row(x) + 12:z_row(x) + 13, :]
     sub = iota((8, 128), 0)
     lane = iota((8, 128), 1)
     upper = sub >= 4
@@ -305,8 +360,8 @@
     spread = []
     for d in range(2):
         node = jnp.where(block % 2 == d, block, block + side)
-        spread.append(jnp.dot(c4[...], (j == node).astype(F32), precision=lax.Precision.HIGHEST,
-                              preferred_element_type=F32))
+        chosen = (j == node).astype(jnp.bfloat16)
+        spread.append(select_dot(lambda part: (part, chosen), c4[...]))
     for nx in range(4):
         for c in range(2):
             for d in range(2):
@@ -338,16 +393,16 @@
             total = term if total is None else total + term
         return total
 
-    def pressures(index, carry):
-        x, t = index // NT, index % NT
-        lanes = pl.ds(pl.multiple_of(t * 128, 128), 128)
-        for zb in range(2):
-            p = prolong(lambda s: basis[s, x, 8 * zb:8 * zb + 8, lanes], x + 4, t, zb)
-            p_s[x + 1, t, 8 + 8 * zb:16 + 8 * zb, :] = p
-            pressure_out[x, 8 * zb:8 * zb + 8, lanes] = p
+    def pressures(x, carry):
+        for t in range(NT):
+            lanes = pl.ds(t * 128, 128)
+            for zb in range(2):
+                p = prolong(lambda s: basis[s, x, 8 * zb:8 * zb + 8, lanes], x + 4, t, zb)
+                p_s[x + 1, t, 8 + 8 * zb:16 + 8 * zb, :] = p
+                pressure_out[x, 8 * zb:8 * zb + 8, lanes] = p
         return carry
 
-    lax.fori_loop(0, 16 * NT, pressures, 0)
+    lax.fori_loop(0, 16, pressures, 0)
 
     def outer(t, carry):
         lanes = pl.ds(pl.multiple_of(t * 128, 128), 128)
@@ -379,33 +434,48 @@
     for copy in loads:
         copy.wait()
 
+    @pl.when(lax.axis_index("tile") == lax.axis_size("tile") - 1)
+    def _():
+        for t in range(NT):
+            tx_s[16, t, 8:24, :] = jnp.zeros((16, 128), F32)
+
+    @pl.when(lax.axis_index("gz") == lax.axis_size("gz") - 1)
+    def _():
+        for x in range(16):
+            for t in range(NT):
+                tz_s[x, t, 23:24, :] = jnp.zeros((1, 128), F32)
+
     def to_prev(value, left):
         return roll(jnp.where(lane == 127, left, value), 1)
 
     def to_next(value, right):
         return roll(jnp.where(lane == 0, right, value), 127)
 
-    def residuals(index, carry):
-        x, t = index // NT, index % NT
-        lanes = pl.ds(pl.multiple_of(t * 128, 128), 128)
-        tl, tr = jnp.maximum(t - 1, 0), jnp.minimum(t + 1, NT - 1)
-        for zb in range(2):
-            R = 8 + 8 * zb
-            rows = pl.ds(R, 8)
-            p = p_s[x + 1, t, rows, :]
-            ty = ty_s[x, t, rows, :]
-            tym = jnp.where((lane == 0) & (t == 0), 0.0, to_prev(ty, ty_s[x, tl, rows, :]))
-            flow = acc[x, 8 * zb:8 * zb + 8, lanes] * p
-            flow += tx_s[x + 1, t, rows, :] * (p - p_s[x + 2, t, rows, :])
-            flow += tx_s[x, t, rows, :] * (p - p_s[x, t, rows, :])
-            flow += tz_s[x, t, rows, :] * (p - p_s[x + 1, t, pl.ds(R + 1, 8), :])
-            flow += tz_s[x, t, pl.ds(R - 1, 8), :] * (p - p_s[x + 1, t, pl.ds(R - 1, 8), :])
-            flow += ty * (p - to_next(p, p_s[x + 1, tr, rows, :]))
-            flow += tym * (p - to_prev(p, p_s[x + 1, tl, rows, :]))
-            residual_out[x, 8 * zb:8 * zb + 8, lanes] = rhs[x, 8 * zb:8 * zb + 8, lanes] - flow
+    def residuals(x, carry):
+        for t in range(NT):
+            lanes = pl.ds(t * 128, 128)
+            tl, tr = max(t - 1, 0), min(t + 1, NT - 1)
+            for zb in range(2):
+                R = 8 + 8 * zb
+                rows = pl.ds(R, 8)
+                p = p_s[x + 1, t, rows, :]
+                ty = ty_s[x, t, rows, :]
+                tym = to_prev(ty, ty_s[x, tl, rows, :])
+                if t == 0:
+                    tym = jnp.where(lane == 0, 0.0, tym)
+                if t == NT - 1:
+                    ty = jnp.where(lane == 127, 0.0, ty)
+                flow = acc[x, 8 * zb:8 * zb + 8, lanes] * p
+                flow += tx_s[x + 1, t, rows, :] * (p - p_s[x + 2, t, rows, :])
+                flow += tx_s[x, t, rows, :] * (p - p_s[x, t, rows, :])
+                flow += tz_s[x, t, rows, :] * (p - p_s[x + 1, t, pl.ds(R + 1, 8), :])
+                flow += tz_s[x, t, pl.ds(R - 1, 8), :] * (p - p_s[x + 1, t, pl.ds(R - 1, 8), :])
+                flow += ty * (p - to_next(p, p_s[x + 1, tr, rows, :]))
+                flow += tym * (p - to_prev(p, p_s[x + 1, tl, rows, :]))
+                residual_out[x, 8 * zb:8 * zb + 8, lanes] = rhs[x, 8 * zb:8 * zb + 8, lanes] - flow
         return carry
 
-    lax.fori_loop(0, 16 * NT, residuals, 0)
+    lax.fori_loop(0, 16, residuals, 0)
 
 
 VMEM_SPEC = pl.BlockSpec(memory_space=pltpu.VMEM)
@@ -413,7 +483,7 @@
 ANY_SPEC = pl.BlockSpec(memory_space=pl.ANY)
 
 
-def run_main(txe, tye, tze, acc, src, wcell, wrate):
+def run_main(tx, ty, tz, halos, acc, src, wcell, wrate):
     field = pltpu.VMEM((NXE, NT, NR, 128), F32)
     return pl.pallas_call(
         main_kernel,
@@ -421,35 +491,35 @@
         out_shape=(jax.ShapeDtypeStruct((8, 16, 16, 512), F32), jax.ShapeDtypeStruct((2, 32, 128), F32),
                    jax.ShapeDtypeStruct((16, 16, 512), F32), jax.ShapeDtypeStruct((8, 2, 16, 512), F32),
                    jax.ShapeDtypeStruct((8, 2, 16, 512), F32)),
-        in_specs=[ANY_SPEC] * 3 + [VMEM_SPEC] * 2 + [SMEM_SPEC] * 2,
+        in_specs=[ANY_SPEC] * 5 + [VMEM_SPEC] * 5 + [SMEM_SPEC] * 2,
         out_specs=(ANY_SPEC, VMEM_SPEC, VMEM_SPEC, ANY_SPEC, VMEM_SPEC),
         scratch_shapes=[
             pltpu.VMEM((NXE + 1, NT, NR, 128), F32), field, field, field, field,
             pltpu.VMEM((8, NXE, NT, NR, 128), F32), pltpu.VMEM((8, NXE, NT, NR, 128), F32),
             pltpu.VMEM((NT, 448, 128), F32),
-            pltpu.SemaphoreType.DMA((3 * NT,)), pltpu.SemaphoreType.DMA((8 * NT,)),
+            pltpu.SemaphoreType.DMA((9 * NT,)), pltpu.SemaphoreType.DMA((8 * NT,)),
             pltpu.SemaphoreType.DMA((16 * NT,)),
         ],
         compiler_params=pltpu.CompilerParams(vmem_limit_bytes=60 * 1024 * 1024),
         interpret=INTERPRET,
-    )(txe, tye, tze, acc, src, wcell, wrate)
-
-
-def run_finish(txe, tye, tze, basis, xh, zh, c4, acc, rhs):
+    )(tx, ty, tz, *halos, acc, src, wcell, wrate)
+
+
+def run_finish(tx, ty, tz, xlo, zlo, basis, xh, zh, c4, acc, rhs):
     return pl.pallas_call(
         finish_kernel,
         name="finish",
         out_shape=(jax.ShapeDtypeStruct((16, 16, 512), F32), jax.ShapeDtypeStruct((16, 16, 512), F32)),
-        in_specs=[ANY_SPEC] * 3 + [VMEM_SPEC] * 6,
+        in_specs=[ANY_SPEC] * 4 + [VMEM_SPEC] * 7,
         out_specs=(VMEM_SPEC, VMEM_SPEC),
         scratch_shapes=[
             pltpu.VMEM((17, NT, 24, 128), F32), pltpu.VMEM((16, NT, 24, 128), F32), pltpu.VMEM((16, NT, 24, 128), F32),
             pltpu.VMEM((4, 4, NT, 16, 128), F32), pltpu.VMEM((18, NT, NR, 128), F32),
-            pltpu.SemaphoreType.DMA((3 * NT,)),
+            pltpu.SemaphoreType.DMA((4 * NT,)),
         ],
         compiler_params=pltpu.CompilerParams(vmem_limit_bytes=60 * 1024 * 1024),
         interpret=INTERPRET,
-    )(txe, tye, tze, basis, xh, zh, c4, acc, rhs)
+    )(tx, ty, tz, xlo, zlo, basis, xh, zh, c4, acc, rhs)
 
 
 NEAR = [(dt, dg) for dt in (-1, 0, 1) for dg in (-1, 0, 1) if (dt, dg) != (0, 0)]
@@ -480,9 +550,9 @@
     pl.semaphore_wait(barrier, count)
 
 
-def coarse_kernel(packed, c_out, ops, got, mine, op_send, op_recv, c_send, c_recv):
+def coarse_kernel(packed, c_out, table, got, mine, op_send, op_recv, c_send, c_recv):
     near = neighbours()
-    ops[...] = jnp.zeros(ops.shape, F32)
+    table[...] = jnp.zeros(table.shape, F32)
     got[...] = jnp.zeros(got.shape, F32)
     greet(near)
 
@@ -490,7 +560,7 @@
         made = []
         for n, xb in enumerate({1: (1,), -1: (0,), 0: (0, 1)}[dt]):
             made.append(pltpu.make_async_remote_copy(
-                src_ref=packed.at[xb], dst_ref=ops.at[2 * (1 - dt) + xb, 1 - dg],
+                src_ref=packed.at[xb], dst_ref=table.at[pl.ds(((2 * (1 - dt) + xb) * 3 + 1 - dg) * 32, 32)],
                 send_sem=op_send.at[slot_of(dt, dg), n], recv_sem=op_recv.at[slot_of(-dt, -dg), n],
                 device_id=device, device_id_type=pl.DeviceIdType.MESH))
         return made
@@ -515,13 +585,12 @@
 
     for xb in range(2):
         mine[0, xb:xb + 1, :] = COARSE_STEP * packed[xb, 27:28, :] / packed[xb, 28:29, :]
-        ops[2 + xb, 1] = packed[xb]
+        table[((2 + xb) * 3 + 1) * 32:((2 + xb) * 3 + 2) * 32, :] = packed[xb]
     send(0)
     each(lambda dt, dg, device: [c.start() for c in op_copies(dt, dg, device)])
 
     lane = iota((8, 128), 1)
     row = iota((8, 128), 0)
-    table = ops.reshape(8 * 3 * 32, 128)
 
     def entry(g, k):
         return table[pl.ds(g * 32 + k, 8, stride=96), :]
@@ -594,7 +663,7 @@
         in_specs=[VMEM_SPEC],
         out_specs=VMEM_SPEC,
         scratch_shapes=[
-            pltpu.VMEM((8, 3, 32, 128), F32), pltpu.VMEM((3, 9, 8, 128), F32), pltpu.VMEM((3, 8, 128), F32),
+            pltpu.VMEM((8 * 3 * 32, 128), F32), pltpu.VMEM((3, 9, 8, 128), F32), pltpu.VMEM((3, 8, 128), F32),
             pltpu.SemaphoreType.DMA((9, 2)), pltpu.SemaphoreType.DMA((9, 2)),
             pltpu.SemaphoreType.DMA((3, 9)), pltpu.SemaphoreType.DMA((3, 9)),
         ],
@@ -603,44 +672,85 @@
     )(packed)
 
 
-def shift_up(value, axis):
-    size = lax.axis_size(axis)
-    return lax.ppermute(value, axis, [(i, i + 1) for i in range(size - 1)])
-
-
-def shift_down(value, axis):
-    size = lax.axis_size(axis)
-    return lax.ppermute(value, axis, [(i + 1, i) for i in range(size - 1)])
-
-
-def extend(tx, ty, tz):
-    up = jnp.concatenate([tx[:, 12:], ty[:, 12:], tz[:, 11:]], 1)
-    down = jnp.concatenate([tx[:, :4], ty[:, :4], tz[:, :4]], 1)
-    low, high = shift_up(up, "gz"), shift_down(down, "gz")
-    fill = jnp.zeros((16, 4, 512), F32)
-    txz = jnp.concatenate([low[:, :4], tx, high[:, :4]], 1)
-    tyz = jnp.concatenate([low[:, 4:8], ty, high[:, 4:8]], 1)
-    tzz = jnp.concatenate([low[:, 9:13], tz, high[:, 8:12]], 1)
-    up = jnp.concatenate([txz[11:], tyz[12:], tzz[12:]], 0)
-    down = jnp.concatenate([txz[:4], tyz[:4], tzz[:4]], 0)
-    lowx, highx = shift_up(up, "tile"), shift_down(down, "tile")
-    txe = jnp.pad(jnp.concatenate([lowx[:5], txz, highx[:4]], 0), ((0, 0), (4, 4), (0, 0)))
-    tye = jnp.pad(jnp.concatenate([lowx[5:9], tyz, highx[4:8]], 0), ((0, 0), (4, 4), (0, 0)))
-    tze = jnp.pad(jnp.concatenate([lowx[9:13], tzz, highx[8:12]], 0), ((0, 0), (4, 4), (0, 0)))
-    extra = jnp.pad(low[:, 8:9], ((4, 4), (3, 28), (0, 0)))
-    return txe, tye, tze + extra
+def halo_kernel(tx, ty, tz, xlo, xhi, zlo, zhi, corners, up, down, x_send, x_recv, z_send, z_recv):
+    near = neighbours()
+    exists = {(dt, dg): here for dt, dg, here, _ in near}
+    landing = {(-1, 0): xlo, (1, 0): xhi, (0, -1): zlo, (0, 1): zhi,
+               (-1, -1): corners.at[0], (-1, 1): corners.at[1], (1, -1): corners.at[2], (1, 1): corners.at[3]}
+    for where, ref in landing.items():
+        @pl.when(jnp.logical_not(exists[where]))
+        def _():
+            ref[...] = jnp.zeros(ref.shape, F32)
+    for pack, spans, ends in ((up, LO_SPANS, 16), (down, HI_SPANS, None)):
+        for x in range(16):
+            for at, count, ref in zip((0, 4, 8), spans, (tx, ty, tz)):
+                row = 0 if ends is None else ends - count
+                for t in range(NT):
+                    base = z_row(x) + at
+                    pack[t, base:base + count, :] = ref[x, row:row + count, 128 * t:128 * t + 128]
+    greet(near)
+
+    def copies(dt, dg, device):
+        def remote(src, dst, send, recv):
+            return pltpu.make_async_remote_copy(src_ref=src, dst_ref=dst, send_sem=send, recv_sem=recv,
+                                                device_id=device, device_id_type=pl.DeviceIdType.MESH)
+        if dg == 0:
+            made, at = [], 0
+            spans = (5, 4, 4) if dt == 1 else (4, 4, 4)
+            out = xlo if dt == 1 else xhi
+            side = 0 if dt == 1 else 1
+            for n, (ref, count) in enumerate(zip((tx, ty, tz), spans)):
+                first = 16 - count if dt == 1 else 0
+                made.append(remote(ref.at[pl.ds(first, count)], out.at[pl.ds(at, count)],
+                                   x_send.at[side, n], x_recv.at[side, n]))
+                at += count
+            return made
+        pack = up if dg == 1 else down
+        n = slot_of(dt, dg)
+        m = slot_of(-dt, -dg)
+        if dt == 0:
+            return [remote(pack, zlo if dg == 1 else zhi, z_send.at[n], z_recv.at[m])]
+        first = ZROWS - 56 if dt == 1 else 0
+        corner = (0 if dt == 1 else 2) + (0 if dg == 1 else 1)
+        return [remote(pack.at[:, pl.ds(first, 56), :], corners.at[corner], z_send.at[n], z_recv.at[m])]
+
+    for dt, dg, here, device in sorted(near, key=lambda v: abs(v[0]) + abs(v[1])):
+        @pl.when(here)
+        def _():
+            for copy in copies(dt, dg, device):
+                copy.start()
+    for dt, dg, here, device in near:
+        @pl.when(here)
+        def _():
+            for copy in copies(-dt, -dg, device):
+                copy.wait_recv()
+            for copy in copies(dt, dg, device):
+                copy.wait_send()
+
+
+def run_halo(tx, ty, tz):
+    shapes = ((13, 16, 512), (12, 16, 512), (NT, ZROWS, 128), (NT, ZROWS, 128), (4, NT, 56, 128))
+    return pl.pallas_call(
+        halo_kernel,
+        name="halo",
+        out_shape=tuple(jax.ShapeDtypeStruct(shape, F32) for shape in shapes),
+        in_specs=[VMEM_SPEC] * 3,
+        out_specs=(VMEM_SPEC,) * 5,
+        scratch_shapes=[
+            pltpu.VMEM((NT, ZROWS, 128), F32), pltpu.VMEM((NT, ZROWS, 128), F32),
+            pltpu.SemaphoreType.DMA((2, 3)), pltpu.SemaphoreType.DMA((2, 3)),
+            pltpu.SemaphoreType.DMA((9,)), pltpu.SemaphoreType.DMA((9,)),
+        ],
+        compiler_params=pltpu.CompilerParams(collective_id=0, has_side_effects=True),
+        interpret=COMM_INTERPRET,
+    )(tx, ty, tz)
 
 
 def body(trans_x, trans_y, trans_z, accumulation, source, well_cell, well_rate):
-    last_x = lax.axis_index("tile") == lax.axis_size("tile") - 1
-    last_z = lax.axis_index("gz") == lax.axis_size("gz") - 1
-    tx = jnp.where((jnp.arange(16) == 15)[:, None, None] & last_x, 0.0, trans_x)
-    tz = jnp.where((jnp.arange(16) == 15)[None, :, None] & last_z, 0.0, trans_z)
-    ty = jnp.where((jnp.arange(512) == 511)[None, None, :], 0.0, trans_y)
-    txe, tye, tze = extend(tx, ty, tz)
-    basis, packed, rhs, xh, zh = run_main(txe, tye, tze, accumulation, source, well_cell, well_rate)
+    halos = run_halo(trans_x, trans_y, trans_z)
+    basis, packed, rhs, xh, zh = run_main(trans_x, trans_y, trans_z, halos, accumulation, source, well_cell, well_rate)
     c4 = run_coarse(packed)
-    pressure, residual = run_finish(txe, tye, tze, basis, xh, zh, c4, accumulation, rhs)
+    pressure, residual = run_finish(trans_x, trans_y, trans_z, halos[0], halos[2], basis, xh, zh, c4, accumulation, rhs)
     return basis, pressure, residual
 
 

time: 148 us -> 102 us (0.69)
  waiting for transfers between devices: 30.2 us -> 0 us
  starting transfers between devices: 11.5 us -> 0 us
  other arithmetic: 6.93 us -> 0 us
  Pallas kernels: 93 us -> 97.8 us
  local copies, waits for them, and re-layouts: 4.82 us -> 2.65 us
    pallas_call x0 -> x1, Pallas kernels: none -> 40.9 us  [run_halo(): pl.pallas_call(halo_kernel, name='halo', out_shape=tuple((jax.ShapeDtypeS...]
    ppermute x4 -> x0, waiting for transfers between devices: 30.2 us -> none  [the longest x2 15.1 us: shift_up(): return lax.ppermute(value, axis, [(i, i + 1) for i in range(size - 1)])]
    pallas_call x1, Pallas kernels: 60.6 us -> 31.5 us  [run_main(): pl.pallas_call(main_kernel, name='sweeps', out_shape=(jax.ShapeDtypeStruc...]
    ppermute x4 -> x0, starting transfers between devices: 11.5 us -> none  [the longest x2 6.81 us: shift_down(): return lax.ppermute(value, axis, [(i + 1, i) for i in range(size - 1)])]
    pallas_call x1, Pallas kernels: 12 us -> 7.02 us  [run_finish(): pl.pallas_call(finish_kernel, name='finish', out_shape=(jax.ShapeDtypeStr...]
    concatenate x6 -> x0, other arithmetic: 4.06 us -> none  [the longest x1 1.46 us: extend(): jnp.concatenate([lowx[:5], txz, highx[:4]], 0)]
    slice x9 -> x0, local copies, waits for them, and re-layouts: 3.47 us -> none  [the longest x1 1.15 us: extend(): highx[8:12]]
    pallas_call x1, Pallas kernels: 20.4 us -> 18.4 us  [run_coarse(): pl.pallas_call(coarse_kernel, name='coarse', out_shape=jax.ShapeDtypeStru...]
  transfers between devices with their start and end apart: 4 -> 0, of which waited for: 4 -> 0; matrix products, arithmetic and copies ran while one was open for 2% -> 0% of each run, Pallas kernels for 0% -> 0%
where the time goes in v3:
time: 102 us; the launch traced here: 101 us
  Pallas kernels  97.8 us (96%)
  local copies, waits for them, and re-layouts  2.65 us (3%)
    pallas_call x1, Pallas kernels, run_halo(): pl.pallas_call(halo_kernel, name='halo', out_shape=tuple((jax.ShapeDtypeS...  40.9 us
    pallas_call x1, Pallas kernels, run_main(): pl.pallas_call(main_kernel, name='sweeps', out_shape=(jax.ShapeDtypeStruc...  31.5 us
    pallas_call x1, Pallas kernels, run_coarse(): pl.pallas_call(coarse_kernel, name='coarse', out_shape=jax.ShapeDtypeStru...  18.4 us
    pallas_call x1, Pallas kernels, run_finish(): pl.pallas_call(finish_kernel, name='finish', out_shape=(jax.ShapeDtypeStr...  7.02 us
    unnamed x2, local copies, waits for them, and re-layouts  2.65 us

profile of v3, /device:TPU:36, one launch (start us, length us, event | category | flops | bytes accessed | tf_op | source)
XLA Modules:
  0.0 101.1 jit_solution(3169070181386268558)
XLA Ops:
  0.6 1.3 %copy.10.wcell = s32[16,1]{1,0:T(8,128)} copy(s32[16,1]{0,1:T(1,128)} %param.12) | data formatting | bytes 128 | tf_op args[5]
  2.0 1.3 %copy.11.wrate = f32[16,1]{1,0:T(8,128)} copy(f32[16,1]{0,1:T(1,128)} %param.13) | data formatting | bytes 128 | tf_op args[6]
  3.3 40.9 %halo.1 = (f32[13,16,512]{2,1,0:T(8,128)}, f32[12,16,512]{2,1,0:T(8,128)}, f32[4,216,128]{2,1,0:T(8,128)}, f32[4,216,128]{2,1,0:T(8,128)}, f32[4,4,56,128]{3,2,1,0:T(8,128)}) custom-call(f32[16,16,512]{2,1,0:T(8,128)} %tx_in.3, f32[16,16,512]{2,1,0:T(8,128)} %ty_in.3, f32[16,16,512]{2,1,0:T(8,128)} %tz_in.3), custom_call_target="tpu_custom_call" | custom-call | tf_op jit(solution)/shard_map/halo/pallas_call | solution.py:733
  44.2 31.5 %sweeps.1 = (f32[8,16,16,512]{3,2,1,0:T(8,128)}, f32[2,32,128]{2,1,0:T(8,128)}, f32[16,16,512]{2,1,0:T(8,128)}, f32[8,2,16,512]{3,2,1,0:T(8,128)}, f32[8,2,16,512]{3,2,1,0:T(8,128)}) custom-call(f32[16,16,512]{2,1,0:T(8,128)} %tx_in.3, f32[16,16,512]{2,1,0:T(8,128)} %ty_in.3, f32[16,16,512]{2,1,0:T(8,128)} %tz_in.3, f32[13,16,512]{2,1,0:T(8,128)} %get-tuple-element.15.xlo, ...), custom_call_target="tpu_custom_call" | custom-call | tf_op jit(solution)/shard_map/sweeps/pallas_call | solution.py:488
  75.7 18.4 %coarse.1.c4 = f32[32,128]{1,0:T(8,128)} custom-call(f32[2,32,128]{2,1,0:T(8,128)} %get-tuple-element.23.packed), custom_call_target="tpu_custom_call" | custom-call | tf_op jit(solution)/shard_map/coarse/pallas_call | solution.py:659
  94.1 7.0 %finish.1 = (f32[16,16,512]{2,1,0:T(8,128)}, f32[16,16,512]{2,1,0:T(8,128)}) custom-call(f32[16,16,512]{2,1,0:T(8,128)} %tx_in.3, f32[16,16,512]{2,1,0:T(8,128)} %ty_in.3, f32[16,16,512]{2,1,0:T(8,128)} %tz_in.3, f32[13,16,512]{2,1,0:T(8,128)} %get-tuple-element.15.xlo, f32[4,216,128]{2,1,0:T(8,128)} %get-tuple-element.17.zlo, ...), custom_call_target="tpu_custom_call" | custom-call | tf_op jit(solution)/shard_map/finish/pallas_call | solution.py:509

commit v4 on v3

--- a/solution.py
+++ b/solution.py
@@ -35,6 +35,7 @@
 LO_SPANS = (4, 4, 5)
 HI_SPANS = (4, 4, 4)
 ZROWS = 216
+CORNER_ROWS = (0, 0, 12, 21, 27)
 
 
 def z_row(x):
@@ -58,21 +59,26 @@
     for x in range(-4, 20):
         for side, top, spans in ((0, 4, LO_SPANS), (1, 24, HI_SPANS)):
             for t in range(NT):
-                if 0 <= x < 16:
-                    piece, base = (zlo, zhi)[side], z_row(x)
-                else:
-                    piece, base = corners.at[2 * (x >= 16) + side], 13 * (x % 16) - 156 * (x < 0)
-                for at, count, ref, shift in zip((0, 4, 8), spans, (tx_s, ty_s, tz_s), (5, 4, 4)):
-                    row = top - (count - 4)
-                    ref[x + shift, t, row:row + count, :] = piece[t, base + at:base + at + count, :]
+                for f, (ref, shift) in enumerate(((tx_s, 5), (ty_s, 4), (tz_s, 4))):
+                    if 0 <= x < 16:
+                        count = spans[f]
+                        row = top - (count - 4)
+                        base = z_row(x) + 4 * f
+                        ref[x + shift, t, row:row + count, :] = (zlo, zhi)[side][t, base:base + count, :]
+                    else:
+                        layer = -x if x < 0 else x - 15
+                        count = 5 - layer
+                        row = top if side else 8 - count
+                        base = CORNER_ROWS[layer] + f * count
+                        ref[x + shift, t, row:row + count, :] = corners[2 * (x >= 16) + side, t, base:base + count, :]
     rhs_out[...] = src[...]
     lane_y = iota((1, 512), 1)
     for w in range(16):
-        cell = wcell[w, 0]
+        cell = wcell[0, w]
         row = cell // 512
         x, z, y = row // 16, row % 16, cell % 512
         old = rhs_out[x, pl.ds(z, 1), :]
-        rhs_out[x, pl.ds(z, 1), :] = old + jnp.where(lane_y == y, wrate[w, 0], 0.0)
+        rhs_out[x, pl.ds(z, 1), :] = old + jnp.where(lane_y == y, wrate[0, w], 0.0)
     for copy in loads:
         copy.wait()
 
@@ -99,18 +105,24 @@
     def to_next(value, right):
         return roll(jnp.where(lane == 0, right, value), 127)
 
+    def distance(X):
+        xo = (X + 4) % 8
+        return jnp.where(xo < 4, xo + 1, 8 - xo)
+
     def first(X, carry):
-        for t in range(NT):
-            first_tile(X, t)
+        dist = distance(X)
+        for kind, here in ((1, dist == 1), (2, (dist == 2) | (dist == 3)), (4, dist == 4)):
+            @pl.when(here)
+            def _():
+                for t in range(NT):
+                    first_tile(X, t, kind)
         return carry
 
-    def first_tile(X, t):
+    def first_tile(X, t, kind):
         tl = max(t - 1, 0)
         par = ((X + 4) // 8 + 1) % 2
         xo = (X + 4) % 8
         own_base, flip_base = par * 4, 4 - par * 4
-        lo_x = (xo == 0).astype(F32)
-        hi_x = (xo == 7).astype(F32)
         for r in range(3):
             R = 4 + 8 * r
             rows = pl.ds(R, 8)
@@ -127,7 +139,7 @@
             half = diag * 0.5 + 1e-30
             tym_s[X, t, rows, :] = tym
             dd_s[X, t, rows, :] = half
-            txb = lo_x * txm + hi_x * tx
+            txb = jnp.where(xo == 0, txm, tx) if kind == 1 else zero
             tzb = jnp.where(sub == 3, tz, jnp.where(sub == 4, tzm, 0.0))
             tyb = jnp.where(yo == 7, ty, jnp.where(yo == 0, tym, 0.0))
             own = half + (diag - txb - tzb - tyb)
@@ -139,15 +151,16 @@
                     in_row, in_lane = row_par == c, lane_par == d
                     value = jnp.where(in_row, jnp.where(in_lane, own, vy), jnp.where(in_lane, vz, 0.0))
                     b0[own_base + 2 * c + d, X, t, rows, :] = value
-                    b0[flip_base + 2 * c + d, X, t, rows, :] = jnp.where(in_row & in_lane, vx, 0.0)
-                    b1[flip_base + 2 * c + d, X, t, rows, :] = zero
+                    if kind == 1:
+                        b0[flip_base + 2 * c + d, X, t, rows, :] = jnp.where(in_row & in_lane, vx, 0.0)
+                    if kind == 4:
+                        b1[flip_base + 2 * c + d, X, t, rows, :] = zero
 
     lax.fori_loop(0, NXE, first, 0)
 
     def sweep(old, new, k):
-        reach = min(k, 3)
-
-        def block(X, t, n_slots, par):
+        def block(X, t, kind, par, up):
+            n_slots = 4 if kind == 0 else 8
             tl, tr = max(t - 1, 0), min(t + 1, NT - 1)
             own_base, flip_base = par * 4, 4 - par * 4
             for r in range(3):
@@ -162,10 +175,17 @@
                 for cd in range(n_slots):
                     c, d = (cd // 2) % 2, cd % 2
                     s = (own_base if cd < 4 else flip_base) + cd % 4
+                    toward = tx_s[X + up, t, rows, :] * old[s, X - 1 + 2 * up, t, rows, :]
+                    if cd >= 4 and kind == 1:
+                        values.append(toward)
+                        continue
                     b = old[s, X, t, rows, :]
                     v = half * b
-                    v += tx * old[s, X + 1, t, rows, :]
-                    v += txm * old[s, X - 1, t, rows, :]
+                    if cd >= 4 and kind == 2:
+                        v += toward
+                    else:
+                        v += tx * old[s, X + 1, t, rows, :]
+                        v += txm * old[s, X - 1, t, rows, :]
                     v += tz * old[s, X, t, pl.ds(R + 1, 8), :]
                     v += tzm * old[s, X, t, pl.ds(R - 1, 8), :]
                     v += ty * to_next(b, old[s, X, tr, rows, :])
@@ -183,21 +203,20 @@
                     s = (own_base if cd < 4 else flip_base) + cd % 4
                     new[s, X, t, rows, :] = values[cd] * inv
 
+        kinds = {}
+        for away in range(1, 5):
+            kind = 0 if away > min(k, 3) else 3 if away <= k - 2 else 2 if away == k - 1 else 1
+            kinds.setdefault(kind, []).append(away)
+
         def step(X, carry):
             par = ((X + 4) // 8 + 1) % 2
-            xo = (X + 4) % 8
-            dist = jnp.where(xo < 4, xo + 1, 8 - xo)
-
-            @pl.when(dist <= reach)
-            def _():
-                for t in range(NT):
-                    block(X, t, 8, par)
-
-            @pl.when(dist > reach)
-            def _():
-                for t in range(NT):
-                    block(X, t, 4, par)
-
+            up = ((X + 4) % 8 >= 4).astype(jnp.int32)
+            dist = distance(X)
+            for kind, aways in kinds.items():
+                @pl.when((dist >= aways[0]) & (dist <= aways[-1]))
+                def _():
+                    for t in range(NT):
+                        block(X, t, kind, par, up)
             return carry
 
         lax.fori_loop(k - 1, 25 - k, step, 0)
@@ -237,7 +256,11 @@
         R = 8 + 8 * zb
 
         def edges(index, carry):
-            xb, t = index // NT, index % NT
+            for n in range(2):
+                edge_tile(index // 2, 2 * (index % 2) + n)
+            return carry
+
+        def edge_tile(xb, t):
             tl, tr = jnp.maximum(t - 1, 0), jnp.minimum(t + 1, NT - 1)
             rows = pl.ds(R, 8)
             lanes = pl.ds(pl.multiple_of(t * 128, 128), 128)
@@ -282,9 +305,8 @@
                     sums[t, pl.ds(pl.multiple_of(u * 16 + 8 * zb, 8), 8), :] = groups[g][cd]
             sums[t, pl.ds(pl.multiple_of((24 + xb) * 16 + 8 * zb, 8), 8), :] = scale
             sums[t, pl.ds(pl.multiple_of((26 + xb) * 16 + 8 * zb, 8), 8), :] = right
-            return carry
-
-        lax.fori_loop(0, 2 * NT, edges, 0)
+
+        lax.fori_loop(0, 4, edges, 0)
 
     l_y, l_j = iota((128, 128), 0), iota((128, 128), 1)
     folded = jnp.zeros((448, 128), F32)
@@ -672,7 +694,7 @@
     )(packed)
 
 
-def halo_kernel(tx, ty, tz, xlo, xhi, zlo, zhi, corners, up, down, x_send, x_recv, z_send, z_recv):
+def halo_kernel(tx, ty, tz, xlo, xhi, zlo, zhi, corners, up, down, angles, x_send, x_recv, z_send, z_recv):
     near = neighbours()
     exists = {(dt, dg): here for dt, dg, here, _ in near}
     landing = {(-1, 0): xlo, (1, 0): xhi, (0, -1): zlo, (0, 1): zhi,
@@ -681,13 +703,6 @@
         @pl.when(jnp.logical_not(exists[where]))
         def _():
             ref[...] = jnp.zeros(ref.shape, F32)
-    for pack, spans, ends in ((up, LO_SPANS, 16), (down, HI_SPANS, None)):
-        for x in range(16):
-            for at, count, ref in zip((0, 4, 8), spans, (tx, ty, tz)):
-                row = 0 if ends is None else ends - count
-                for t in range(NT):
-                    base = z_row(x) + at
-                    pack[t, base:base + count, :] = ref[x, row:row + count, 128 * t:128 * t + 128]
     greet(near)
 
     def copies(dt, dg, device):
@@ -710,15 +725,37 @@
         m = slot_of(-dt, -dg)
         if dt == 0:
             return [remote(pack, zlo if dg == 1 else zhi, z_send.at[n], z_recv.at[m])]
-        first = ZROWS - 56 if dt == 1 else 0
         corner = (0 if dt == 1 else 2) + (0 if dg == 1 else 1)
-        return [remote(pack.at[:, pl.ds(first, 56), :], corners.at[corner], z_send.at[n], z_recv.at[m])]
-
-    for dt, dg, here, device in sorted(near, key=lambda v: abs(v[0]) + abs(v[1])):
-        @pl.when(here)
-        def _():
-            for copy in copies(dt, dg, device):
-                copy.start()
+        return [remote(angles.at[corner], corners.at[corner], z_send.at[n], z_recv.at[m])]
+
+    def start(chosen):
+        for dt, dg, here, device in near:
+            if chosen(dt, dg):
+                @pl.when(here)
+                def _():
+                    for copy in copies(dt, dg, device):
+                        copy.start()
+
+    start(lambda dt, dg: dg == 0)
+    for pack, spans, step in ((up, LO_SPANS, 1), (down, HI_SPANS, -1)):
+        for x in range(16):
+            for f, ref in enumerate((tx, ty, tz)):
+                row = 16 - spans[f] if step == 1 else 0
+                base = z_row(x) + 4 * f
+                for t in range(NT):
+                    pack[t, base:base + spans[f], :] = ref[x, row:row + spans[f], 128 * t:128 * t + 128]
+        start(lambda dt, dg: dt == 0 and dg == step)
+    for dt in (1, -1):
+        for dg in (1, -1):
+            corner = (0 if dt == 1 else 2) + (0 if dg == 1 else 1)
+            for layer in range(1, 5):
+                x, count = (16 - layer if dt == 1 else layer - 1), 5 - layer
+                row = 16 - count if dg == 1 else 0
+                for f, ref in enumerate((tx, ty, tz)):
+                    base = CORNER_ROWS[layer] + f * count
+                    for t in range(NT):
+                        angles[corner, t, base:base + count, :] = ref[x, row:row + count, 128 * t:128 * t + 128]
+    start(lambda dt, dg: dt != 0 and dg != 0)
     for dt, dg, here, device in near:
         @pl.when(here)
         def _():
@@ -729,7 +766,7 @@
 
 
 def run_halo(tx, ty, tz):
-    shapes = ((13, 16, 512), (12, 16, 512), (NT, ZROWS, 128), (NT, ZROWS, 128), (4, NT, 56, 128))
+    shapes = ((13, 16, 512), (12, 16, 512), (NT, ZROWS, 128), (NT, ZROWS, 128), (4, NT, 32, 128))
     return pl.pallas_call(
         halo_kernel,
         name="halo",
@@ -737,7 +774,7 @@
         in_specs=[VMEM_SPEC] * 3,
         out_specs=(VMEM_SPEC,) * 5,
         scratch_shapes=[
-            pltpu.VMEM((NT, ZROWS, 128), F32), pltpu.VMEM((NT, ZROWS, 128), F32),
+            pltpu.VMEM((NT, ZROWS, 128), F32), pltpu.VMEM((NT, ZROWS, 128), F32), pltpu.VMEM((4, NT, 32, 128), F32),
             pltpu.SemaphoreType.DMA((2, 3)), pltpu.SemaphoreType.DMA((2, 3)),
             pltpu.SemaphoreType.DMA((9,)), pltpu.SemaphoreType.DMA((9,)),
         ],
@@ -748,7 +785,8 @@
 
 def body(trans_x, trans_y, trans_z, accumulation, source, well_cell, well_rate):
     halos = run_halo(trans_x, trans_y, trans_z)
-    basis, packed, rhs, xh, zh = run_main(trans_x, trans_y, trans_z, halos, accumulation, source, well_cell, well_rate)
+    basis, packed, rhs, xh, zh = run_main(trans_x, trans_y, trans_z, halos, accumulation, source,
+                                            well_cell.reshape(1, 16), well_rate.reshape(1, 16))
     c4 = run_coarse(packed)
     pressure, residual = run_finish(trans_x, trans_y, trans_z, halos[0], halos[2], basis, xh, zh, c4, accumulation, rhs)
     return basis, pressure, residual

time: 102 us -> 95.7 us (0.938)
  Pallas kernels: 97.8 us -> 94.2 us
  local copies, waits for them, and re-layouts: 2.65 us -> 0 us
    unnamed x2 -> x0, local copies, waits for them, and re-layouts: 2.65 us -> none
    pallas_call x1, Pallas kernels: 40.9 us -> 38.5 us  [run_halo(): pl.pallas_call(halo_kernel, name='halo', out_shape=tuple((jax.ShapeDtypeS...]
where the time goes in v4:
time: 95.7 us; the launch traced here: 94.9 us
  Pallas kernels  94.2 us (98%)
    pallas_call x1, Pallas kernels, run_halo(): pl.pallas_call(halo_kernel, name='halo', out_shape=tuple((jax.ShapeDtypeS...  38.5 us
    pallas_call x1, Pallas kernels, run_main(): pl.pallas_call(main_kernel, name='sweeps', out_shape=(jax.ShapeDtypeStruc...  30.8 us
    pallas_call x1, Pallas kernels, run_coarse(): pl.pallas_call(coarse_kernel, name='coarse', out_shape=jax.ShapeDtypeStru...  17.9 us
    pallas_call x1, Pallas kernels, run_finish(): pl.pallas_call(finish_kernel, name='finish', out_shape=(jax.ShapeDtypeStr...  7.02 us

profile of v4, /device:TPU:36, one launch (start us, length us, event | category | flops | bytes accessed | tf_op | source)
XLA Modules:
  0.0 94.9 jit_solution(4046427896522230528)
XLA Ops:
  0.6 38.5 %halo.1 = (f32[13,16,512]{2,1,0:T(8,128)}, f32[12,16,512]{2,1,0:T(8,128)}, f32[4,216,128]{2,1,0:T(8,128)}, f32[4,216,128]{2,1,0:T(8,128)}, f32[4,4,32,128]{3,2,1,0:T(8,128)}) custom-call(f32[16,16,512]{2,1,0:T(8,128)} %tx_in.3, f32[16,16,512]{2,1,0:T(8,128)} %ty_in.3, f32[16,16,512]{2,1,0:T(8,128)} %tz_in.3), custom_call_target="tpu_custom_call" | custom-call | tf_op jit(solution)/shard_map/halo/pallas_call | solution.py:770
  39.2 30.8 %sweeps.1 = (f32[8,16,16,512]{3,2,1,0:T(8,128)}, f32[2,32,128]{2,1,0:T(8,128)}, f32[16,16,512]{2,1,0:T(8,128)}, f32[8,2,16,512]{3,2,1,0:T(8,128)}, f32[8,2,16,512]{3,2,1,0:T(8,128)}) custom-call(f32[16,16,512]{2,1,0:T(8,128)} %tx_in.3, f32[16,16,512]{2,1,0:T(8,128)} %ty_in.3, f32[16,16,512]{2,1,0:T(8,128)} %tz_in.3, f32[13,16,512]{2,1,0:T(8,128)} %get-tuple-element.15.xlo, ...), custom_call_target="tpu_custom_call" | custom-call | tf_op jit(solution)/shard_map/sweeps/pallas_call | solution.py:510
  70.0 17.9 %coarse.1.c4 = f32[32,128]{1,0:T(8,128)} custom-call(f32[2,32,128]{2,1,0:T(8,128)} %get-tuple-element.23.packed), custom_call_target="tpu_custom_call" | custom-call | tf_op jit(solution)/shard_map/coarse/pallas_call | solution.py:681
  87.9 7.0 %finish.1 = (f32[16,16,512]{2,1,0:T(8,128)}, f32[16,16,512]{2,1,0:T(8,128)}) custom-call(f32[16,16,512]{2,1,0:T(8,128)} %tx_in.3, f32[16,16,512]{2,1,0:T(8,128)} %ty_in.3, f32[16,16,512]{2,1,0:T(8,128)} %tz_in.3, f32[13,16,512]{2,1,0:T(8,128)} %get-tuple-element.15.xlo, f32[4,216,128]{2,1,0:T(8,128)} %get-tuple-element.17.zlo, ...), custom_call_target="tpu_custom_call" | custom-call | tf_op jit(solution)/shard_map/finish/pallas_call | solution.py:531

commit v5 on v4

--- a/solution.py
+++ b/solution.py
@@ -42,9 +42,9 @@
     return 13 * x + 4 * (x >= 4)
 
 
-def main_kernel(tx_in, ty_in, tz_in, xlo, xhi, zlo, zhi, corners, acc, src, wcell, wrate,
+def main_kernel(tx_in, ty_in, tz_in, xlo, xhi, zlo, zhi, corners, acc_in, src_in, wcell, wrate,
                 basis_out, coarse_out, rhs_out, xh_out, zh_out,
-                tx_s, ty_s, tz_s, tym_s, dd_s, b0, b1, sums, sem_in, sem_out, sem_x):
+                tx_s, ty_s, tz_s, tym_s, dd_s, b0, b1, sums, acc, sem_in, sem_out, sem_x):
     loads = []
     pieces = ((tx_in, 0, 16, tx_s, 5), (xlo, 0, 5, tx_s, 0), (xhi, 0, 4, tx_s, 21),
               (ty_in, 0, 16, ty_s, 4), (xlo, 5, 4, ty_s, 0), (xhi, 4, 4, ty_s, 20),
@@ -56,6 +56,10 @@
                                          sem_in.at[k * NT + t])
             copy.start()
             loads.append(copy)
+    fields = [pltpu.make_async_copy(hbm, vmem, sem_in.at[9 * NT + n])
+              for n, (hbm, vmem) in enumerate(((src_in, rhs_out), (acc_in, acc)))]
+    for copy in fields:
+        copy.start()
     for x in range(-4, 20):
         for side, top, spans in ((0, 4, LO_SPANS), (1, 24, HI_SPANS)):
             for t in range(NT):
@@ -71,14 +75,6 @@
                         row = top if side else 8 - count
                         base = CORNER_ROWS[layer] + f * count
                         ref[x + shift, t, row:row + count, :] = corners[2 * (x >= 16) + side, t, base:base + count, :]
-    rhs_out[...] = src[...]
-    lane_y = iota((1, 512), 1)
-    for w in range(16):
-        cell = wcell[0, w]
-        row = cell // 512
-        x, z, y = row // 16, row % 16, cell % 512
-        old = rhs_out[x, pl.ds(z, 1), :]
-        rhs_out[x, pl.ds(z, 1), :] = old + jnp.where(lane_y == y, wrate[0, w], 0.0)
     for copy in loads:
         copy.wait()
 
@@ -116,6 +112,7 @@
             def _():
                 for t in range(NT):
                     first_tile(X, t, kind)
+                    first_tile(NXE - 1 - X, t, kind)
         return carry
 
     def first_tile(X, t, kind):
@@ -156,7 +153,7 @@
                     if kind == 4:
                         b1[flip_base + 2 * c + d, X, t, rows, :] = zero
 
-    lax.fori_loop(0, NXE, first, 0)
+    lax.fori_loop(0, NXE // 2, first, 0)
 
     def sweep(old, new, k):
         def block(X, t, kind, par, up):
@@ -217,9 +214,10 @@
                 def _():
                     for t in range(NT):
                         block(X, t, kind, par, up)
+                        block(NXE - 1 - X, t, kind, 1 - par, 1 - up)
             return carry
 
-        lax.fori_loop(k - 1, 25 - k, step, 0)
+        lax.fori_loop(k - 1, NXE // 2, step, 0)
 
     sweep(b0, b1, 2)
     sweep(b1, b0, 3)
@@ -252,6 +250,15 @@
 
     lax.fori_loop(0, 8 * NT, rows_of, 0)
 
+    for copy in fields:
+        copy.wait()
+    lane_y = iota((1, 512), 1)
+    for w in range(16):
+        cell = wcell[0, w]
+        row = cell // 512
+        x, z, y = row // 16, row % 16, cell % 512
+        old = rhs_out[x, pl.ds(z, 1), :]
+        rhs_out[x, pl.ds(z, 1), :] = old + jnp.where(lane_y == y, wrate[0, w], 0.0)
     for zb in range(2):
         R = 8 + 8 * zb
 
@@ -359,9 +366,19 @@
         copy.wait()
 
 
-def finish_kernel(tx_in, ty_in, tz_in, xlo, zlo, basis, xh, zh, c4, acc, rhs, pressure_out, residual_out,
-                  tx_s, ty_s, tz_s, g_s, p_s, sem_in):
-    loads = []
+def finish_kernel(tx_in, ty_in, tz_in, xlo, basis_in, xh_in, zh_in, acc_in, rhs_in, zlo, c4, pressure_out, residual_out,
+                  tx_s, ty_s, tz_s, g_s, p_s, basis, xh, zh, acc, rhs, sem_in, sem_b):
+    def plane(x):
+        return pltpu.make_async_copy(basis_in.at[:, x], basis.at[:, x], sem_b.at[x])
+
+    sides = [pltpu.make_async_copy(hbm, vmem, sem_b.at[16 + n])
+             for n, (hbm, vmem) in enumerate(((xh_in, xh), (zh_in, zh)))]
+    loads = [pltpu.make_async_copy(hbm, vmem, sem_b.at[18 + n])
+             for n, (hbm, vmem) in enumerate(((acc_in, acc), (rhs_in, rhs)))]
+    for x in range(16):
+        plane(x).start()
+    for copy in sides + loads:
+        copy.start()
     pieces = ((tx_in, 0, 16, tx_s, 1), (xlo, 4, 1, tx_s, 0), (ty_in, 0, 16, ty_s, 0), (tz_in, 0, 16, tz_s, 0))
     for t in range(NT):
         for k, (hbm, first_in, count, vmem, first_out) in enumerate(pieces):
@@ -416,6 +433,7 @@
         return total
 
     def pressures(x, carry):
+        plane(x).wait()
         for t in range(NT):
             lanes = pl.ds(t * 128, 128)
             for zb in range(2):
@@ -425,6 +443,9 @@
         return carry
 
     lax.fori_loop(0, 16, pressures, 0)
+
+    for copy in sides:
+        copy.wait()
 
     def outer(t, carry):
         lanes = pl.ds(pl.multiple_of(t * 128, 128), 128)
@@ -513,13 +534,13 @@
         out_shape=(jax.ShapeDtypeStruct((8, 16, 16, 512), F32), jax.ShapeDtypeStruct((2, 32, 128), F32),
                    jax.ShapeDtypeStruct((16, 16, 512), F32), jax.ShapeDtypeStruct((8, 2, 16, 512), F32),
                    jax.ShapeDtypeStruct((8, 2, 16, 512), F32)),
-        in_specs=[ANY_SPEC] * 5 + [VMEM_SPEC] * 5 + [SMEM_SPEC] * 2,
+        in_specs=[ANY_SPEC] * 5 + [VMEM_SPEC] * 3 + [ANY_SPEC] * 2 + [SMEM_SPEC] * 2,
         out_specs=(ANY_SPEC, VMEM_SPEC, VMEM_SPEC, ANY_SPEC, VMEM_SPEC),
         scratch_shapes=[
             pltpu.VMEM((NXE + 1, NT, NR, 128), F32), field, field, field, field,
             pltpu.VMEM((8, NXE, NT, NR, 128), F32), pltpu.VMEM((8, NXE, NT, NR, 128), F32),
-            pltpu.VMEM((NT, 448, 128), F32),
-            pltpu.SemaphoreType.DMA((9 * NT,)), pltpu.SemaphoreType.DMA((8 * NT,)),
+            pltpu.VMEM((NT, 448, 128), F32), pltpu.VMEM((16, 16, 512), F32),
+            pltpu.SemaphoreType.DMA((9 * NT + 2,)), pltpu.SemaphoreType.DMA((8 * NT,)),
             pltpu.SemaphoreType.DMA((16 * NT,)),
         ],
         compiler_params=pltpu.CompilerParams(vmem_limit_bytes=60 * 1024 * 1024),
@@ -532,16 +553,18 @@
         finish_kernel,
         name="finish",
         out_shape=(jax.ShapeDtypeStruct((16, 16, 512), F32), jax.ShapeDtypeStruct((16, 16, 512), F32)),
-        in_specs=[ANY_SPEC] * 4 + [VMEM_SPEC] * 7,
+        in_specs=[ANY_SPEC] * 9 + [VMEM_SPEC] * 2,
         out_specs=(VMEM_SPEC, VMEM_SPEC),
         scratch_shapes=[
             pltpu.VMEM((17, NT, 24, 128), F32), pltpu.VMEM((16, NT, 24, 128), F32), pltpu.VMEM((16, NT, 24, 128), F32),
             pltpu.VMEM((4, 4, NT, 16, 128), F32), pltpu.VMEM((18, NT, NR, 128), F32),
-            pltpu.SemaphoreType.DMA((4 * NT,)),
+            pltpu.VMEM((8, 16, 16, 512), F32), pltpu.VMEM((8, 2, 16, 512), F32), pltpu.VMEM((8, 2, 16, 512), F32),
+            pltpu.VMEM((16, 16, 512), F32), pltpu.VMEM((16, 16, 512), F32),
+            pltpu.SemaphoreType.DMA((4 * NT,)), pltpu.SemaphoreType.DMA((20,)),
         ],
         compiler_params=pltpu.CompilerParams(vmem_limit_bytes=60 * 1024 * 1024),
         interpret=INTERPRET,
-    )(tx, ty, tz, xlo, zlo, basis, xh, zh, c4, acc, rhs)
+    )(tx, ty, tz, xlo, basis, xh, zh, acc, rhs, zlo, c4)
 
 
 NEAR = [(dt, dg) for dt in (-1, 0, 1) for dg in (-1, 0, 1) if (dt, dg) != (0, 0)]

time: 95.7 us -> 92.3 us (0.964)
  Pallas kernels: 94.2 us -> 90.8 us
    pallas_call x1, Pallas kernels: 30.8 us -> 27.4 us  [run_main(): pl.pallas_call(main_kernel, name='sweeps', out_shape=(jax.ShapeDtypeStruc...]
where the time goes in v5:
time: 92.3 us; the launch traced here: 91.5 us
  Pallas kernels  90.8 us (98%)
    pallas_call x1, Pallas kernels, run_halo(): pl.pallas_call(halo_kernel, name='halo', out_shape=tuple((jax.ShapeDtypeS...  38.5 us
    pallas_call x1, Pallas kernels, run_main(): pl.pallas_call(main_kernel, name='sweeps', out_shape=(jax.ShapeDtypeStruc...  27.4 us
    pallas_call x1, Pallas kernels, run_coarse(): pl.pallas_call(coarse_kernel, name='coarse', out_shape=jax.ShapeDtypeStru...  17.9 us
    pallas_call x1, Pallas kernels, run_finish(): pl.pallas_call(finish_kernel, name='finish', out_shape=(jax.ShapeDtypeStr...  7.04 us

profile of v5, /device:TPU:36, one launch (start us, length us, event | category | flops | bytes accessed | tf_op | source)
XLA Modules:
  0.0 91.5 jit_solution(8959727697355950742)
XLA Ops:
  0.6 38.5 %halo.1 = (f32[13,16,512]{2,1,0:T(8,128)}, f32[12,16,512]{2,1,0:T(8,128)}, f32[4,216,128]{2,1,0:T(8,128)}, f32[4,216,128]{2,1,0:T(8,128)}, f32[4,4,32,128]{3,2,1,0:T(8,128)}) custom-call(f32[16,16,512]{2,1,0:T(8,128)} %tx_in.3, f32[16,16,512]{2,1,0:T(8,128)} %ty_in.3, f32[16,16,512]{2,1,0:T(8,128)} %tz_in.3), custom_call_target="tpu_custom_call" | custom-call | tf_op jit(solution)/shard_map/halo/pallas_call | solution.py:793
  39.2 27.4 %sweeps.1 = (f32[8,16,16,512]{3,2,1,0:T(8,128)}, f32[2,32,128]{2,1,0:T(8,128)}, f32[16,16,512]{2,1,0:T(8,128)}, f32[8,2,16,512]{3,2,1,0:T(8,128)}, f32[8,2,16,512]{3,2,1,0:T(8,128)}) custom-call(f32[16,16,512]{2,1,0:T(8,128)} %tx_in.3, f32[16,16,512]{2,1,0:T(8,128)} %ty_in.3, f32[16,16,512]{2,1,0:T(8,128)} %tz_in.3, f32[13,16,512]{2,1,0:T(8,128)} %get-tuple-element.15.xlo, ...), custom_call_target="tpu_custom_call" | custom-call | tf_op jit(solution)/shard_map/sweeps/pallas_call | solution.py:531
  66.5 17.9 %coarse.1.c4 = f32[32,128]{1,0:T(8,128)} custom-call(f32[2,32,128]{2,1,0:T(8,128)} %get-tuple-element.24.packed), custom_call_target="tpu_custom_call" | custom-call | tf_op jit(solution)/shard_map/coarse/pallas_call | solution.py:704
  84.4 7.0 %finish.1 = (f32[16,16,512]{2,1,0:T(8,128)}, f32[16,16,512]{2,1,0:T(8,128)}) custom-call(f32[16,16,512]{2,1,0:T(8,128)} %tx_in.3, f32[16,16,512]{2,1,0:T(8,128)} %ty_in.3, f32[16,16,512]{2,1,0:T(8,128)} %tz_in.3, f32[13,16,512]{2,1,0:T(8,128)} %get-tuple-element.15.xlo, f32[8,16,16,512]{3,2,1,0:T(8,128)} %get-tuple-element.12.basis_in, ...), custom_call_target="tpu_custom_call" | custom-call | tf_op jit(solution)/shard_map/finish/pallas_call | solution.py:552
